TPU v7x, 256 devices: a whole 4x4x8 slice. The times are simulated.
256 devices in a mesh: img: 8 (over x, z_hi), tile: 32 (over z_lo, y, core).
Axes of the slice: x: 4, y: 4, z: 8 (z_hi: 2, z_lo: 4; z = z_hi * 4 + z_lo), core: 2. Of those that a mesh axis runs over, the one named last changes fastest.
Arguments:
- block_feature_map: bfloat16 [8, 192, 256, 256], P('img', None, 'tile'), may hold values from -12 to 12, as said below
- upstream_sensitivity: bfloat16 [8, 192, 256, 256], P('img', None, 'tile'), may hold values from -12 to 12, as said below
- triple_mixer: bfloat16 [576, 192], replicated, may hold values from -0.4375 to 0.4375
- spatial_stencil: float32 [576, 3, 3], replicated, may hold values from -2 to 2
- outgoing_mixer: bfloat16 [192, 192], replicated, may hold values from -0.4375 to 0.4375
- sharpness_factor: float32 [4], replicated, may hold values from 1 to 8
- standardize_scaling: float32 [192], replicated, may hold values from 0.5 to 1.5
- standardize_offset: float32 [192], replicated, may hold values from -1.5 to 1.5
Outputs:
- feature_map_adjoint: bfloat16 [8, 192, 256, 256], P('img', None, 'tile')
- triple_mixer_adjoint: float32 [576, 192], replicated
- spatial_stencil_adjoint: float32 [576, 3, 3], replicated
- outgoing_mixer_adjoint: float32 [192, 192], replicated
- sharpness_adjoint: float32 [4], replicated
- scaling_adjoint: float32 [192], replicated
- offset_adjoint: float32 [192], replicated
Inputs may be any that keep to these rules, and one draw needn't show every extreme that they name: `block_feature_map`: the block's input feature map. `upstream_sensitivity`: gradient of the loss with respect to the block's output.
All inputs are finite; a program needn't handle non-finite values.
Results may differ from a plain program's by a relative error of at most 0.0072.
Values may be sent and summed in bfloat16 or wider, within the bound.
No kernel may reach another device: no remote copies, remote signals or barrier semaphores. Data moves between devices by JAX's collectives and lax.ppermute only.
A program may use at most 64 MiB of HBM per device.

v0:
```python
import jax
import jax.numpy as jnp
from jax import lax
from jax.sharding import PartitionSpec as P


def padded_2(array, sides, width):
    for axis, dim in sides:
        count, length = (lax.axis_size(axis), array.shape[dim])
        up = [(i, (i + 1) % count) for i in range(count - 1)]
        down = [(j, i) for i, j in up]
        last = lax.slice_in_dim(array, length - width, length, axis=dim)
        leading = lax.slice_in_dim(array, 0, width, axis=dim)
        before = lax.ppermute(last, axis, up)
        after = lax.ppermute(leading, axis, down)
        array = jnp.concatenate([before, array, after], axis=dim)
    return array


def depthwise(padded, spatial_stencil):
    row_count = padded.shape[-2] - 2
    col_count = padded.shape[-1]
    widened = jnp.pad(padded.astype(jnp.float32), [(0, 0)] * (padded.ndim - 1) + [(1, 1)])
    summed = jnp.zeros(padded.shape[:-2] + (row_count, col_count), jnp.float32)
    for row_off in range(3):
        for col_off in range(3):
            summed = (
                summed
                + spatial_stencil[:, row_off, col_off, None, None]
                * widened[..., row_off : row_off + row_count, col_off : col_off + col_count]
            )
    return summed


def depthwise_back(padded, spatial_stencil):
    row_count = padded.shape[-2] - 2
    col_count = padded.shape[-1]
    widened = jnp.pad(padded.astype(jnp.float32), [(0, 0)] * (padded.ndim - 1) + [(1, 1)])
    summed = jnp.zeros(padded.shape[:-2] + (row_count, col_count), jnp.float32)
    for row_off in range(3):
        for col_off in range(3):
            summed = (
                summed
                + spatial_stencil[:, row_off, col_off, None, None]
                * widened[
                    ...,
                    2 - row_off : 2 - row_off + row_count,
                    2 - col_off : 2 - col_off + col_count,
                ]
            )
    return summed


def kernel_grad(grad_mixed, padded):
    row_count = grad_mixed.shape[-2]
    col_count = grad_mixed.shape[-1]
    grad_float = grad_mixed.astype(jnp.float32)
    widened = jnp.pad(padded.astype(jnp.float32), [(0, 0)] * (padded.ndim - 1) + [(1, 1)])
    reduce_axes = tuple((i for i in range(grad_mixed.ndim) if i != grad_mixed.ndim - 3))
    partials = []
    for row_off in range(3):
        for col_off in range(3):
            partials.append(
                jnp.sum(
                    grad_float
                    * widened[..., row_off : row_off + row_count, col_off : col_off + col_count],
                    axis=reduce_axes,
                )
            )
    return jnp.stack(partials, axis=-1).reshape(grad_mixed.shape[-3], 3, 3)


def local(
    block_feature_map,
    upstream_sensitivity,
    triple_mixer,
    spatial_stencil,
    outgoing_mixer,
    sharpness_factor,
    standardize_scaling,
    standardize_offset,
):
    images, channels, row_count, col_count = block_feature_map.shape
    group_ordinal = sharpness_factor.shape[0]
    head_size = channels // group_ordinal
    pixel_count = row_count * col_count
    as_float = block_feature_map.astype(jnp.float32)
    average = jnp.mean(as_float, axis=1, keepdims=True)
    centered = as_float - average
    inverse = lax.rsqrt(jnp.mean(centered * centered, axis=1, keepdims=True) + 1e-05)
    standard = centered * inverse
    normed = (
        standard * standardize_scaling[:, None, None] + standardize_offset[:, None, None]
    ).astype(jnp.bfloat16)
    projected = jnp.einsum(
        "oc,bchw->bohw", triple_mixer, normed, preferred_element_type=jnp.float32
    ).astype(jnp.bfloat16)
    padded = padded_2(projected, (("tile", 2),), 1)
    mixed = depthwise(padded, spatial_stencil).astype(jnp.bfloat16)
    query_part = mixed[:, :channels].reshape(images, group_ordinal, head_size, pixel_count)
    key_part = mixed[:, channels : 2 * channels].reshape(
        images, group_ordinal, head_size, pixel_count
    )
    value_part = mixed[:, 2 * channels :].reshape(images, group_ordinal, head_size, pixel_count)
    gram_raw = jnp.einsum(
        "bhip,bhjp->bhij", query_part, key_part, preferred_element_type=jnp.float32
    )
    query_float = query_part.astype(jnp.float32)
    key_float = key_part.astype(jnp.float32)
    query_sq = jnp.sum(query_float * query_float, axis=3)
    key_sq = jnp.sum(key_float * key_float, axis=3)
    flat_dy = upstream_sensitivity.reshape(images, channels, pixel_count)
    gram_raw, query_sq, key_sq = lax.psum((gram_raw, query_sq, key_sq), "tile")
    query_len = jnp.sqrt(query_sq + 1e-06)
    key_len = jnp.sqrt(key_sq + 1e-06)
    normalized_affinity = gram_raw / (query_len[..., :, None] * key_len[..., None, :])
    normalized_exp_logits = jnp.exp(normalized_affinity * sharpness_factor[None, :, None, None])
    attention = normalized_exp_logits / jnp.sum(normalized_exp_logits, axis=3, keepdims=True)
    attention_b = attention.astype(jnp.bfloat16)
    attended = jnp.einsum(
        "bhij,bhjp->bhip", attention_b, value_part, preferred_element_type=jnp.float32
    ).astype(jnp.bfloat16)
    flat_out = attended.reshape(images, channels, pixel_count)
    outgoing_mixer_adjoint = jnp.einsum(
        "bop,bcp->oc", flat_dy, flat_out, preferred_element_type=jnp.float32
    )
    grad_attended = jnp.einsum(
        "oc,bop->bcp", outgoing_mixer, flat_dy, preferred_element_type=jnp.float32
    ).astype(jnp.bfloat16)
    grad_attended = grad_attended.reshape(images, group_ordinal, head_size, pixel_count)
    grad_attention = jnp.einsum(
        "bhip,bhjp->bhij", grad_attended, value_part, preferred_element_type=jnp.float32
    )
    grad_attention = lax.psum(grad_attention, "tile")
    grad_value = jnp.einsum(
        "bhij,bhip->bhjp", attention_b, grad_attended, preferred_element_type=jnp.float32
    )
    logits_adjoint = attention * (
        grad_attention - jnp.sum(attention * grad_attention, axis=3, keepdims=True)
    )
    leading_accelerator = (lax.axis_index("tile") == 0).astype(jnp.float32)
    sharpness_adjoint = leading_accelerator * jnp.sum(
        logits_adjoint * normalized_affinity, axis=(0, 2, 3)
    )
    affinity_adjoint = logits_adjoint * sharpness_factor[None, :, None, None]
    grad_gram = (affinity_adjoint / (query_len[..., :, None] * key_len[..., None, :])).astype(
        jnp.bfloat16
    )
    grad_query = jnp.einsum(
        "bhij,bhjp->bhip", grad_gram, key_part, preferred_element_type=jnp.float32
    )
    grad_key = jnp.einsum(
        "bhij,bhip->bhjp", grad_gram, query_part, preferred_element_type=jnp.float32
    )
    row_terms = jnp.sum(grad_query * query_float, axis=3)
    col_terms = jnp.sum(grad_key * key_float, axis=3)
    row_terms, col_terms = lax.psum((row_terms, col_terms), "tile")
    grad_query = grad_query - query_float * (row_terms / (query_sq + 1e-06))[..., None]
    grad_key = grad_key - key_float * (col_terms / (key_sq + 1e-06))[..., None]
    grad_mixed = jnp.concatenate([grad_query, grad_key, grad_value], axis=1)
    grad_mixed = grad_mixed.reshape(images, 3 * channels, row_count, col_count).astype(jnp.bfloat16)
    grad_padded = padded_2(grad_mixed, (("tile", 2),), 1)
    grad_projected = depthwise_back(grad_padded, spatial_stencil).astype(jnp.bfloat16)
    spatial_stencil_adjoint = kernel_grad(grad_mixed, padded)
    flat_gproj = grad_projected.reshape(images, 3 * channels, pixel_count)
    triple_mixer_adjoint = jnp.einsum(
        "bop,bcp->oc",
        flat_gproj,
        normed.reshape(images, channels, pixel_count),
        preferred_element_type=jnp.float32,
    )
    grad_normed = jnp.einsum(
        "oc,bop->bcp", triple_mixer, flat_gproj, preferred_element_type=jnp.float32
    )
    grad_normed = grad_normed.reshape(images, channels, row_count, col_count)
    scaling_adjoint = jnp.sum(grad_normed * standard, axis=(0, 2, 3))
    offset_adjoint = jnp.sum(grad_normed, axis=(0, 2, 3))
    scaled = grad_normed * standardize_scaling[:, None, None]
    first_mean = jnp.mean(scaled, axis=1, keepdims=True)
    second_mean = jnp.mean(scaled * standard, axis=1, keepdims=True)
    feature_map_adjoint = (
        upstream_sensitivity.astype(jnp.float32)
        + (scaled - first_mean - standard * second_mean) * inverse
    ).astype(jnp.bfloat16)
    (
        triple_mixer_adjoint,
        spatial_stencil_adjoint,
        outgoing_mixer_adjoint,
        sharpness_adjoint,
        scaling_adjoint,
        offset_adjoint,
    ) = lax.psum(
        (
            triple_mixer_adjoint,
            spatial_stencil_adjoint,
            outgoing_mixer_adjoint,
            sharpness_adjoint,
            scaling_adjoint,
            offset_adjoint,
        ),
        ("img", "tile"),
    )
    return (
        feature_map_adjoint,
        triple_mixer_adjoint,
        spatial_stencil_adjoint,
        outgoing_mixer_adjoint,
        sharpness_adjoint,
        scaling_adjoint,
        offset_adjoint,
    )


def solution(mesh):
    return jax.shard_map(
        local,
        mesh=mesh,
        in_specs=(
            P("img", None, "tile", None),
            P("img", None, "tile", None),
            P(),
            P(),
            P(),
            P(),
            P(),
            P(),
        ),
        out_specs=(P("img", None, "tile", None), P(), P(), P(), P(), P(), P()),
        check_vma=False,
    )
```

profile of v0, /device:TPU:1, one launch (start us, length us, event | category | flops | bytes accessed | tf_op | source)
XLA Modules:
  0.0 733.8 jit_solution(2483517607310810542)
XLA Ops:
  7.3 1.4 convert_reduce_fusion
  8.7 1.4 fusion.40
  10.1 1.6 fusion.51
  11.8 0.8 convert_bitcast_fusion
  12.6 4.6 collective-permute-start
  17.2 1.9 collective-permute-start.1
  19.2 0.1 slice_reduce_fusion.8
  19.3 0.2 copy.35
  19.5 0.4 convolution_convert_fusion.1
  19.9 1.0 collective-permute-done
  20.9 4.4 collective-permute-done.1
  25.3 0.5 maximum_convert_fusion.1
  25.8 8.7 %add_convert_fusion = bf16[1,576,8,256]{3,1,2,0:T(8,128)(2,1)S(1)} fusion(f32[1,576,10,256]{3,1,2,0:T(8,128)S(1)} %maximum_convert_fusion.1, f32[576]{0:T(1024)S(1)} %get-tuple-element.41, f32[576]{0:T(1024)S(1)} %get-tuple-element.42, f32[576]{0:T(1024)S(1)} %get-tuple-element.35, f32[576]{0:T(1024)S(1)} %get-tuple-element.36, ...), kind=kLoop, calls=%fused_computation.49 | loop fusion | flops 21233664 | bytes 22450176 | tf_op jit(solution)/shard_map/convert_element_type | solution.py:99
  34.5 0.4 multiply_reduce_fusion.1
  34.8 0.2 fusion.71
  35.1 1.3 copy.23
  36.4 2.2 reshape.360
  38.6 0.7 reduce_sum.209
  39.3 0.7 reduce_sum.211
  39.9 1.3 copy.22
  41.2 1.4 reshape.357
  42.7 1.3 copy.21
  44.0 1.4 reshape.356
  45.5 2.1 convolution_bitcast_fusion.2
  47.6 1.0 convolution_bitcast_fusion.3
  48.6 0.0 all-reduce.9.cloned.1.call-start
  48.7 272.6 %all-reduce.11.cloned.1.call-done = (f32[1,4,48,48]{3,2,1,0:T(8,128)}, f32[1,4,48]{2,1,0:T(4,128)}, f32[1,4,48]{2,1,0:T(4,128)}, f32[1,4,48,48]{3,2,1,0:T(8,128)}) async-done(((f32[1,4,48,48]{3,2,1,0:T(8,128)}, f32[1,4,48]{2,1,0:T(4,128)}, f32[1,4,48]{2,1,0:T(4,128)}, f32[1,4,48,48]{3,2,1,0:T(8,128)}), (f32[1,4,48,48]{3,2,1,0:T(8,128)}, f32[1,4,48]{2,1,0:T(4,128)}, f32[1,4,48]{2,1,0:T(4,128)}, ...) | async-done | bytes 75280 | tf_op jit(solution)/shard_map/psum | solution.py:113
  321.3 0.7 sqrt_bitcast_fusion
  322.0 1.1 fusion.57
  323.1 2.3 convolution_bitcast_fusion
  325.4 2.5 convolution_convert_fusion
  327.9 1.2 multiply_reduce_fusion.3
  329.1 1.2 multiply_reduce_fusion.2
  330.3 2.7 fusion.44
  332.9 1.7 fusion.41
  334.6 67.8 %all-reduce.4 = (f32[1,4,48]{2,1,0:T(4,128)S(1)}, f32[1,4,48]{2,1,0:T(4,128)S(1)}) all-reduce(f32[1,4,48]{2,1,0:T(4,128)S(1)} %bitcast.126, f32[1,4,48]{2,1,0:T(4,128)S(1)} %bitcast.127), channel_id=1, replica_groups=mesh['img'=8,'tile'=32] {'tile'}, use_global_device_ids=true, to_apply=%region_13.14 | all-reduce | flops 384 | bytes 3072 | tf_op jit(solution)/shard_map/psum | solution.py:157
  402.5 1.7 fusion.46
  404.2 1.8 fusion.43
  406.0 0.3 maximum_convert_fusion
  406.2 0.8 copy.36
  407.0 0.6 slice-done.1
  407.6 12.1 %fusion.23 = (f32[576]{0:T(1024)S(1)}, f32[576]{0:T(1024)S(1)}, f32[576]{0:T(1024)S(1)}, f32[576]{0:T(1024)S(1)}, f32[576]{0:T(1024)S(1)}, /*index=5*/f32[576]{0...) fusion(f32[1,576,10,256]{3,1,2,0:T(8,128)S(1)} %bitcast.112, bf16[1,576,8,256]{3,2,1,0:T(8,128)(2,1)S(1)} %bitcast.113), kind=kLoop, calls=%fused_computation.44 | loop fusion | flops 22408128 | bytes 22434048 | tf_op jit(solution)/shard_map/reduce_sum | solution.py:64
  419.7 0.5 copy.26
  420.2 0.8 fusion.70
  421.1 1.9 collective-permute-start.2
  423.0 6.4 collective-permute-start.3
  429.6 0.1 stack.39
  429.6 2.2 convolution_bitcast_fusion.1
  431.8 1.6 maximum_convert_fusion.2
  433.5 2.5 copy-done.2
  436.0 9.7 %fusion.48 = f32[576,192]{0,1:T(8,128)} fusion(bf16[192,8,256]{2,1,0:T(8,128)(2,1)S(1)} %copy-done.10, f32[1,576,10,256]{3,1,2,0:T(8,128)S(1)} %maximum_convert_fusion.2, f32[576]{0:T(1024)S(1)} %get-tuple-element.41, f32[576]{0:T(1024)S(1)} %get-tuple-element.42, f32[576]{0:T(1024)S(1)} %get-tuple-element.35, f32[576]{0:T(1024)S(1)} %get-tuple-element.36, ...), kind=kOutput, calls=%fused_computation.90 | convolution fusion | flops 474218496 | bytes 21319680 | tf_op jit(solution)/shard_map/bop,bcp->oc/dot_general | solution.py:166
  445.7 18.9 %fusion.87 = bf16[72,8,8,256]{3,1,0,2:T(8,128)(2,1)S(1)} fusion(f32[576]{0:T(1024)S(1)} %get-tuple-element.41, f32[1,576,10,256]{3,1,2,0:T(8,128)} %copy-done.2, f32[576]{0:T(1024)S(1)} %get-tuple-element.42, f32[576]{0:T(1024)S(1)} %get-tuple-element.35, f32[576]{0:T(1024)S(1)} %get-tuple-element.36, f32[576]{0:T(1024)S(1)} %get-tuple-element.37, ...), kind=kLoop, calls=%fused_computation.136 | loop fusion | flops 21233664 | bytes 22434048
  464.6 0.3 copy.37
  465.0 0.3 copy-done.15
  465.3 0.8 fusion.47
  466.2 0.2 reduce_sum.231
  466.3 0.9 copy-done.4
  467.3 2.0 copy.38
  469.3 1.6 fusion.39
  471.0 74.6 %all-reduce.2 = (f32[576,3,3]{0,2,1:T(4,128)}, f32[4]{0:T(128)}, f32[192]{0:T(256)}, f32[192]{0:T(256)}) all-reduce(f32[576,3,3]{0,2,1:T(4,128)S(1)} %reshape.366, f32[4]{0:T(128)S(1)} %broadcast_multiply_fusion.3, f32[192]{0:T(256)S(1)} %get-tuple-element.30, f32[192]{0:T(256)S(1)} %reduce_sum.231), channel_id=1, replica_groups=mesh['img'=8,'tile'=32] {'img','tile'}, use_global_device_ids=true, to_apply=%region_26.27 | all-reduce | flops 5572 | bytes 44576 | tf_op jit(solution)/shard_map/psum | solution.py:192
  545.6 1.4 fusion.38
  547.0 176.4 %all-reduce.9.cloned.1.call-done = (f32[576,192]{0,1:T(8,128)}, f32[192,192]{0,1:T(8,128)}) async-done(((f32[576,192]{0,1:T(8,128)}, f32[192,192]{0,1:T(8,128)}), (f32[576,192]{0,1:T(8,128)}, f32[192,192]{0,1:T(8,128)})) %all-reduce.9.cloned.1.call-update) | async-done | bytes 589840 | tf_op jit(solution)/shard_map/psum | solution.py:192
  723.4 1.7 copy.32
  725.1 1.8 copy.59
  (61 shorter events, 0.3 us)
Async XLA Ops:
  7.2 4.6 copy-start
  7.2 12.0 %copy-start.14 = (f32[576,3,3]{0,2,1:T(4,128)S(1)}, f32[576,3,3]{0,2,1:T(4,128)}, u32[]{:S(2)}) copy-start(f32[576,3,3]{0,2,1:T(4,128)} %param.11) | copy-start | bytes 62212
  7.2 12.1 %copy-start.7 = (bf16[1,192,8,256]{3,2,1,0:T(8,128)(2,1)S(1)}, bf16[1,192,8,256]{3,2,1,0:T(8,128)(2,1)}, u32[]{:S(2)}) copy-start(bf16[1,192,8,256]{3,2,1,0:T(8,128)(2,1)} %param.9) | copy-start | bytes 2359300
  7.2 12.3 %copy-start.12 = (bf16[192,192]{1,0:T(8,128)(2,1)S(1)}, bf16[192,192]{1,0:T(8,128)(2,1)}, u32[]{:S(2)}) copy-start(bf16[192,192]{1,0:T(8,128)(2,1)} %param.12) | copy-start | bytes 221188
  7.2 314.1 %all-reduce.11.cloned.1.call-start = ((), (), s32[]{:S(2)}) async-start(), calls=%async_computation.1 | async-start | bytes 401408 | tf_op jit(solution)/shard_map/psum | solution.py:113
  11.8 7.5 %copy-start.9 = (bf16[192,8,256]{2,1,0:T(8,128)(2,1)}, bf16[192,8,256]{2,1,0:T(8,128)(2,1)S(1)}, u32[]{:S(2)}) copy-start(bf16[192,8,256]{2,1,0:T(8,128)(2,1)S(1)} %fusion.51) | copy-start | bytes 2359300
  12.6 8.2 %collective-permute-start = (bf16[1,576,1,256]{3,1,2,0:T(8,128)(2,1)S(1)}, bf16[1,576,1,256]{3,1,2,0:T(8,128)(2,1)S(1)}, u32[]{:S(2)}, u32[]{:S(2)}) collective-permute-start(bf16[1,576,1,256]{3,1,2,0:T(8,128)(2,1)S(1)} %get-tuple-element.60), channel_id=1, source_target_pairs={{0,1},{1,2},{2,3},{3,4},{4,5},{5,6},{6,7},{7,8},{8,9},{9,10},{10,1... | collective-permute-start | bytes 884744 | tf_op jit(solution)/shard_map/ppermute | solution.py:14
  17.2 8.0 %collective-permute-start.1 = (bf16[1,576,1,256]{3,1,2,0:T(8,128)(2,1)S(1)}, bf16[1,576,1,256]{3,1,2,0:T(8,128)(2,1)S(1)}, u32[]{:S(2)}, u32[]{:S(2)}) collective-permute-start(bf16[1,576,1,256]{3,1,2,0:T(8,128)(2,1)S(1)} %get-tuple-element.61), channel_id=1, source_target_pairs={{1,0},{2,1},{3,2},{4,3},{5,4},{6,5},{7,6},{8,7},{9,8},{10,9},{11,1... | collective-permute-start | bytes 884744 | tf_op jit(solution)/shard_map/ppermute | solution.py:15
  25.8 8.7 %copy-start.1 = (f32[1,576,10,256]{3,1,2,0:T(8,128)}, f32[1,576,10,256]{3,1,2,0:T(8,128)S(1)}, u32[]{:S(2)}) copy-start(f32[1,576,10,256]{3,1,2,0:T(8,128)S(1)} %maximum_convert_fusion.1) | copy-start | bytes 17694724
  39.9 282.1 %copy-start.13 = (f32[4]{0:T(128)S(1)}, f32[4]{0:T(128)}, u32[]{:S(2)}) copy-start(f32[4]{0:T(128)} %param.13) | copy-start | bytes 52
  48.6 674.8 %all-reduce.9.cloned.1.call-start = ((), (), s32[]{:S(2)}) async-start(), calls=%async_computation | async-start | bytes 1376256 | tf_op jit(solution)/shard_map/psum | solution.py:192
  321.3 11.6 %copy-start.5 = (f32[1,4,48,48]{3,2,1,0:T(8,128)S(1)}, f32[1,4,48,48]{3,2,1,0:T(8,128)}, u32[]{:S(2)}) copy-start(f32[1,4,48,48]{3,2,1,0:T(8,128)} %get-tuple-element.51) | copy-start | bytes 110596
  321.3 11.6 %copy-start.11 = (f32[1,4,48,48]{3,2,1,0:T(8,128)S(1)}, f32[1,4,48,48]{3,2,1,0:T(8,128)}, u32[]{:S(2)}) copy-start(f32[1,4,48,48]{3,2,1,0:T(8,128)} %get-tuple-element.54) | copy-start | bytes 110596
  325.4 77.0 %copy-start.17 = (f32[1,4,48]{2,1,0:T(4,128)S(1)}, f32[1,4,48]{2,1,0:T(4,128)}, u32[]{:S(2)}) copy-start(f32[1,4,48]{2,1,0:T(4,128)} %get-tuple-element.52) | copy-start | bytes 2308
  325.4 77.0 %copy-start.16 = (f32[1,4,48]{2,1,0:T(4,128)S(1)}, f32[1,4,48]{2,1,0:T(4,128)}, u32[]{:S(2)}) copy-start(f32[1,4,48]{2,1,0:T(4,128)} %get-tuple-element.53) | copy-start | bytes 2308
  332.9 73.0 %copy-start.6 = (bf16[1,4,48,2048]{3,2,1,0:T(8,128)(2,1)S(1)}, bf16[1,4,48,2048]{3,2,1,0:T(8,128)(2,1)}, u32[]{:S(2)}) copy-start(bf16[1,4,48,2048]{3,2,1,0:T(8,128)(2,1)} %convolution_bitcast_fusion) | copy-start | bytes 2359300
  404.1 2.9 slice-start
  406.0 1.7 slice-start.1
  421.1 10.8 %collective-permute-start.2 = (bf16[1,576,1,256]{3,1,2,0:T(8,128)(2,1)}, bf16[1,576,1,256]{3,1,2,0:T(8,128)(2,1)}, u32[]{:S(2)}, u32[]{:S(2)}) collective-permute-start(bf16[1,576,1,256]{3,1,2,0:T(8,128)(2,1)} %get-tuple-element.55), channel_id=1, source_target_pairs={{0,1},{1,2},{2,3},{3,4},{4,5},{5,6},{6,7},{7,8},{8,9},{9,10},{10,1... | collective-permute-start | bytes 884744 | tf_op jit(solution)/shard_map/ppermute | solution.py:14
  423.0 8.8 %collective-permute-start.3 = (bf16[1,576,1,256]{3,1,2,0:T(8,128)(2,1)}, bf16[1,576,1,256]{3,1,2,0:T(8,128)(2,1)}, u32[]{:S(2)}, u32[]{:S(2)}) collective-permute-start(bf16[1,576,1,256]{3,1,2,0:T(8,128)(2,1)} %get-tuple-element.56), channel_id=1, source_target_pairs={{1,0},{2,1},{3,2},{4,3},{5,4},{6,5},{7,6},{8,7},{9,8},{10,9},{11,1... | collective-permute-start | bytes 884744 | tf_op jit(solution)/shard_map/ppermute | solution.py:15
  431.8 4.1 copy-start.10
  433.4 2.5 copy-start.2
  464.6 0.7 copy-start.15
  464.9 4.3 copy-start.3
  466.1 1.2 copy-start.4
  466.1 79.4 %copy-start.8 = (bf16[1,192,8,256]{3,2,1,0:T(8,128)(2,1)S(1)}, bf16[1,192,8,256]{3,2,1,0:T(8,128)(2,1)}, u32[]{:S(2)}) copy-start(bf16[1,192,8,256]{3,2,1,0:T(8,128)(2,1)} %param.9) | copy-start | bytes 2359300
Sparse Core Ops, SparseCore 0:
  48.7 272.5 all-reduce.10
  471.1 252.2 all-reduce.8
where the time goes:
time: 735 us; the launch traced here: 734 us
  waiting for transfers between devices  454 us (62%)
  blocking collectives  142 us (19%)
  other arithmetic  57.7 us (8%)
  matrix products  26.2 us (4%)
  local copies, waits for them, and re-layouts  23.5 us (3%)
  starting transfers between devices  14.9 us (2%)
  between operations  14.6 us (2%)
    psum x1, waiting for transfers between devices, local(): gram_raw, query_sq, key_sq = lax.psum((gram_raw, query_sq, key_sq), 'tile')  273 us
    psum x1, waiting for transfers between devices, local(): lax.psum((triple_mixer_adjoint, spatial_stencil_adjoint, outgoing_mixer_a...  176 us
    psum x1, blocking collectives, local(): lax.psum((triple_mixer_adjoint, spatial_stencil_adjoint, outgoing_mixer_a...  74.6 us
    psum x1, blocking collectives, local(): row_terms, col_terms = lax.psum((row_terms, col_terms), 'tile')  67.8 us
    unnamed x2, other arithmetic  18.9 us
  transfers between devices with their start and end apart: 6, of which 4 were waited for; matrix products, arithmetic and copies ran while one was open for 1% of the time, Pallas kernels for 0%

commit v1 on v0

v1 whole, which is shorter than its diff:
```python
import functools

import jax
import jax.numpy as jnp
from jax import lax
from jax.experimental import pallas as pl
from jax.experimental.pallas import tpu as pltpu
from jax.sharding import PartitionSpec as P

F32 = jnp.float32
BF16 = jnp.bfloat16
AXES = ("img", "tile")
NT = (((1,), (1,)), ((), ()))
TN = (((0,), (0,)), ((), ()))
VMEM = pl.BlockSpec(memory_space=pltpu.VMEM)
SMEM = pl.BlockSpec(memory_space=pltpu.SMEM)
HI = lax.Precision.HIGHEST


def params(limit_mib):
    return pltpu.CompilerParams(vmem_limit_bytes=limit_mib << 20)


def call(body, outs, n_in, smem=(), scratch=(), limit=32, flops=0, name=None, moved=0):
    return pl.pallas_call(
        body,
        out_shape=tuple(jax.ShapeDtypeStruct(s, d) for s, d in outs),
        in_specs=[SMEM if i in smem else VMEM for i in range(n_in)],
        out_specs=tuple(VMEM for _ in outs),
        scratch_shapes=list(scratch),
        compiler_params=params(limit),
        cost_estimate=pl.CostEstimate(flops=flops, bytes_accessed=moved, transcendentals=0),
        name=name,
    )


def mm(a, b, dims=None, precision=None):
    dims = dims or (((1,), (0,)), ((), ()))
    return lax.dot_general(a, b, dims, preferred_element_type=F32, precision=precision)


def iota(shape, axis):
    return lax.broadcasted_iota(jnp.int32, shape, axis)


def to_column(row):
    n = row.shape[1]
    eye = iota((n, n), 0) == iota((n, n), 1)
    return jnp.sum(jnp.where(eye, row, 0.0), axis=1, keepdims=True)


def shift_right(v):
    return jnp.where(iota(v.shape, 1) == 0, 0.0, pltpu.roll(v, 1, 1))


def shift_left(v):
    n = v.shape[1]
    return jnp.where(iota(v.shape, 1) == n - 1, 0.0, pltpu.roll(v, n - 1, 1))


def spread_body(x_ref, dy_ref, x2_ref, dy2_ref, up_ref, dn_ref, s):
    c, rows, w = x_ref.shape
    for src, dst, k, off in ((x_ref, x2_ref, 2, 0), (dy_ref, dy2_ref, 1, 2)):
        for i in range(w // 128):
            block = src[:, :, i * 128 : (i + 1) * 128]
            s[i, :, :] = block.astype(F32).reshape(c * rows, 128)
        for h in range(rows):
            v = [s[i, pl.ds(h, c, stride=rows), :] for i in range(w // 128)]
            v = jnp.concatenate(v, axis=1).astype(BF16)
            dst[:, h * w : (h + 1) * w] = v
            if h < k:
                dn_ref[:, (off + h) * w : (off + h + 1) * w] = v
            if h >= rows - k:
                u = off + h - rows + k
                up_ref[:, u * w : (u + 1) * w] = v


def normalise(x, gain, bias):
    average = jnp.mean(x, axis=0, keepdims=True)
    centered = x - average
    inverse = lax.rsqrt(jnp.mean(centered * centered, axis=0, keepdims=True) + 1e-05)
    standard = centered * inverse
    return standard, inverse, (standard * gain + bias).astype(BF16)


def project_body(x2_ref, w_ref, gain_ref, bias_ref, p_ref, std_ref, inv_ref, *, w):
    gain = to_column(gain_ref[...])
    bias = to_column(bias_ref[...])
    for h in range(x2_ref.shape[1] // w):
        at = slice(h * w, (h + 1) * w)
        standard, inverse, normed = normalise(x2_ref[:, at].astype(F32), gain, bias)
        std_ref[:, at] = standard.astype(BF16)
        inv_ref[:, at] = jnp.broadcast_to(inverse, (8, w))
        p_ref[:, at] = mm(w_ref[...], normed).astype(BF16)


def taps_to_columns(taps_ref, wide, coef):
    n = taps_ref.shape[2]
    wide[...] = jnp.zeros_like(wide)
    for a in range(3):
        for b in range(3):
            wide[3 * a + b : 3 * a + b + 1, 0:n] = taps_ref[a, b : b + 1, :]
    coef[...] = wide[...].T


def mix_body(
    flags, p_ref, up_ref, dn_ref, dy2_ref, w_ref, wot_ref, taps_ref, gain_ref, bias_ref,
    mixed_ref, ph_ref, pay_ref, t_ref, wide, coef, sq, gs, *, w, heads,
):
    c3 = p_ref.shape[0]
    c = c3 // 3
    hs = c // heads
    rows = p_ref.shape[1] // w
    gain = to_column(gain_ref[...])
    bias = to_column(bias_ref[...])
    keep_up = 1.0 - flags[0].astype(F32)
    keep_dn = 1.0 - flags[1].astype(F32)
    for src, keep, base in ((up_ref, keep_up, 0), (dn_ref, keep_dn, 2)):
        for h in range(2):
            normed = normalise(src[:, h * w : (h + 1) * w].astype(F32), gain, bias)[2]
            at = slice((base + h) * w, (base + h + 1) * w)
            ph_ref[:, at] = (mm(w_ref[...], normed) * keep).astype(BF16)
    taps_to_columns(taps_ref, wide, coef)

    def group(g, carry):
        ch = pl.ds(pl.multiple_of(g * 16, 16), 16)
        cf = coef[ch, :]
        k = [jnp.broadcast_to(cf[:, t : t + 1], (16, w)) for t in range(9)]

        def row(r):
            if r < 0:
                return ph_ref[ch, (r + 2) * w : (r + 3) * w].astype(F32)
            if r >= rows:
                return ph_ref[ch, (r - rows + 2) * w : (r - rows + 3) * w].astype(F32)
            return p_ref[ch, r * w : (r + 1) * w].astype(F32)

        window = [row(-2), row(-1), None]
        total = jnp.zeros((16, w), F32)
        for r in range(-1, rows + 1):
            window[2] = row(r + 1)
            u = [sum(k[3 * a + b] * window[a] for a in range(3)) for b in range(3)]
            out = (u[1] + shift_right(u[0]) + shift_left(u[2])).astype(BF16)
            mixed_ref[ch, (r + 1) * w : (r + 2) * w] = out
            if 0 <= r < rows:
                out = out.astype(F32)
                total = total + out * out
            window = [window[1], window[2], None]
        sq[ch, :] = jnp.broadcast_to(jnp.sum(total, axis=1, keepdims=True), (16, 128))
        return carry

    lax.fori_loop(0, c3 // 16, group, 0)

    own = slice(w, (rows + 1) * w)
    query = mixed_ref[0:c, own]
    key = mixed_ref[c : 2 * c, own]
    value = mixed_ref[2 * c : 3 * c, own]
    gs[0, :, 0:c] = mm(query, key, NT)
    t = mm(dy2_ref[...], value, NT)
    t_ref[...] = t
    gs[1, :, 0:c] = mm(wot_ref[...].astype(F32), t, precision=HI)
    lane = iota((hs, 128), 1)
    for h in range(heads):
        at = slice(h * hs, (h + 1) * hs)
        gram = pltpu.roll(gs[0, at, :], (256 - hs * h) % 256, 1)[:, 0:128]
        grad = pltpu.roll(gs[1, at, :], (256 + hs - hs * h) % 256, 1)[:, 0:128]
        key_sq = sq[c + h * hs : c + (h + 1) * hs, :]
        rest = jnp.where(lane == 2 * hs, sq[at, :], key_sq)
        pay_ref[at, :] = jnp.where(lane < hs, gram, jnp.where(lane < 2 * hs, grad, rest))


def back_body(
    flags, sharp, mine_ref, other_ref, mixed_ref, p_ref, ph_ref, dy2_ref, up_ref, dn_ref, std_ref,
    t_ref, wot_ref, taps_ref,
    gp_ref, left_ref, right_ref, pay, wide, coef, mats, vecs, gm, aug, grads, *, w, heads,
):
    c = mixed_ref.shape[0] // 3
    hs = c // heads
    rows = p_ref.shape[1] // w
    first_core = flags[3] == 0
    mine = mine_ref[...]
    other = other_ref[...]
    pay[0 : c // 2, :] = jnp.where(first_core, mine, other)
    pay[c // 2 : c, :] = jnp.where(first_core, other, mine)
    lane = iota((hs, 128), 1)
    valid = lane < hs
    eye = lane == iota((hs, 128), 0)
    pad = jnp.zeros((hs, 128), F32)
    sharp_row = jnp.zeros((1, 128), F32)
    for h in range(heads):
        at = slice(h * hs, (h + 1) * hs)
        block = pay[at, :]
        gram = jnp.where(valid, block, 0.0)
        grad = jnp.where(valid, pltpu.roll(block, 128 - hs, 1), 0.0)
        query_sq = block[:, 2 * hs : 2 * hs + 1] + 1e-06
        key_sq = (
            jnp.sum(jnp.where(eye, block[:, 2 * hs + 1 : 2 * hs + 2], 0.0), axis=0, keepdims=True)
            + 1e-06
        )
        length = jnp.sqrt(query_sq) * jnp.sqrt(key_sq)
        cosine = gram / length
        weights = jnp.where(valid, jnp.exp(cosine * sharp[h]), 0.0)
        attention = weights / jnp.sum(weights, axis=1, keepdims=True)
        scores = attention * (grad - jnp.sum(attention * grad, axis=1, keepdims=True))
        terms = scores * cosine
        sharp_h = jnp.sum(jnp.sum(terms, axis=1, keepdims=True), axis=0, keepdims=True)
        sharp_row = jnp.where(iota((1, 128), 1) == h, sharp_h, sharp_row)
        grad_cos = scores * sharp[h]
        terms = grad_cos * cosine
        alpha = jnp.sum(terms, axis=1, keepdims=True) / query_sq
        beta = jnp.sum(terms, axis=0, keepdims=True) / key_sq
        beta = jnp.sum(jnp.where(eye, beta, 0.0), axis=1, keepdims=True)
        vecs[at, 0:128] = jnp.broadcast_to(alpha, (hs, 128))
        vecs[at, 128:256] = jnp.broadcast_to(beta, (hs, 128))
        for i, m in enumerate((grad_cos / length, attention)):
            placed = pltpu.roll(jnp.concatenate([m, pad], axis=1), hs * h, 1)
            mats[i, at, :] = placed.astype(BF16)

    grad_gram = mats[0, :, 0:c]
    grad_gram_t = grad_gram.astype(F32).T.astype(BF16)
    attention_b = mats[1, :, 0:c]
    attention_t = attention_b.astype(F32).T.astype(BF16)
    outgoing = mm(t_ref[...], attention_b.astype(F32), NT, precision=HI)
    alpha = jnp.concatenate([vecs[:, 0:128]] * (w // 128), axis=1)
    beta = jnp.concatenate([vecs[:, 128:256]] * (w // 128), axis=1)
    wot = wot_ref[...]
    for r in range(rows + 2):
        at = slice(r * w, (r + 1) * w)
        if r == 0:
            dy = up_ref[:, 2 * w : 3 * w]
        elif r == rows + 1:
            dy = dn_ref[:, 2 * w : 3 * w]
        else:
            dy = dy2_ref[:, (r - 1) * w : r * w]
        query = mixed_ref[0:c, at]
        key = mixed_ref[c : 2 * c, at]
        grad_attended = mm(wot, dy).astype(BF16)
        parts = (
            mm(grad_gram, key) - query.astype(F32) * alpha,
            mm(grad_gram_t, query) - key.astype(F32) * beta,
            mm(attention_t, grad_attended),
        )
        for i, part in enumerate(parts):
            if r == 0:
                part = part * (1.0 - flags[0].astype(F32))
            if r == rows + 1:
                part = part * (1.0 - flags[1].astype(F32))
            gm[i * c : (i + 1) * c, at] = part.astype(BF16)

    taps_to_columns(taps_ref, wide, coef)

    def group(g, carry):
        ch = pl.ds(pl.multiple_of(g * 16, 16), 16)
        cf = coef[ch, :]
        k = [jnp.broadcast_to(cf[:, t : t + 1], (16, w)) for t in range(9)]
        window = [None, gm[ch, 0:w].astype(F32), gm[ch, w : 2 * w].astype(F32)]
        for r in range(rows):
            window = [window[1], window[2], gm[ch, (r + 2) * w : (r + 3) * w].astype(F32)]
            u = [sum(k[3 * a + b] * window[2 - a] for a in range(3)) for b in range(3)]
            out = u[1] + shift_left(u[0]) + shift_right(u[2])
            gp_ref[ch, r * w : (r + 1) * w] = out.astype(BF16)
        return carry

    lax.fori_loop(0, gm.shape[0] // 16, group, 0)

    def stencil(g, carry):
        ch = pl.ds(pl.multiple_of(g * 16, 16), 16)

        def row(r):
            if r < 0:
                return ph_ref[ch, w : 2 * w].astype(F32)
            if r >= rows:
                return ph_ref[ch, 2 * w : 3 * w].astype(F32)
            return p_ref[ch, r * w : (r + 1) * w].astype(F32)

        acc = [jnp.zeros((16, 128), F32) for _ in range(9)]
        window = [None, row(-1), row(0)]
        for r in range(rows):
            window = [window[1], window[2], row(r + 1)]
            v = gm[ch, (r + 1) * w : (r + 2) * w].astype(F32)
            moved = (shift_left(v), v, shift_right(v))
            for a in range(3):
                for b in range(3):
                    prod = moved[b] * window[a]
                    for i in range(w // 128):
                        acc[3 * a + b] = acc[3 * a + b] + prod[:, i * 128 : (i + 1) * 128]
        lanes = iota((16, 128), 1)
        out = jnp.zeros((16, 128), F32)
        for t in range(9):
            out = jnp.where(lanes == t, jnp.sum(acc[t], axis=1, keepdims=True), out)
        coef[ch, :] = out
        return carry

    lax.fori_loop(0, gm.shape[0] // 16, stencil, 0)

    aug[0:c, :] = std_ref[...]
    aug[c : c + 16, :] = jnp.where(iota((16, rows * w), 0) == 0, 1.0, 0.0).astype(BF16)
    c3 = 3 * c
    grads[...] = jnp.zeros_like(grads)
    grads[0 : c + 16, 0:c3] = mm(aug[...], gp_ref[...], NT)
    grads[c + 16 : c + 32, :] = coef[...].T[0:16, :]
    lead = 1.0 - jnp.minimum(flags[2], 1).astype(F32)
    grads[c + 1 : c + 2, 0:128] = sharp_row * lead
    out_pad = jnp.concatenate([outgoing, jnp.zeros((c, 256 - c), F32)], axis=1)
    half = c3 % 128
    tail = grads[0:c, c3 - half : c3 - half + 128]
    moved = pltpu.roll(out_pad[:, 128:256], half, 1)
    grads[0:c, c3 - half : c3 - half + 128] = jnp.where(iota((c, 128), 1) < half, tail, moved)
    left_ref[...] = grads[:, 0:384].astype(BF16)
    right_ref[:, 0:256] = grads[:, 384:640].astype(BF16)
    right_ref[0:c, 256:384] = out_pad[:, 0:128].astype(BF16)
    right_ref[c : c + 32, 256:384] = jnp.zeros((32, 128), BF16)


def output_body(gp_ref, wt_ref, std_ref, inv_ref, dy_ref, gain_ref, out_ref, s, *, w):
    c, rows, _ = out_ref.shape
    gain = to_column(gain_ref[...])
    for h in range(rows):
        at = slice(h * w, (h + 1) * w)
        scaled = mm(wt_ref[...], gp_ref[:, at]) * gain
        standard = std_ref[:, at].astype(F32)
        first = jnp.mean(scaled, axis=0, keepdims=True)
        second = jnp.mean(scaled * standard, axis=0, keepdims=True)
        v = (scaled - first - standard * second) * inv_ref[0:1, at]
        for i in range(w // 128):
            s[i, pl.ds(h, c, stride=rows), :] = v[:, i * 128 : (i + 1) * 128]
    for i in range(w // 128):
        at = slice(i * 128, (i + 1) * 128)
        v = dy_ref[:, :, at].astype(F32) + s[i, :, :].reshape(c, rows, 128)
        out_ref[:, :, at] = v.astype(BF16)


def finish_body(
    flags, mine_ref, other_ref, wt_ref, gain_ref, bias_ref,
    triple_ref, taps_ref, outgoing_ref, sharp_ref, scaling_ref, offset_ref, full,
):
    c, c3 = wt_ref.shape
    first_core = flags[3] == 0
    mine = mine_ref[...].astype(F32)
    other = other_ref[...].astype(F32)
    full[:, 0:384] = jnp.where(first_core, mine, other)
    full[:, 384:768] = jnp.where(first_core, other, mine)
    m = full[0:c, 0:c3]
    s = full[c : c + 1, 0:c3]
    gain = to_column(gain_ref[...])
    bias = to_column(bias_ref[...])
    wt = wt_ref[...].astype(F32)
    triple_ref[...] = m * gain + bias * s
    eye = iota((c, c), 0) == iota((c, c), 1)
    scaling = jnp.sum(wt * m, axis=1, keepdims=True)
    offset = jnp.sum(wt * s, axis=1, keepdims=True)
    scaling_ref[...] = jnp.sum(jnp.where(eye, scaling, 0.0), axis=0, keepdims=True)
    offset_ref[...] = jnp.sum(jnp.where(eye, offset, 0.0), axis=0, keepdims=True)
    for a in range(3):
        taps_ref[a, :, :] = full[c + 16 + 3 * a : c + 19 + 3 * a, 0:c3]
    half = c3 % 128
    outgoing_ref[:, 0:128] = full[0:c, 640:768]
    tail = pltpu.roll(full[0:c, 512:640], 128 - half, 1)
    outgoing_ref[:, 128:c] = tail[:, 0 : c - 128]
    sharp_ref[...] = full[c + 1 : c + 2, 0:128]


def swap(v, even, odd, count):
    pairs = [(i, i ^ (odd if i & 1 else even)) for i in range(count)]
    return lax.ppermute(v, AXES, pairs)


def rounds(total, tile):
    if total == 256 and tile == 32:
        inner = ((2, 8), (6, 16), (8, 2), (16, 6))
        outer = ((2, 64), (6, 192), (8, 2), (16, 6), (48, 8), (64, 16), (192, 48))
        return inner, outer
    bits = [1 << i for i in range(1, 20)]
    return tuple((b, b) for b in bits if b < tile), tuple((b, b) for b in bits if b < total)


def solution(mesh):
    img, tile = (mesh.shape["img"], mesh.shape["tile"])
    total = img * tile
    inner, outer = rounds(total, tile)

    def local(x, dy, triple, stencil, out_mixer, sharpness, gain, bias):
        _, c, rows, w = x.shape
        heads = sharpness.shape[0]
        c3 = 3 * c
        n = rows * w
        ext = (rows + 2) * w
        place = lax.axis_index("tile")
        core = place % 2
        flags = jnp.stack([place == 0, place == tile - 1, place, core]).astype(jnp.int32)
        x3 = x.reshape(c, rows, w)
        dy3 = dy.reshape(c, rows, w)
        taps = jnp.transpose(stencil, (1, 2, 0))
        wt = triple.T
        wot = out_mixer.T
        gain_row = gain.reshape(1, c)
        bias_row = bias.reshape(1, c)

        x2, dy2, up, dn = call(
            spread_body,
            [((c, n), BF16), ((c, n), BF16), ((c, 3 * w), BF16), ((c, 3 * w), BF16)],
            2,
            scratch=[pltpu.VMEM((w // 128, c * rows, 128), F32)],
            limit=16,
            name="spread",
            moved=4 << 20,
        )(x3, dy3)
        up_in = lax.ppermute(up, "tile", [(i, i + 1) for i in range(tile - 1)])
        dn_in = lax.ppermute(dn, "tile", [(i + 1, i) for i in range(tile - 1)])
        p, std, inv = call(
            functools.partial(project_body, w=w),
            [((c3, n), BF16), ((c, n), BF16), ((8, n), F32)],
            4,
            limit=16,
            flops=2 * c3 * c * n,
            moved=8 << 20,
            name="project",
        )(x2, triple, gain_row, bias_row)
        mixed, ph, pay, t = call(
            functools.partial(mix_body, w=w, heads=heads),
            [((c3, ext), BF16), ((c3, 4 * w), BF16), ((c, 128), F32), ((c, c), F32)],
            10,
            smem=(0,),
            scratch=[
                pltpu.VMEM((128, 640), F32),
                pltpu.VMEM((640, 128), F32),
                pltpu.VMEM((c3, 128), F32),
                pltpu.VMEM((2, c, 256), F32),
            ],
            flops=8 * c * c * n,
            moved=8 << 20,
            name="mix",
        )(flags, p, up_in, dn_in, dy2, triple, wot, taps, gain_row, bias_row)

        half = c // 2
        mine = jnp.where(core == 0, pay[:half], pay[half:])
        theirs = jnp.where(core == 0, pay[half:], pay[:half])
        mine = mine + swap(theirs, 1, 1, total)
        for even, odd in inner:
            mine = mine + swap(mine, even, odd, total)
        other = swap(mine, 1, 1, total)

        gp, left, right = call(
            functools.partial(back_body, w=w, heads=heads),
            [((c3, n), BF16), ((c + 32, 384), BF16), ((c + 32, 384), BF16)],
            14,
            smem=(0, 1),
            scratch=[
                pltpu.VMEM((c, 128), F32),
                pltpu.VMEM((128, 640), F32),
                pltpu.VMEM((640, 128), F32),
                pltpu.VMEM((2, c, 256), BF16),
                pltpu.VMEM((c, 256), F32),
                pltpu.VMEM((c3, ext), BF16),
                pltpu.VMEM((c + 16, n), BF16),
                pltpu.VMEM((c + 32, 640), F32),
            ],
            flops=20 * c * c * n,
            moved=8 << 20,
            name="back",
        )(flags, sharpness, mine, other, mixed, p, ph, dy2, up_in, dn_in, std, t, wot, taps)

        part = jnp.where(core == 0, left, right)
        away = jnp.where(core == 0, right, left)

        def add(a, b):
            return (a.astype(F32) + b.astype(F32)).astype(BF16)

        part = add(part, swap(away, 1, 1, total))
        for even, odd in outer:
            part = add(part, swap(part, even, odd, total))
        rest = swap(part, 1, 1, total)

        (fm,) = call(
            functools.partial(output_body, w=w),
            [((c, rows, w), BF16)],
            6,
            scratch=[pltpu.VMEM((w // 128, c * rows, 128), F32)],
            limit=24,
            flops=2 * c3 * c * n,
            moved=6 << 20,
            name="output",
        )(gp, wt, std, inv, dy3, gain_row)
        outs = call(
            finish_body,
            [((c, c3), F32), ((3, 3, c3), F32), ((c, c), F32), ((1, 128), F32), ((1, c), F32), ((1, c), F32)],
            6,
            smem=(0,),
            scratch=[pltpu.VMEM((c + 32, 768), F32)],
            limit=16,
            name="finish",
            moved=2 << 20,
        )(flags, part, rest, wt, gain_row, bias_row)
        triple_t, taps_t, outgoing, sharp_row, scaling, offset = outs
        return (
            fm.reshape(x.shape),
            triple_t.T,
            jnp.transpose(taps_t, (2, 0, 1)),
            outgoing,
            sharp_row[0, :heads],
            scaling.reshape(c),
            offset.reshape(c),
        )

    return jax.shard_map(
        local,
        mesh=mesh,
        in_specs=(P("img", None, "tile", None), P("img", None, "tile", None)) + (P(),) * 6,
        out_specs=(P("img", None, "tile", None),) + (P(),) * 6,
        check_vma=False,
    )
```

time: 735 us -> 129 us (0.18)
  waiting for transfers between devices: 454 us -> 39.5 us
  blocking collectives: 142 us -> 0 us
  other arithmetic: 57.7 us -> 0.55 us
  Pallas kernels: 0 us -> 40.1 us
  starting transfers between devices: 14.9 us -> 42.4 us
  matrix products: 26.2 us -> 0 us
  local copies, waits for them, and re-layouts: 23.5 us -> 4.9 us
  between operations: 14.6 us -> 0.85 us
    psum x2 -> x0, waiting for transfers between devices: 449 us -> none  [the longest x1 273 us: local(): gram_raw, query_sq, key_sq = lax.psum((gram_raw, query_sq, key_sq), 'tile')]
    psum x2 -> x0, blocking collectives: 142 us -> none  [the longest x1 74.6 us: local(): lax.psum((triple_mixer_adjoint, spatial_stencil_adjoint, outgoing_mixer_a...]
    pallas_call x0 -> x6, Pallas kernels: none -> 40.1 us  [the longest x1 19.9 us: local(): call(functools.partial(back_body, w=w, heads=heads), [((c3, n), BF16), ((...]
    ppermute x4 -> x17, waiting for transfers between devices: 5.38 us -> 39.5 us  [the longest x15 36.8 us: swap(): return lax.ppermute(v, AXES, pairs)]
    ppermute x4 -> x17, starting transfers between devices: 14.9 us -> 42.4 us  [the longest x15 35.9 us: swap(): return lax.ppermute(v, AXES, pairs)]
    dot_general x11 -> x0, matrix products: 26.2 us -> none  [the longest x1 9.72 us: local(): jnp.einsum('bop,bcp->oc', flat_gproj, normed.reshape(images, channels, pi...]
    reduce_sum x9 -> x0, other arithmetic: 20.5 us -> none  [the longest x1 12.1 us: kernel_grad(): jnp.sum(grad_float * widened[..., row_off:row_off + row_count, col_off:co...]
    unnamed x2 -> x0, other arithmetic: 18.9 us -> none
  transfers between devices with their start and end apart: 6 -> 17, of which waited for: 4 -> 15; matrix products, arithmetic and copies ran while one was open for 1% -> 2% of each run, Pallas kernels for 0% -> 3%
where the time goes in v1:
time: 129 us; the launch traced here: 128 us
  starting transfers between devices  42.4 us (33%)
  Pallas kernels  40.1 us (31%)
  waiting for transfers between devices  39.5 us (31%)
  local copies, waits for them, and re-layouts  4.9 us (4%)
    ppermute x15, waiting for transfers between devices, swap(): return lax.ppermute(v, AXES, pairs)  36.8 us
    ppermute x15, starting transfers between devices, swap(): return lax.ppermute(v, AXES, pairs)  35.9 us
    pallas_call x1, Pallas kernels, local(): call(functools.partial(back_body, w=w, heads=heads), [((c3, n), BF16), ((...  19.9 us
    pallas_call x1, Pallas kernels, local(): call(functools.partial(mix_body, w=w, heads=heads), [((c3, ext), BF16), (...  13.9 us
    ppermute x1, starting transfers between devices, local(): up_in = lax.ppermute(up, 'tile', [(i, i + 1) for i in range(tile - 1)])  4.58 us
    unnamed x18, local copies, waits for them, and re-layouts  4.39 us
    ppermute x1, waiting for transfers between devices, local(): dn_in = lax.ppermute(dn, 'tile', [(i + 1, i) for i in range(tile - 1)])  2.64 us
    pallas_call x1, Pallas kernels, local(): call(functools.partial(output_body, w=w), [((c, rows, w), BF16)], 6, scra...  2.58 us
  transfers between devices with their start and end apart: 17, of which 15 were waited for; matrix products, arithmetic and copies ran while one was open for 2% of the time, Pallas kernels for 3%

profile of v1, /device:TPU:1, one launch (start us, length us, event | category | flops | bytes accessed | tf_op | source)
XLA Modules:
  0.0 128.3 jit_solution(7256784066541100507)
XLA Ops:
  0.6 0.0 copy-start.6
  0.6 0.0 copy-start.5
  0.7 0.0 copy-start
  0.7 1.1 copy-done
  1.8 0.0 copy-start.3
  1.8 1.1 copy-done.3
  2.9 0.0 copy-start.4
  2.9 0.8 spread.1
  3.8 4.6 %collective-permute-start = (bf16[192,768]{1,0:T(8,128)(2,1)S(1)}, bf16[192,768]{1,0:T(8,128)(2,1)S(1)}, u32[]{:S(2)}, u32[]{:S(2)}) collective-permute-start(bf16[192,768]{1,0:T(8,128)(2,1)S(1)} %get-tuple-element.29), channel_id=1, source_target_pairs={{0,1},{1,2},{2,3},{3,4},{4,5},{5,6},{6,7},{7,8},{8,9},{9,10},{10,1... | collective-permute-start | bytes 884744 | tf_op jit(solution)/shard_map/ppermute | solution.py:407
  8.4 1.9 %collective-permute-start.1 = (bf16[192,768]{1,0:T(8,128)(2,1)S(1)}, bf16[192,768]{1,0:T(8,128)(2,1)S(1)}, u32[]{:S(2)}, u32[]{:S(2)}) collective-permute-start(bf16[192,768]{1,0:T(8,128)(2,1)S(1)} %get-tuple-element.30), channel_id=1, source_target_pairs={{1,0},{2,1},{3,2},{4,3},{5,4},{6,5},{7,6},{8,7},{9,8},{10,9},{11,1... | collective-permute-start | bytes 884744 | tf_op jit(solution)/shard_map/ppermute | solution.py:408
  10.3 1.0 copy.16
  11.3 1.1 copy.15.w_ref
  12.4 0.0 copy-done.6
  12.4 0.0 copy-done.5
  12.4 1.2 project.1
  13.7 0.1 pad_add_fusion.flags
  13.8 0.0 collective-permute-done.up_ref
  13.8 2.6 %collective-permute-done.1.dn_ref = bf16[192,768]{1,0:T(8,128)(2,1)S(1)} collective-permute-done((bf16[192,768]{1,0:T(8,128)(2,1)S(1)}, bf16[192,768]{1,0:T(8,128)(2,1)S(1)}, u32[]{:S(2)}, u32[]{:S(2)}) %collective-permute-start.1) | collective-permute-done | bytes 294944 | tf_op jit(solution)/shard_map/ppermute | solution.py:408
  16.4 0.0 copy-done.4
  16.4 0.0 copy-start.7
  16.4 13.9 %mix.1 = (bf16[576,2560]{1,0:T(8,128)(2,1)S(1)}, bf16[576,1024]{1,0:T(8,128)(2,1)S(1)}, f32[192,128]{1,0:T(8,128)S(1)}, f32[192,192]{1,0:T(8,128)S(1)}) custom-call(s32[4]{0:T(128)S(1)} %pad_add_fusion.flags, bf16[576,2048]{1,0:T(8,128)(2,1)S(1)} %get-tuple-element.28.p_ref, bf16[192,768]{1,0:T(8,128)(2,1)S(1)} %collective-permute-done.up_ref, ...), custom_call_target="tpu_custom_call" | custom-call | flops 603979776 | bytes 8388608 | tf_op jit(solution)/shard_map/mix/pallas_call | solution.py:418
  30.4 0.1 collective-permute-start.2
  30.5 1.2 collective-permute-done.2
  31.7 2.1 %collective-permute-start.3 = (f32[96,128]{1,0:T(8,128)S(1)}, f32[96,128]{1,0:T(8,128)S(1)}, u32[]{:S(2)}, u32[]{:S(2)}) collective-permute-start(f32[96,128]{1,0:T(8,128)S(1)} %select_add_fusion), channel_id=1, source_target_pairs={{0,2},{1,9},{2,0},{3,11},{4,6},{5,13},{6,4},{7,15},{8,10},{9,1},{1... | collective-permute-start | bytes 147464 | tf_op jit(solution)/shard_map/ppermute | solution.py:364
  33.8 1.8 %collective-permute-done.3 = f32[96,128]{1,0:T(8,128)S(1)} collective-permute-done((f32[96,128]{1,0:T(8,128)S(1)}, f32[96,128]{1,0:T(8,128)S(1)}, u32[]{:S(2)}, u32[]{:S(2)}) %collective-permute-start.3) | collective-permute-done | bytes 49184 | tf_op jit(solution)/shard_map/ppermute | solution.py:364
  35.6 2.8 %collective-permute-start.4 = (f32[96,128]{1,0:T(8,128)S(1)}, f32[96,128]{1,0:T(8,128)S(1)}, u32[]{:S(2)}, u32[]{:S(2)}) collective-permute-start(f32[96,128]{1,0:T(8,128)S(1)} %add.45), channel_id=1, source_target_pairs={{0,6},{1,17},{2,4},{3,19},{4,2},{5,21},{6,0},{7,23},{8,14},{9,25},... | collective-permute-start | bytes 147464 | tf_op jit(solution)/shard_map/ppermute | solution.py:364
  38.4 1.5 %collective-permute-done.4 = f32[96,128]{1,0:T(8,128)S(1)} collective-permute-done((f32[96,128]{1,0:T(8,128)S(1)}, f32[96,128]{1,0:T(8,128)S(1)}, u32[]{:S(2)}, u32[]{:S(2)}) %collective-permute-start.4) | collective-permute-done | bytes 49184 | tf_op jit(solution)/shard_map/ppermute | solution.py:364
  39.9 1.3 collective-permute-start.5
  41.2 1.8 %collective-permute-done.5 = f32[96,128]{1,0:T(8,128)S(1)} collective-permute-done((f32[96,128]{1,0:T(8,128)S(1)}, f32[96,128]{1,0:T(8,128)S(1)}, u32[]{:S(2)}, u32[]{:S(2)}) %collective-permute-start.5) | collective-permute-done | bytes 49184 | tf_op jit(solution)/shard_map/ppermute | solution.py:364
  42.9 4.3 %collective-permute-start.6 = (f32[96,128]{1,0:T(8,128)S(1)}, f32[96,128]{1,0:T(8,128)S(1)}, u32[]{:S(2)}, u32[]{:S(2)}) collective-permute-start(f32[96,128]{1,0:T(8,128)S(1)} %add.47), channel_id=1, source_target_pairs={{0,16},{1,7},{2,18},{3,5},{4,20},{5,3},{6,22},{7,1},{8,24},{9,15},... | collective-permute-start | bytes 147464 | tf_op jit(solution)/shard_map/ppermute | solution.py:364
  47.3 1.5 %collective-permute-done.6 = f32[96,128]{1,0:T(8,128)S(1)} collective-permute-done((f32[96,128]{1,0:T(8,128)S(1)}, f32[96,128]{1,0:T(8,128)S(1)}, u32[]{:S(2)}, u32[]{:S(2)}) %collective-permute-start.6) | collective-permute-done | bytes 49184 | tf_op jit(solution)/shard_map/ppermute | solution.py:364
  48.8 4.3 %collective-permute-start.7 = (f32[96,128]{1,0:T(8,128)S(1)}, f32[96,128]{1,0:T(8,128)S(1)}, u32[]{:S(2)}, u32[]{:S(2)}) collective-permute-start(f32[96,128]{1,0:T(8,128)S(1)} %add.48.mine_ref), channel_id=1, source_target_pairs={{0,1},{1,0},{2,3},{3,2},{4,5},{5,4},{6,7},{7,6},{8,9},{9,8},{10,11... | collective-permute-start | bytes 147464 | tf_op jit(solution)/shard_map/ppermute | solution.py:364
  53.0 0.9 collective-permute-done.7.other_ref
  53.9 0.0 copy-done.7
  53.9 19.9 %back.1 = (bf16[576,2048]{1,0:T(8,128)(2,1)S(1)}, bf16[224,384]{1,0:T(8,128)(2,1)S(1)}, bf16[224,384]{1,0:T(8,128)(2,1)S(1)}) custom-call(s32[4]{0:T(128)S(1)} %pad_add_fusion.flags, f32[4]{0:T(128)S(1)} %copy-done.7, f32[96,128]{1,0:T(8,128)S(1)} %add.48.mine_ref, f32[96,128]{1,0:T(8,128)S(1)} %collective-permute-done.7.other_ref, ...), custom_call_target="tpu_custom_call" | custom-call | flops 1509949440 | bytes 8388608 | tf_op jit(solution)/shard_map/back/pallas_call | solution.py:442
  73.8 0.0 copy-start.1
  73.9 0.0 copy-start.2
  73.9 0.4 collective-permute-start.8
  74.3 1.1 collective-permute-done.8
  75.4 0.1 add_convert_fusion.7
  75.5 1.3 %collective-permute-start.9 = (bf16[224,384]{1,0:T(8,128)(2,1)S(1)}, bf16[224,384]{1,0:T(8,128)(2,1)S(1)}, u32[]{:S(2)}, u32[]{:S(2)}) collective-permute-start(bf16[224,384]{1,0:T(8,128)(2,1)S(1)} %add_convert_fusion.7), channel_id=1, source_target_pairs={{0,2},{1,65},{2,0},{3,67},{4,6},{5,69},{6,4},{7,71},{8,10},{9,73},... | collective-permute-start | bytes 516104 | tf_op jit(solution)/shard_map/ppermute | solution.py:364
  76.8 3.3 %collective-permute-done.9 = bf16[224,384]{1,0:T(8,128)(2,1)S(1)} collective-permute-done((bf16[224,384]{1,0:T(8,128)(2,1)S(1)}, bf16[224,384]{1,0:T(8,128)(2,1)S(1)}, u32[]{:S(2)}, u32[]{:S(2)}) %collective-permute-start.9) | collective-permute-done | bytes 172064 | tf_op jit(solution)/shard_map/ppermute | solution.py:364
  80.2 2.7 %collective-permute-start.10 = (bf16[224,384]{1,0:T(8,128)(2,1)S(1)}, bf16[224,384]{1,0:T(8,128)(2,1)S(1)}, u32[]{:S(2)}, u32[]{:S(2)}) collective-permute-start(bf16[224,384]{1,0:T(8,128)(2,1)S(1)} %add_convert_fusion.6), channel_id=1, source_target_pairs={{0,6},{1,193},{2,4},{3,195},{4,2},{5,197},{6,0},{7,199},{8,14},{9,... | collective-permute-start | bytes 516104 | tf_op jit(solution)/shard_map/ppermute | solution.py:364
  82.9 3.3 %collective-permute-done.10 = bf16[224,384]{1,0:T(8,128)(2,1)S(1)} collective-permute-done((bf16[224,384]{1,0:T(8,128)(2,1)S(1)}, bf16[224,384]{1,0:T(8,128)(2,1)S(1)}, u32[]{:S(2)}, u32[]{:S(2)}) %collective-permute-start.10) | collective-permute-done | bytes 172064 | tf_op jit(solution)/shard_map/ppermute | solution.py:364
  86.2 0.1 collective-permute-start.11
  86.3 4.2 %collective-permute-done.11 = bf16[224,384]{1,0:T(8,128)(2,1)S(1)} collective-permute-done((bf16[224,384]{1,0:T(8,128)(2,1)S(1)}, bf16[224,384]{1,0:T(8,128)(2,1)S(1)}, u32[]{:S(2)}, u32[]{:S(2)}) %collective-permute-start.11) | collective-permute-done | bytes 172064 | tf_op jit(solution)/shard_map/ppermute | solution.py:364
  90.6 3.0 %collective-permute-start.12 = (bf16[224,384]{1,0:T(8,128)(2,1)S(1)}, bf16[224,384]{1,0:T(8,128)(2,1)S(1)}, u32[]{:S(2)}, u32[]{:S(2)}) collective-permute-start(bf16[224,384]{1,0:T(8,128)(2,1)S(1)} %add_convert_fusion.4), channel_id=1, source_target_pairs={{0,16},{1,7},{2,18},{3,5},{4,20},{5,3},{6,22},{7,1},{8,24},{9,15},... | collective-permute-start | bytes 516104 | tf_op jit(solution)/shard_map/ppermute | solution.py:364
  93.7 2.8 %collective-permute-done.12 = bf16[224,384]{1,0:T(8,128)(2,1)S(1)} collective-permute-done((bf16[224,384]{1,0:T(8,128)(2,1)S(1)}, bf16[224,384]{1,0:T(8,128)(2,1)S(1)}, u32[]{:S(2)}, u32[]{:S(2)}) %collective-permute-start.12) | collective-permute-done | bytes 172064 | tf_op jit(solution)/shard_map/ppermute | solution.py:364
  96.5 1.4 %collective-permute-start.13 = (bf16[224,384]{1,0:T(8,128)(2,1)S(1)}, bf16[224,384]{1,0:T(8,128)(2,1)S(1)}, u32[]{:S(2)}, u32[]{:S(2)}) collective-permute-start(bf16[224,384]{1,0:T(8,128)(2,1)S(1)} %add_convert_fusion.3), channel_id=1, source_target_pairs={{0,48},{1,9},{2,50},{3,11},{4,52},{5,13},{6,54},{7,15},{8,56},{9,1... | collective-permute-start | bytes 516104 | tf_op jit(solution)/shard_map/ppermute | solution.py:364
  97.9 3.8 %collective-permute-done.13 = bf16[224,384]{1,0:T(8,128)(2,1)S(1)} collective-permute-done((bf16[224,384]{1,0:T(8,128)(2,1)S(1)}, bf16[224,384]{1,0:T(8,128)(2,1)S(1)}, u32[]{:S(2)}, u32[]{:S(2)}) %collective-permute-start.13) | collective-permute-done | bytes 172064 | tf_op jit(solution)/shard_map/ppermute | solution.py:364
  101.7 1.9 %collective-permute-start.14 = (bf16[224,384]{1,0:T(8,128)(2,1)S(1)}, bf16[224,384]{1,0:T(8,128)(2,1)S(1)}, u32[]{:S(2)}, u32[]{:S(2)}) collective-permute-start(bf16[224,384]{1,0:T(8,128)(2,1)S(1)} %add_convert_fusion.2), channel_id=1, source_target_pairs={{0,64},{1,17},{2,66},{3,19},{4,68},{5,21},{6,70},{7,23},{8,72},{9,... | collective-permute-start | bytes 516104 | tf_op jit(solution)/shard_map/ppermute | solution.py:364
  103.6 5.5 %collective-permute-done.14 = bf16[224,384]{1,0:T(8,128)(2,1)S(1)} collective-permute-done((bf16[224,384]{1,0:T(8,128)(2,1)S(1)}, bf16[224,384]{1,0:T(8,128)(2,1)S(1)}, u32[]{:S(2)}, u32[]{:S(2)}) %collective-permute-start.14) | collective-permute-done | bytes 172064 | tf_op jit(solution)/shard_map/ppermute | solution.py:364
  109.2 4.0 %collective-permute-start.15 = (bf16[224,384]{1,0:T(8,128)(2,1)S(1)}, bf16[224,384]{1,0:T(8,128)(2,1)S(1)}, u32[]{:S(2)}, u32[]{:S(2)}) collective-permute-start(bf16[224,384]{1,0:T(8,128)(2,1)S(1)} %add_convert_fusion.1), channel_id=1, source_target_pairs={{0,192},{1,49},{2,194},{3,51},{4,196},{5,53},{6,198},{7,55},{8,200... | collective-permute-start | bytes 516104 | tf_op jit(solution)/shard_map/ppermute | solution.py:364
  113.1 4.2 %collective-permute-done.15 = bf16[224,384]{1,0:T(8,128)(2,1)S(1)} collective-permute-done((bf16[224,384]{1,0:T(8,128)(2,1)S(1)}, bf16[224,384]{1,0:T(8,128)(2,1)S(1)}, u32[]{:S(2)}, u32[]{:S(2)}) %collective-permute-start.15) | collective-permute-done | bytes 172064 | tf_op jit(solution)/shard_map/ppermute | solution.py:364
  117.4 6.2 %collective-permute-start.16 = (bf16[224,384]{1,0:T(8,128)(2,1)S(1)}, bf16[224,384]{1,0:T(8,128)(2,1)S(1)}, u32[]{:S(2)}, u32[]{:S(2)}) collective-permute-start(bf16[224,384]{1,0:T(8,128)(2,1)S(1)} %add_convert_fusion.mine_ref), channel_id=1, source_target_pairs={{0,1},{1,0},{2,3},{3,2},{4,5},{5,4},{6,7},{7,6},{8,9},{9,8},{10,11... | collective-permute-start | bytes 516104 | tf_op jit(solution)/shard_map/ppermute | solution.py:364
  123.6 0.0 copy-done.1
  123.6 0.0 copy-done.2
  123.6 2.6 %output.1 = bf16[192,8,256]{2,1,0:T(8,128)(2,1)} custom-call(bf16[576,2048]{1,0:T(8,128)(2,1)S(1)} %get-tuple-element.37.gp_ref, bf16[192,576]{1,0:T(8,128)(2,1)S(1)} %bitcast.20, bf16[192,2048]{1,0:T(8,128)(2,1)S(1)} %get-tuple-element.35.std_ref, f32[8,2048]{1,0:T(8,128)S(1)} %get-tuple-element.38.inv_ref, bf16[192,8,256]{2,1,0:T(8,128)(2,1)S(1)} %bitcast.19, ...), custom_call_target="tpu_custom_call" | custom-call | flops 452984832 | bytes 6291456 | tf_op jit(solution)/shard_map/output/pallas_call | solution.py:473
  126.1 0.0 collective-permute-done.16.other_ref
  126.2 1.6 %finish.1 = (f32[192,576]{1,0:T(8,128)}, f32[3,3,576]{2,1,0:T(4,128)}, f32[192,192]{1,0:T(8,128)}, f32[1,128]{1,0:T(1,128)S(1)}, f32[1,192]{1,0:T(1,128)}, /*index=5*/f32[1,192]{1,0:T(1,128)}) custom-call(s32[4]{0:T(128)S(1)} %pad_add_fusion.flags, bf16[224,384]{1,0:T(8,128)(2,1)S(1)} %add_convert_fusion.mine_ref, ...), custom_call_target="tpu_custom_call" | custom-call | bytes 2097152 | tf_op jit(solution)/shard_map/finish/pallas_call | solution.py:483
  127.8 0.5 slice_bitcast_fusion
  (14 shorter events, 0.4 us)
Async XLA Ops:
  0.6 11.8 %copy-start.6 = (f32[192]{0:T(256)S(1)}, f32[192]{0:T(256)}, u32[]{:S(2)}) copy-start(f32[192]{0:T(256)} %param.15) | copy-start | bytes 2308
  0.6 11.8 %copy-start.5 = (f32[192]{0:T(256)S(1)}, f32[192]{0:T(256)}, u32[]{:S(2)}) copy-start(f32[192]{0:T(256)} %param.14) | copy-start | bytes 2308
  0.7 1.1 copy-start
  1.8 1.1 copy-start.3
  2.9 13.5 %copy-start.4 = (f32[576,3,3]{0,2,1:T(4,128)S(1)}, f32[576,3,3]{0,2,1:T(4,128)}, u32[]{:S(2)}) copy-start(f32[576,3,3]{0,2,1:T(4,128)} %param.11) | copy-start | bytes 62212
  3.8 10.0 %collective-permute-start = (bf16[192,768]{1,0:T(8,128)(2,1)S(1)}, bf16[192,768]{1,0:T(8,128)(2,1)S(1)}, u32[]{:S(2)}, u32[]{:S(2)}) collective-permute-start(bf16[192,768]{1,0:T(8,128)(2,1)S(1)} %get-tuple-element.29), channel_id=1, source_target_pairs={{0,1},{1,2},{2,3},{3,4},{4,5},{5,6},{6,7},{7,8},{8,9},{9,10},{10,1... | collective-permute-start | bytes 884744 | tf_op jit(solution)/shard_map/ppermute | solution.py:407
  8.4 8.0 %collective-permute-start.1 = (bf16[192,768]{1,0:T(8,128)(2,1)S(1)}, bf16[192,768]{1,0:T(8,128)(2,1)S(1)}, u32[]{:S(2)}, u32[]{:S(2)}) collective-permute-start(bf16[192,768]{1,0:T(8,128)(2,1)S(1)} %get-tuple-element.30), channel_id=1, source_target_pairs={{1,0},{2,1},{3,2},{4,3},{5,4},{6,5},{7,6},{8,7},{9,8},{10,9},{11,1... | collective-permute-start | bytes 884744 | tf_op jit(solution)/shard_map/ppermute | solution.py:408
  16.4 37.5 %copy-start.7 = (f32[4]{0:T(128)S(1)}, f32[4]{0:T(128)}, u32[]{:S(2)}) copy-start(f32[4]{0:T(128)} %sharp.1) | copy-start | bytes 52
  30.4 1.3 %collective-permute-start.2 = (f32[96,128]{1,0:T(8,128)S(1)}, f32[96,128]{1,0:T(8,128)S(1)}, u32[]{:S(2)}, u32[]{:S(2)}) collective-permute-start(f32[96,128]{1,0:T(8,128)S(1)} %slice_select_fusion), channel_id=1, source_target_pairs={{0,1},{1,0},{2,3},{3,2},{4,5},{5,4},{6,7},{7,6},{8,9},{9,8},{10,11... | collective-permute-start | bytes 147464 | tf_op jit(solution)/shard_map/ppermute | solution.py:364
  31.7 3.9 %collective-permute-start.3 = (f32[96,128]{1,0:T(8,128)S(1)}, f32[96,128]{1,0:T(8,128)S(1)}, u32[]{:S(2)}, u32[]{:S(2)}) collective-permute-start(f32[96,128]{1,0:T(8,128)S(1)} %select_add_fusion), channel_id=1, source_target_pairs={{0,2},{1,9},{2,0},{3,11},{4,6},{5,13},{6,4},{7,15},{8,10},{9,1},{1... | collective-permute-start | bytes 147464 | tf_op jit(solution)/shard_map/ppermute | solution.py:364
  35.6 4.3 %collective-permute-start.4 = (f32[96,128]{1,0:T(8,128)S(1)}, f32[96,128]{1,0:T(8,128)S(1)}, u32[]{:S(2)}, u32[]{:S(2)}) collective-permute-start(f32[96,128]{1,0:T(8,128)S(1)} %add.45), channel_id=1, source_target_pairs={{0,6},{1,17},{2,4},{3,19},{4,2},{5,21},{6,0},{7,23},{8,14},{9,25},... | collective-permute-start | bytes 147464 | tf_op jit(solution)/shard_map/ppermute | solution.py:364
  39.9 3.0 %collective-permute-start.5 = (f32[96,128]{1,0:T(8,128)S(1)}, f32[96,128]{1,0:T(8,128)S(1)}, u32[]{:S(2)}, u32[]{:S(2)}) collective-permute-start(f32[96,128]{1,0:T(8,128)S(1)} %add.46), channel_id=1, source_target_pairs={{0,8},{1,3},{2,10},{3,1},{4,12},{5,7},{6,14},{7,5},{8,0},{9,11},{1... | collective-permute-start | bytes 147464 | tf_op jit(solution)/shard_map/ppermute | solution.py:364
  42.9 5.8 %collective-permute-start.6 = (f32[96,128]{1,0:T(8,128)S(1)}, f32[96,128]{1,0:T(8,128)S(1)}, u32[]{:S(2)}, u32[]{:S(2)}) collective-permute-start(f32[96,128]{1,0:T(8,128)S(1)} %add.47), channel_id=1, source_target_pairs={{0,16},{1,7},{2,18},{3,5},{4,20},{5,3},{6,22},{7,1},{8,24},{9,15},... | collective-permute-start | bytes 147464 | tf_op jit(solution)/shard_map/ppermute | solution.py:364
  48.8 5.2 %collective-permute-start.7 = (f32[96,128]{1,0:T(8,128)S(1)}, f32[96,128]{1,0:T(8,128)S(1)}, u32[]{:S(2)}, u32[]{:S(2)}) collective-permute-start(f32[96,128]{1,0:T(8,128)S(1)} %add.48.mine_ref), channel_id=1, source_target_pairs={{0,1},{1,0},{2,3},{3,2},{4,5},{5,4},{6,7},{7,6},{8,9},{9,8},{10,11... | collective-permute-start | bytes 147464 | tf_op jit(solution)/shard_map/ppermute | solution.py:364
  73.8 49.7 %copy-start.1 = (bf16[1,192,8,256]{3,2,1,0:T(8,128)(2,1)S(1)}, bf16[1,192,8,256]{3,2,1,0:T(8,128)(2,1)}, u32[]{:S(2)}) copy-start(bf16[1,192,8,256]{3,2,1,0:T(8,128)(2,1)} %param.9) | copy-start | bytes 2359300
  73.9 49.7 %copy-start.2 = (bf16[576,192]{0,1:T(8,128)(2,1)S(1)}, bf16[576,192]{0,1:T(8,128)(2,1)}, u32[]{:S(2)}) copy-start(bf16[576,192]{0,1:T(8,128)(2,1)} %param.10) | copy-start | bytes 663556
  73.9 1.5 %collective-permute-start.8 = (bf16[224,384]{1,0:T(8,128)(2,1)S(1)}, bf16[224,384]{1,0:T(8,128)(2,1)S(1)}, u32[]{:S(2)}, u32[]{:S(2)}) collective-permute-start(bf16[224,384]{1,0:T(8,128)(2,1)S(1)} %broadcast_select_fusion), channel_id=1, source_target_pairs={{0,1},{1,0},{2,3},{3,2},{4,5},{5,4},{6,7},{7,6},{8,9},{9,8},{10,11... | collective-permute-start | bytes 516104 | tf_op jit(solution)/shard_map/ppermute | solution.py:364
  75.5 4.6 %collective-permute-start.9 = (bf16[224,384]{1,0:T(8,128)(2,1)S(1)}, bf16[224,384]{1,0:T(8,128)(2,1)S(1)}, u32[]{:S(2)}, u32[]{:S(2)}) collective-permute-start(bf16[224,384]{1,0:T(8,128)(2,1)S(1)} %add_convert_fusion.7), channel_id=1, source_target_pairs={{0,2},{1,65},{2,0},{3,67},{4,6},{5,69},{6,4},{7,71},{8,10},{9,73},... | collective-permute-start | bytes 516104 | tf_op jit(solution)/shard_map/ppermute | solution.py:364
  80.2 6.0 %collective-permute-start.10 = (bf16[224,384]{1,0:T(8,128)(2,1)S(1)}, bf16[224,384]{1,0:T(8,128)(2,1)S(1)}, u32[]{:S(2)}, u32[]{:S(2)}) collective-permute-start(bf16[224,384]{1,0:T(8,128)(2,1)S(1)} %add_convert_fusion.6), channel_id=1, source_target_pairs={{0,6},{1,193},{2,4},{3,195},{4,2},{5,197},{6,0},{7,199},{8,14},{9,... | collective-permute-start | bytes 516104 | tf_op jit(solution)/shard_map/ppermute | solution.py:364
  86.2 4.3 %collective-permute-start.11 = (bf16[224,384]{1,0:T(8,128)(2,1)S(1)}, bf16[224,384]{1,0:T(8,128)(2,1)S(1)}, u32[]{:S(2)}, u32[]{:S(2)}) collective-permute-start(bf16[224,384]{1,0:T(8,128)(2,1)S(1)} %add_convert_fusion.5), channel_id=1, source_target_pairs={{0,8},{1,3},{2,10},{3,1},{4,12},{5,7},{6,14},{7,5},{8,0},{9,11},{1... | collective-permute-start | bytes 516104 | tf_op jit(solution)/shard_map/ppermute | solution.py:364
  90.6 5.8 %collective-permute-start.12 = (bf16[224,384]{1,0:T(8,128)(2,1)S(1)}, bf16[224,384]{1,0:T(8,128)(2,1)S(1)}, u32[]{:S(2)}, u32[]{:S(2)}) collective-permute-start(bf16[224,384]{1,0:T(8,128)(2,1)S(1)} %add_convert_fusion.4), channel_id=1, source_target_pairs={{0,16},{1,7},{2,18},{3,5},{4,20},{5,3},{6,22},{7,1},{8,24},{9,15},... | collective-permute-start | bytes 516104 | tf_op jit(solution)/shard_map/ppermute | solution.py:364
  96.5 5.2 %collective-permute-start.13 = (bf16[224,384]{1,0:T(8,128)(2,1)S(1)}, bf16[224,384]{1,0:T(8,128)(2,1)S(1)}, u32[]{:S(2)}, u32[]{:S(2)}) collective-permute-start(bf16[224,384]{1,0:T(8,128)(2,1)S(1)} %add_convert_fusion.3), channel_id=1, source_target_pairs={{0,48},{1,9},{2,50},{3,11},{4,52},{5,13},{6,54},{7,15},{8,56},{9,1... | collective-permute-start | bytes 516104 | tf_op jit(solution)/shard_map/ppermute | solution.py:364
  101.7 7.4 %collective-permute-start.14 = (bf16[224,384]{1,0:T(8,128)(2,1)S(1)}, bf16[224,384]{1,0:T(8,128)(2,1)S(1)}, u32[]{:S(2)}, u32[]{:S(2)}) collective-permute-start(bf16[224,384]{1,0:T(8,128)(2,1)S(1)} %add_convert_fusion.2), channel_id=1, source_target_pairs={{0,64},{1,17},{2,66},{3,19},{4,68},{5,21},{6,70},{7,23},{8,72},{9,... | collective-permute-start | bytes 516104 | tf_op jit(solution)/shard_map/ppermute | solution.py:364
  109.2 8.2 %collective-permute-start.15 = (bf16[224,384]{1,0:T(8,128)(2,1)S(1)}, bf16[224,384]{1,0:T(8,128)(2,1)S(1)}, u32[]{:S(2)}, u32[]{:S(2)}) collective-permute-start(bf16[224,384]{1,0:T(8,128)(2,1)S(1)} %add_convert_fusion.1), channel_id=1, source_target_pairs={{0,192},{1,49},{2,194},{3,51},{4,196},{5,53},{6,198},{7,55},{8,200... | collective-permute-start | bytes 516104 | tf_op jit(solution)/shard_map/ppermute | solution.py:364
  117.4 8.8 %collective-permute-start.16 = (bf16[224,384]{1,0:T(8,128)(2,1)S(1)}, bf16[224,384]{1,0:T(8,128)(2,1)S(1)}, u32[]{:S(2)}, u32[]{:S(2)}) collective-permute-start(bf16[224,384]{1,0:T(8,128)(2,1)S(1)} %add_convert_fusion.mine_ref), channel_id=1, source_target_pairs={{0,1},{1,0},{2,3},{3,2},{4,5},{5,4},{6,7},{7,6},{8,9},{9,8},{10,11... | collective-permute-start | bytes 516104 | tf_op jit(solution)/shard_map/ppermute | solution.py:364

commit v2 on v1

v2 whole, which is shorter than its diff:
```python
import functools

import jax
import jax.numpy as jnp
from jax import lax
from jax.experimental import pallas as pl
from jax.experimental.pallas import tpu as pltpu
from jax.sharding import Mesh
from jax.sharding import PartitionSpec as P

F32 = jnp.float32
BF16 = jnp.bfloat16
NT = (((1,), (1,)), ((), ()))
TN = (((0,), (0,)), ((), ()))
VMEM = pl.BlockSpec(memory_space=pltpu.VMEM)
SMEM = pl.BlockSpec(memory_space=pltpu.SMEM)
HBM = pl.BlockSpec(memory_space=pltpu.HBM)
HI = lax.Precision.HIGHEST


def params(limit_mib):
    return pltpu.CompilerParams(vmem_limit_bytes=limit_mib << 20)


def call(body, outs, n_in, smem=(), hbm=(), scratch=(), limit=32, flops=0, name=None, moved=0):
    return pl.pallas_call(
        body,
        out_shape=tuple(jax.ShapeDtypeStruct(s, d) for s, d in outs),
        in_specs=[SMEM if i in smem else HBM if i in hbm else VMEM for i in range(n_in)],
        out_specs=tuple(VMEM for _ in outs),
        scratch_shapes=list(scratch),
        compiler_params=params(limit),
        cost_estimate=pl.CostEstimate(flops=flops, bytes_accessed=moved, transcendentals=0),
        name=name,
    )


def mm(a, b, dims=None, precision=None):
    dims = dims or (((1,), (0,)), ((), ()))
    return lax.dot_general(a, b, dims, preferred_element_type=F32, precision=precision)


def iota(shape, axis):
    return lax.broadcasted_iota(jnp.int32, shape, axis)


def to_column(row):
    n = row.shape[1]
    eye = iota((n, n), 0) == iota((n, n), 1)
    return jnp.sum(jnp.where(eye, row, 0.0), axis=1, keepdims=True)


def halves(v):
    return [v[:, i : i + 128] for i in range(0, v.shape[1], 128)]


def joined(parts):
    return jnp.concatenate(parts, axis=1)


def shifters(w):
    row, col = iota((w, w), 0), iota((w, w), 1)
    right = jnp.where(row + 1 == col, 1.0, 0.0)
    left = jnp.where(row == col + 1, 1.0, 0.0)
    return jnp.concatenate([right, left], axis=1).astype(BF16)


def moved_rows(blocks, shift):
    w = blocks[0].shape[1]
    n = blocks[0].shape[0]
    both = mm(jnp.concatenate(blocks, axis=0), shift)
    out = []
    for i, v in enumerate(blocks):
        at = slice(i * n, (i + 1) * n)
        out.append((halves(both[at, 0:w]), [x.astype(F32) for x in halves(v)], halves(both[at, w:])))
    return out


def taps_sum(k, rows, order, i):
    total = None
    for a in range(3):
        for b in range(3):
            term = k[3 * a + b] * rows[order[a]][order[b]][i]
            total = term if total is None else total + term
    return total


def spread_body(flags, x_ref, dy_ref, x2_ref, dy2_ref, up_ref, dn_ref, s):
    c, rows, w = x_ref.shape
    for j, (src, dst, k, off) in enumerate(((x_ref, x2_ref, 2, 0), (dy_ref, dy2_ref, 1, 2))):
        for q in range(w // 128):
            block = src[:, :, q * 128 : (q + 1) * 128]
            s[j, q] = block.astype(F32).reshape(c * rows, 128)
        for h in range(rows):
            v = [s[j, q, pl.ds(h, c, stride=rows), :] for q in range(w // 128)]
            v = jnp.concatenate(v, axis=1).astype(BF16)
            dst[:, h * w : (h + 1) * w] = v
            if h < k:
                dn_ref[:, (off + h) * w : (off + h + 1) * w] = v
            if h >= rows - k:
                u = off + h - rows + k
                up_ref[:, u * w : (u + 1) * w] = v


def columns_body(taps_ref, gain_ref, bias_ref, wt_ref, wo_ref, cols_ref, affine_ref, w_ref, wot_ref, wide):
    n = taps_ref.shape[2]
    c = gain_ref.shape[1]
    wide[...] = jnp.zeros_like(wide)
    for a in range(3):
        for b in range(3):
            wide[3 * a + b : 3 * a + b + 1, 0:n] = taps_ref[a, b : b + 1, :]
    w_ref[...] = wt_ref[...].astype(F32).T.astype(BF16)
    wot_ref[...] = wo_ref[...].astype(F32).T.astype(BF16)
    wide[9:10, 0:c] = gain_ref[...]
    wide[10:11, 0:c] = bias_ref[...]
    for g in range(0, 640, 128):
        flat = wide[:, g : g + 128].T
        m = min(128, n - g)
        for t in range(9):
            cols_ref[t, g : g + m, :] = jnp.broadcast_to(flat[0:m, t : t + 1], (m, 128))
        if g < c:
            m = min(128, c - g)
            for t in range(2):
                affine_ref[t, g : g + m, :] = jnp.broadcast_to(flat[0:m, 9 + t : 10 + t], (m, 128))


def affine(affine_ref, w):
    return [jnp.concatenate([affine_ref[i]] * (w // 128), axis=1) for i in range(2)]


def normalise(x, gain, bias):
    average = jnp.mean(x, axis=0, keepdims=True)
    centered = x - average
    inverse = lax.rsqrt(jnp.mean(centered * centered, axis=0, keepdims=True) + 1e-05)
    standard = centered * inverse
    return standard, inverse, (standard * gain + bias).astype(BF16)


def project_body(x2_ref, w_ref, affine_ref, p_ref, std_ref, inv_ref, *, w):
    gain, bias = affine(affine_ref, w)
    for h in range(x2_ref.shape[1] // w):
        at = slice(h * w, (h + 1) * w)
        standard, inverse, normed = normalise(x2_ref[:, at].astype(F32), gain, bias)
        std_ref[:, at] = standard.astype(BF16)
        inv_ref[:, at] = jnp.broadcast_to(inverse, (8, w))
        p_ref[:, at] = mm(w_ref[...], normed).astype(BF16)


def mix_rows(first, last, row, shift, cols_ref, ch, put):
    k = [cols_ref[t, ch, :] for t in range(9)]
    moved = moved_rows([row(r) for r in range(first - 1, last + 1)], shift)
    for r in range(first, last):
        at = r - first
        put(r, [taps_sum(k, moved[at : at + 3], (0, 1, 2), i) for i in range(len(moved[0][0]))])


def channels(g):
    return pl.ds(pl.multiple_of(g * 16, 16), 16)


def row_reader(p_ref, ph_ref, ch, w):
    rows = p_ref.shape[1] // w

    def row(r):
        if r < 0:
            return ph_ref[ch, (r + 2) * w : (r + 3) * w]
        if r >= rows:
            return ph_ref[ch, (r - rows + 2) * w : (r - rows + 3) * w]
        return p_ref[ch, r * w : (r + 1) * w]

    return row


def mix_body(
    flags, p_ref, up_ref, dn_ref, dy2_ref, w_ref, wot_ref, cols_ref, affine_ref,
    mixed_ref, ph_ref, pay_ref, t_ref, sq, gs, shift, *, w, heads,
):
    c3 = p_ref.shape[0]
    c = c3 // 3
    hs = c // heads
    rows = p_ref.shape[1] // w
    gain, bias = affine(affine_ref, w)
    keep_up = 1.0 - flags[0].astype(F32)
    keep_dn = 1.0 - flags[1].astype(F32)
    shift[...] = shifters(w)
    for src, keep, base in ((up_ref, keep_up, 0), (dn_ref, keep_dn, 2)):
        for h in range(2):
            normed = normalise(src[:, h * w : (h + 1) * w].astype(F32), gain, bias)[2]
            at = slice((base + h) * w, (base + h + 1) * w)
            ph_ref[:, at] = (mm(w_ref[...], normed) * keep).astype(BF16)

    def group(g, carry):
        ch = channels(g)
        total = []

        def put(r, out):
            out = joined(out).astype(BF16)
            mixed_ref[ch, r * w : (r + 1) * w] = out
            for v in halves(out):
                v = v.astype(F32)
                total.append(v * v)
                if len(total) > 1:
                    total[:] = [total[0] + total[1]]

        mix_rows(0, rows, row_reader(p_ref, ph_ref, ch, w), shift[...], cols_ref, ch, put)
        sq[ch, :] = jnp.broadcast_to(jnp.sum(total[0], axis=1, keepdims=True), (16, 128))
        return carry

    lax.fori_loop(0, c3 // 16, group, 0)

    query = mixed_ref[0:c, :]
    key = mixed_ref[c : 2 * c, :]
    value = mixed_ref[2 * c : 3 * c, :]
    gs[0, :, 0:c] = mm(query, key, NT)
    t = mm(dy2_ref[...], value, NT)
    t_ref[...] = t
    gs[1, :, 0:c] = mm(wot_ref[...].astype(F32), t, precision=HI)
    lane = iota((hs, 128), 1)
    for h in range(heads):
        at = slice(h * hs, (h + 1) * hs)
        gram = pltpu.roll(gs[0, at, :], (256 - hs * h) % 256, 1)[:, 0:128]
        grad = pltpu.roll(gs[1, at, :], (256 + hs - hs * h) % 256, 1)[:, 0:128]
        key_sq = sq[c + h * hs : c + (h + 1) * hs, :]
        rest = jnp.where(lane == 2 * hs, sq[at, :], key_sq)
        pay_ref[at, :] = jnp.where(lane < hs, gram, jnp.where(lane < 2 * hs, grad, rest))


def edge_body(p_ref, ph_ref, cols_ref, mh_ref, shift, *, w):
    rows = p_ref.shape[1] // w
    shift[...] = shifters(w)

    def group(g, carry):
        places = [channels(2 * g + part) for part in range(2)]
        edges = (-1, rows)
        blocks = []
        for ch in places:
            row = row_reader(p_ref, ph_ref, ch, w)
            blocks += [row(r + d) for r in edges for d in (-1, 0, 1)]
        moved = moved_rows(blocks, shift[...])
        for j, ch in enumerate(places):
            k = [cols_ref[t, ch, :] for t in range(9)]
            for i in range(2):
                near = moved[6 * j + 3 * i : 6 * j + 3 * i + 3]
                out = [taps_sum(k, near, (0, 1, 2), q) for q in range(w // 128)]
                mh_ref[ch, i * w : (i + 1) * w] = joined(out).astype(BF16)
        return carry

    lax.fori_loop(0, p_ref.shape[0] // 32, group, 0)


def back_body(
    flags, sharp, mine_ref, other_ref, mixed_ref, mh_ref, p_ref, ph_ref, dy2_ref, up_ref, dn_ref,
    std_ref, t_ref, wot_ref, cols_ref,
    gp_ref, left_ref, right_ref, pay, coef, mats, vecs, gm, aug, grads, shift, *, w, heads,
):
    c = mixed_ref.shape[0] // 3
    hs = c // heads
    rows = p_ref.shape[1] // w
    first_core = flags[3] == 0
    mine = mine_ref[...]
    other = other_ref[...]
    pay[0 : c // 2, :] = jnp.where(first_core, mine, other)
    pay[c // 2 : c, :] = jnp.where(first_core, other, mine)
    lane = iota((hs, 128), 1)
    valid = lane < hs
    eye = lane == iota((hs, 128), 0)
    pad = jnp.zeros((hs, 128), F32)
    sharp_row = jnp.zeros((1, 128), F32)
    for h in range(heads):
        at = slice(h * hs, (h + 1) * hs)
        block = pay[at, :]
        gram = jnp.where(valid, block, 0.0)
        grad = jnp.where(valid, pltpu.roll(block, 128 - hs, 1), 0.0)
        query_sq = block[:, 2 * hs : 2 * hs + 1] + 1e-06
        key_sq = (
            jnp.sum(jnp.where(eye, block[:, 2 * hs + 1 : 2 * hs + 2], 0.0), axis=0, keepdims=True)
            + 1e-06
        )
        length = jnp.sqrt(query_sq) * jnp.sqrt(key_sq)
        cosine = gram / length
        weights = jnp.where(valid, jnp.exp(cosine * sharp[h]), 0.0)
        attention = weights / jnp.sum(weights, axis=1, keepdims=True)
        scores = attention * (grad - jnp.sum(attention * grad, axis=1, keepdims=True))
        terms = scores * cosine
        sharp_h = jnp.sum(jnp.sum(terms, axis=1, keepdims=True), axis=0, keepdims=True)
        sharp_row = jnp.where(iota((1, 128), 1) == h, sharp_h, sharp_row)
        grad_cos = scores * sharp[h]
        terms = grad_cos * cosine
        alpha = jnp.sum(terms, axis=1, keepdims=True) / query_sq
        beta = jnp.sum(terms, axis=0, keepdims=True) / key_sq
        beta = jnp.sum(jnp.where(eye, beta, 0.0), axis=1, keepdims=True)
        vecs[at, 0:128] = jnp.broadcast_to(alpha, (hs, 128))
        vecs[at, 128:256] = jnp.broadcast_to(beta, (hs, 128))
        for i, m in enumerate((grad_cos / length, attention)):
            placed = pltpu.roll(jnp.concatenate([m, pad], axis=1), hs * h, 1)
            mats[i, at, :] = placed.astype(BF16)

    grad_gram = mats[0, :, 0:c]
    grad_gram_t = grad_gram.astype(F32).T.astype(BF16)
    attention_b = mats[1, :, 0:c]
    attention_t = attention_b.astype(F32).T.astype(BF16)
    outgoing = mm(t_ref[...], attention_b.astype(F32), NT, precision=HI)
    alpha = jnp.concatenate([vecs[:, 0:128]] * (w // 128), axis=1)
    beta = jnp.concatenate([vecs[:, 128:256]] * (w // 128), axis=1)
    wot = wot_ref[...]
    for r in range(rows + 2):
        at = slice(r * w, (r + 1) * w)
        if r == 0:
            dy = up_ref[:, 2 * w : 3 * w]
            src, own = (mh_ref, slice(0, w))
        elif r == rows + 1:
            dy = dn_ref[:, 2 * w : 3 * w]
            src, own = (mh_ref, slice(w, 2 * w))
        else:
            own = slice((r - 1) * w, r * w)
            dy = dy2_ref[:, own]
            src = mixed_ref
        query = src[0:c, own]
        key = src[c : 2 * c, own]
        grad_attended = mm(wot, dy).astype(BF16)
        parts = (
            mm(grad_gram, key) - query.astype(F32) * alpha,
            mm(grad_gram_t, query) - key.astype(F32) * beta,
            mm(attention_t, grad_attended),
        )
        for i, part in enumerate(parts):
            if r == 0:
                part = part * (1.0 - flags[0].astype(F32))
            if r == rows + 1:
                part = part * (1.0 - flags[1].astype(F32))
            gm[i * c : (i + 1) * c, at] = part.astype(BF16)

    shift[...] = shifters(w)

    def group(g, carry):
        ch = channels(g)
        k = [cols_ref[t, ch, :] for t in range(9)]
        row = row_reader(p_ref, ph_ref, ch, w)
        moved = moved_rows([gm[ch, r * w : (r + 1) * w] for r in range(rows + 2)], shift[...])
        acc = [None] * 9
        window = [None] + [[v.astype(F32) for v in halves(row(r))] for r in (-1, 0)]
        for r in range(rows):
            window = [window[1], window[2], [v.astype(F32) for v in halves(row(r + 1))]]
            parts = range(w // 128)
            out = [taps_sum(k, moved[r : r + 3], (2, 1, 0), i) for i in parts]
            gp_ref[ch, r * w : (r + 1) * w] = joined(out).astype(BF16)
            for a in range(3):
                for b in range(3):
                    t = 3 * a + b
                    for i in parts:
                        term = moved[r + 1][2 - b][i] * window[a][i]
                        acc[t] = term if acc[t] is None else acc[t] + term
        lanes = iota((16, 128), 1)
        out = jnp.zeros((16, 128), F32)
        for t in range(9):
            out = jnp.where(lanes == t, jnp.sum(acc[t], axis=1, keepdims=True), out)
        coef[ch, :] = out
        return carry

    lax.fori_loop(0, gm.shape[0] // 16, group, 0)

    aug[0:c, :] = std_ref[...]
    aug[c : c + 16, :] = jnp.where(iota((16, rows * w), 0) == 0, 1.0, 0.0).astype(BF16)
    c3 = 3 * c
    grads[...] = jnp.zeros_like(grads)
    grads[0 : c + 16, 0:c3] = mm(aug[...], gp_ref[...], NT)
    grads[c + 16 : c + 32, :] = coef[...].T[0:16, :]
    lead = 1.0 - jnp.minimum(flags[2], 1).astype(F32)
    grads[c + 1 : c + 2, 0:128] = sharp_row * lead
    out_pad = jnp.concatenate([outgoing, jnp.zeros((c, 256 - c), F32)], axis=1)
    half = c3 % 128
    tail = grads[0:c, c3 - half : c3 - half + 128]
    moved = pltpu.roll(out_pad[:, 128:256], half, 1)
    grads[0:c, c3 - half : c3 - half + 128] = jnp.where(iota((c, 128), 1) < half, tail, moved)
    left_ref[...] = grads[:, 0:384].astype(BF16)
    right_ref[:, 0:256] = grads[:, 384:640].astype(BF16)
    right_ref[0:c, 256:384] = out_pad[:, 0:128].astype(BF16)
    right_ref[c:, 256:384] = jnp.zeros((grads.shape[0] - c, 128), BF16)


def output_body(gp_ref, wt_ref, std_ref, inv_ref, dy_ref, affine_ref, out_ref, s, *, w):
    c, rows, _ = out_ref.shape
    gain = affine(affine_ref, w)[0]
    for h in range(rows):
        at = slice(h * w, (h + 1) * w)
        scaled = mm(wt_ref[...], gp_ref[:, at]) * gain
        standard = std_ref[:, at].astype(F32)
        first = jnp.mean(scaled, axis=0, keepdims=True)
        second = jnp.mean(scaled * standard, axis=0, keepdims=True)
        v = (scaled - first - standard * second) * inv_ref[0:1, at]
        for i in range(w // 128):
            s[i, pl.ds(h, c, stride=rows), :] = v[:, i * 128 : (i + 1) * 128]
    for i in range(w // 128):
        at = slice(i * 128, (i + 1) * 128)
        v = dy_ref[:, :, at].astype(F32) + s[i, :, :].reshape(c, rows, 128)
        out_ref[:, :, at] = v.astype(BF16)


def finish_body(
    flags, mine_ref, other_ref, wt_ref, gain_ref, bias_ref,
    triple_ref, taps_ref, outgoing_ref, sharp_ref, scaling_ref, offset_ref, full,
):
    c, c3 = wt_ref.shape
    first_core = flags[3] == 0
    mine = mine_ref[...].astype(F32)
    other = other_ref[...].astype(F32)
    full[:, 0:384] = jnp.where(first_core, mine, other)
    full[:, 384:768] = jnp.where(first_core, other, mine)
    m = full[0:c, 0:c3]
    s = full[c : c + 1, 0:c3]
    gain = to_column(gain_ref[...])
    bias = to_column(bias_ref[...])
    wt = wt_ref[...].astype(F32)
    triple_ref[...] = m * gain + bias * s
    eye = iota((c, c), 0) == iota((c, c), 1)
    scaling = jnp.sum(wt * m, axis=1, keepdims=True)
    offset = jnp.sum(wt * s, axis=1, keepdims=True)
    scaling_ref[...] = jnp.sum(jnp.where(eye, scaling, 0.0), axis=0, keepdims=True)
    offset_ref[...] = jnp.sum(jnp.where(eye, offset, 0.0), axis=0, keepdims=True)
    for a in range(3):
        taps_ref[a, :, :] = full[c + 16 + 3 * a : c + 19 + 3 * a, 0:c3]
    half = c3 % 128
    outgoing_ref[:, 0:128] = full[0:c, 640:768]
    tail = pltpu.roll(full[0:c, 512:640], 128 - half, 1)
    outgoing_ref[:, 128:c] = tail[:, 0 : c - 128]
    sharp_ref[...] = full[c + 1 : c + 2, 0 : sharp_ref.shape[1]]


GROUP = ("img", "chip")
ALL = ("img", "chip", "core")


def swap(v, mask, count):
    return lax.ppermute(v, ALL, [(i, i ^ mask) for i in range(count)])


def bits(total, tile):
    if total == 256 and tile == 32:
        return (2, 6, 8, 16)
    return tuple(1 << i for i in range(1, 20) if 1 << i < tile)


def solution(mesh):
    img, tile = (mesh.shape["img"], mesh.shape["tile"])
    total = img * tile
    chips = total // 2
    mesh = Mesh(mesh.devices.reshape(img, tile // 2, 2), ALL)
    strip = ("chip", "core")

    def local(x, dy, triple, stencil, out_mixer, sharpness, gain, bias):
        _, c, rows, w = x.shape
        heads = sharpness.shape[0]
        c3 = 3 * c
        n = rows * w
        core = lax.axis_index("core")
        place = lax.axis_index("chip") * 2 + core
        flags = jnp.stack([place == 0, place == tile - 1, place, core]).astype(jnp.int32)
        x3 = x.reshape(c, rows, w)
        dy3 = dy.reshape(c, rows, w)
        taps = jnp.transpose(stencil, (1, 2, 0))
        wt = triple.T
        gain_row = gain.reshape(1, c)
        bias_row = bias.reshape(1, c)

        x2, dy2, up, dn = call(
            spread_body,
            [((c, n), BF16), ((c, n), BF16), ((c, 3 * w), BF16), ((c, 3 * w), BF16)],
            3,
            smem=(0,),
            scratch=[pltpu.VMEM((2, w // 128, c * rows, 128), F32)],
            limit=8,
            name="spread",
            moved=4 << 20,
        )(flags, x3, dy3)
        even = core == 0
        inside = lax.ppermute(jnp.where(even, up, dn), strip, [(i, i ^ 1) for i in range(tile)])
        pairs = [(i, i + 1) for i in range(1, tile - 1, 2)]
        across = jnp.where(even, dn, up)
        across = lax.ppermute(across, strip, pairs + [(j, i) for i, j in pairs])
        cols, aff, w_row, wot = call(
            columns_body,
            [((9, c3, 128), F32), ((2, c, 128), F32), ((c3, c), BF16), ((c, c), BF16)],
            5,
            scratch=[pltpu.VMEM((128, 640), F32)],
            limit=16,
            moved=4 << 20,
            name="columns",
        )(taps, gain_row, bias_row, wt, out_mixer)
        p, std, inv = call(
            functools.partial(project_body, w=w),
            [((c3, n), BF16), ((c, n), BF16), ((8, n), F32)],
            3,
            limit=16,
            flops=2 * c3 * c * n,
            moved=8 << 20,
            name="project",
        )(x2, w_row, aff)
        up_in = jnp.where(even, across, inside)
        dn_in = jnp.where(even, inside, across)
        mixed, ph, pay, t = call(
            functools.partial(mix_body, w=w, heads=heads),
            [((c3, n), BF16), ((c3, 4 * w), BF16), ((c, 128), F32), ((c, c), F32)],
            9,
            smem=(0,),
            scratch=[
                pltpu.VMEM((c3, 128), F32),
                pltpu.VMEM((2, c, 256), F32),
                pltpu.VMEM((w, 2 * w), BF16),
            ],
            limit=12,
            flops=8 * c * c * n,
            moved=8 << 20,
            name="mix",
        )(flags, p, up_in, dn_in, dy2, w_row, wot, cols, aff)

        half = c // 2
        mine = jnp.where(core == 0, pay[:half], pay[half:])
        theirs = jnp.where(core == 0, pay[half:], pay[:half])
        mine = mine + swap(theirs, 1, total)
        (mh,) = call(
            functools.partial(edge_body, w=w),
            [((c3, 2 * w), BF16)],
            3,
            scratch=[pltpu.VMEM((w, 2 * w), BF16)],
            limit=8,
            moved=6 << 20,
            name="edge",
        )(p, ph, cols)
        for i, mask in enumerate(bits(total, tile)):
            mine = mine + swap(mine, mask, total)
            if i == 0:
                mine, mh = lax.optimization_barrier((mine, mh))
        other = swap(mine, 1, total)

        each = pl.cdiv(c + 32, 2 * chips) * 2
        size = each * chips
        gp, left, right = call(
            functools.partial(back_body, w=w, heads=heads),
            [((c3, n), BF16), ((size, 384), BF16), ((size, 384), BF16)],
            15,
            smem=(0, 1),
            scratch=[
                pltpu.VMEM((c, 128), F32),
                pltpu.VMEM((640, 128), F32),
                pltpu.VMEM((2, c, 256), BF16),
                pltpu.VMEM((c, 256), F32),
                pltpu.VMEM((c3, (rows + 2) * w), BF16),
                pltpu.VMEM((c + 16, n), BF16),
                pltpu.VMEM((size, 640), F32),
                pltpu.VMEM((w, 2 * w), BF16),
            ],
            limit=20,
            flops=20 * c * c * n,
            moved=8 << 20,
            name="back",
        )(flags, sharpness, mine, other, mixed, mh, p, ph, dy2, up_in, dn_in, std, t, wot, cols)

        (fm,) = call(
            functools.partial(output_body, w=w),
            [((c, rows, w), BF16)],
            6,
            scratch=[pltpu.VMEM((w // 128, c * rows, 128), F32)],
            limit=10,
            flops=2 * c3 * c * n,
            moved=6 << 20,
            name="output",
        )(gp, wt, std, inv, dy3, aff)
        part = jnp.where(core == 0, left, right)
        away = jnp.where(core == 0, right, left)
        part = (part.astype(F32) + swap(away, 1, total).astype(F32)).astype(BF16)
        got = lax.all_to_all(part.reshape(chips, each, 384), GROUP, 0, 0)
        piece = jnp.sum(got.astype(F32), axis=0, keepdims=True).astype(BF16)
        piece, fm = lax.optimization_barrier((piece, fm))
        part = lax.all_to_all(jnp.broadcast_to(piece, got.shape), GROUP, 0, 0)
        part = part.reshape(size, 384)
        rest = swap(part, 1, total)

        outs = call(
            finish_body,
            [((c, c3), F32), ((3, 3, c3), F32), ((c, c), F32), ((1, heads), F32), ((1, c), F32), ((1, c), F32)],
            6,
            smem=(0,),
            scratch=[pltpu.VMEM((size, 768), F32)],
            limit=16,
            name="finish",
            moved=2 << 20,
        )(flags, part, rest, wt, gain_row, bias_row)
        triple_t, taps_t, outgoing, sharp_row, scaling, offset = outs
        return (
            fm.reshape(x.shape),
            triple_t.T,
            jnp.transpose(taps_t, (2, 0, 1)),
            outgoing,
            sharp_row.reshape(heads),
            scaling.reshape(c),
            offset.reshape(c),
        )

    return jax.shard_map(
        local,
        mesh=mesh,
        in_specs=(P("img", None, strip, None), P("img", None, strip, None)) + (P(),) * 6,
        out_specs=(P("img", None, strip, None),) + (P(),) * 6,
        check_vma=False,
    )
```

time: 129 us -> 125 us (0.969)
  waiting for transfers between devices: 39.5 us -> 20.9 us
  blocking collectives: 0 us -> 17.8 us
  starting transfers between devices: 42.4 us -> 35 us
  Pallas kernels: 40.1 us -> 43.5 us
  local copies, waits for them, and re-layouts: 4.9 us -> 6.32 us
    ppermute x17 -> x10, waiting for transfers between devices: 39.5 us -> 13.1 us  [the longest x8 9.24 us: swap(): return lax.ppermute(v, ALL, [(i, i ^ mask) for i in range(count)])]
    ppermute x17 -> x10, starting transfers between devices: 42.4 us -> 19.8 us  [the longest x8 14.6 us: swap(): return lax.ppermute(v, ALL, [(i, i ^ mask) for i in range(count)])]
    all_to_all x0 -> x1, blocking collectives: none -> 17.8 us  [local(): part = lax.all_to_all(jnp.broadcast_to(piece, got.shape), GROUP, 0, 0)]
    all_to_all x0 -> x1, starting transfers between devices: none -> 15.2 us  [local(): got = lax.all_to_all(part.reshape(chips, each, 384), GROUP, 0, 0)]
    all_to_all x0 -> x1, waiting for transfers between devices: none -> 7.8 us  [local(): got = lax.all_to_all(part.reshape(chips, each, 384), GROUP, 0, 0)]
    pallas_call x1 -> x3, Pallas kernels: 13.9 us -> 19 us  [the longest x1 13.9 us: local(): call(functools.partial(mix_body, w=w, heads=heads), [((c3, n), BF16), ((c...]
    pallas_call x1, Pallas kernels: 19.9 us -> 17.9 us  [local(): call(functools.partial(back_body, w=w, heads=heads), [((c3, n), BF16), ((...]
    unnamed x18 -> x22, local copies, waits for them, and re-layouts: 4.39 us -> 5.38 us
  transfers between devices with their start and end apart: 17 -> 11, of which waited for: 15 -> 9; matrix products, arithmetic and copies ran while one was open for 2% -> 0% of each run, Pallas kernels for 3% -> 7%
where the time goes in v2:
time: 125 us
  Pallas kernels  43.5 us (35%)
  starting transfers between devices  35 us (28%)
  waiting for transfers between devices  20.9 us (17%)
  blocking collectives  17.8 us (14%)
  local copies, waits for them, and re-layouts  6.32 us (5%)
    pallas_call x1, Pallas kernels, local(): call(functools.partial(back_body, w=w, heads=heads), [((c3, n), BF16), ((...  17.9 us
    all_to_all x1, blocking collectives, local(): part = lax.all_to_all(jnp.broadcast_to(piece, got.shape), GROUP, 0, 0)  17.8 us
    all_to_all x1, starting transfers between devices, local(): got = lax.all_to_all(part.reshape(chips, each, 384), GROUP, 0, 0)  15.2 us
    ppermute x8, starting transfers between devices, swap(): return lax.ppermute(v, ALL, [(i, i ^ mask) for i in range(count)])  14.6 us
    pallas_call x1, Pallas kernels, local(): call(functools.partial(mix_body, w=w, heads=heads), [((c3, n), BF16), ((c...  13.9 us
    ppermute x8, waiting for transfers between devices, swap(): return lax.ppermute(v, ALL, [(i, i ^ mask) for i in range(count)])  9.24 us
    all_to_all x1, waiting for transfers between devices, local(): got = lax.all_to_all(part.reshape(chips, each, 384), GROUP, 0, 0)  7.8 us
    unnamed x22, local copies, waits for them, and re-layouts  5.38 us
  transfers between devices with their start and end apart: 11, of which 9 were waited for; matrix products, arithmetic and copies ran while one was open for 0% of the time, Pallas kernels for 7%

profile of v2, /device:TPU:1, one launch (start us, length us, event | category | flops | bytes accessed | tf_op | source)
XLA Modules:
  0.0 125.0 jit_solution(12295563276434415600)
XLA Ops:
  0.6 0.0 copy-start.9
  0.6 0.0 copy-start.8
  0.7 0.0 copy-start.7
  0.7 0.1 pad_add_fusion.flags
  0.8 0.0 copy-start
  0.8 1.1 copy-done
  1.9 0.0 copy-start.5
  1.9 1.1 copy-done.5
  3.0 0.0 copy-start.4
  3.0 0.0 copy-start.6
  3.0 1.4 %spread.1 = (bf16[192,2048]{1,0:T(8,128)(2,1)S(1)}, bf16[192,2048]{1,0:T(8,128)(2,1)S(1)}, bf16[192,768]{1,0:T(8,128)(2,1)S(1)}, bf16[192,768]{1,0:T(8,128)(2,1)S(1)}) custom-call(s32[4]{0:T(128)S(1)} %pad_add_fusion.flags, bf16[192,8,256]{2,1,0:T(8,128)(2,1)S(1)} %bitcast.23, bf16[192,8,256]{2,1,0:T(8,128)(2,1)S(1)} %bitcast.18), custom_call_target="tpu_custom_call" | custom-call | bytes 4194304 | tf_op jit(solution)/shard_map/spread/pallas_call | solution.py:465
  4.5 3.3 %collective-permute-start.1 = (bf16[192,768]{1,0:T(8,128)(2,1)S(1)}, bf16[192,768]{1,0:T(8,128)(2,1)S(1)}, u32[]{:S(2)}, u32[]{:S(2)}) collective-permute-start(bf16[192,768]{1,0:T(8,128)(2,1)S(1)} %get-tuple-element.65), channel_id=1, source_target_pairs={{0,1},{1,0},{2,3},{3,2},{4,5},{5,4},{6,7},{7,6},{8,9},{9,8},{10,11... | collective-permute-start | bytes 884744 | tf_op jit(solution)/shard_map/ppermute | solution.py:476
  7.8 1.9 %collective-permute-start = (bf16[192,768]{1,0:T(8,128)(2,1)S(1)}, bf16[192,768]{1,0:T(8,128)(2,1)S(1)}, u32[]{:S(2)}, u32[]{:S(2)}) collective-permute-start(bf16[192,768]{1,0:T(8,128)(2,1)S(1)} %get-tuple-element.66), channel_id=1, source_target_pairs={{1,2},{3,4},{5,6},{7,8},{9,10},{11,12},{13,14},{15,16},{17,18},{19... | collective-permute-start | bytes 884744 | tf_op jit(solution)/shard_map/ppermute | solution.py:479
  9.7 0.0 copy-done.9
  9.7 0.0 copy-done.8
  9.7 0.0 copy-done.7
  9.7 0.0 copy-done.4
  9.7 0.0 copy-done.6
  9.7 1.1 columns.1
  10.8 1.1 project.1
  12.0 0.0 collective-permute-done.1
  12.0 3.8 %collective-permute-done = bf16[192,768]{1,0:T(8,128)(2,1)S(1)} collective-permute-done((bf16[192,768]{1,0:T(8,128)(2,1)S(1)}, bf16[192,768]{1,0:T(8,128)(2,1)S(1)}, u32[]{:S(2)}, u32[]{:S(2)}) %collective-permute-start) | collective-permute-done | bytes 294944 | tf_op jit(solution)/shard_map/ppermute | solution.py:479
  15.8 13.9 %mix.1 = (bf16[576,2048]{1,0:T(8,128)(2,1)S(1)}, bf16[576,1024]{1,0:T(8,128)(2,1)S(1)}, f32[192,128]{1,0:T(8,128)S(1)}, f32[192,192]{1,0:T(8,128)S(1)}) custom-call(s32[4]{0:T(128)S(1)} %pad_add_fusion.flags, bf16[576,2048]{1,0:T(8,128)(2,1)S(1)} %get-tuple-element.38.p_ref, bf16[192,768]{1,0:T(8,128)(2,1)S(1)} %get-tuple-element.64.up_ref, ...), custom_call_target="tpu_custom_call" | custom-call | flops 603979776 | bytes 8388608 | tf_op jit(solution)/shard_map/mix/pallas_call | solution.py:500
  29.8 0.1 collective-permute-start.2
  29.9 1.2 collective-permute-done.2
  31.1 0.1 collective-permute-start.3
  31.2 0.0 copy-start.10
  31.3 3.9 %edge.1.mh_ref = bf16[576,512]{1,0:T(8,128)(2,1)S(1)} custom-call(bf16[576,2048]{1,0:T(8,128)(2,1)S(1)} %get-tuple-element.38.p_ref, bf16[576,1024]{1,0:T(8,128)(2,1)S(1)} %get-tuple-element.45.ph_ref, f32[9,576,128]{2,1,0:T(8,128)S(1)} %get-tuple-element.43.cols_ref), custom_call_target="tpu_custom_call" | custom-call | bytes 6291456 | tf_op jit(solution)/shard_map/edge/pallas_call | solution.py:520
  35.2 0.0 collective-permute-done.3
  35.2 3.2 %collective-permute-start.4 = (f32[96,128]{1,0:T(8,128)S(1)}, f32[96,128]{1,0:T(8,128)S(1)}, u32[]{:S(2)}, u32[]{:S(2)}) collective-permute-start(f32[96,128]{1,0:T(8,128)S(1)} %add.23), channel_id=1, source_target_pairs={{0,6},{1,7},{2,4},{3,5},{4,2},{5,3},{6,0},{7,1},{8,14},{9,15},{10,... | collective-permute-start | bytes 147464 | tf_op jit(solution)/shard_map/ppermute | solution.py:434
  38.4 1.8 %collective-permute-done.4 = f32[96,128]{1,0:T(8,128)S(1)} collective-permute-done((f32[96,128]{1,0:T(8,128)S(1)}, f32[96,128]{1,0:T(8,128)S(1)}, u32[]{:S(2)}, u32[]{:S(2)}) %collective-permute-start.4) | collective-permute-done | bytes 49184 | tf_op jit(solution)/shard_map/ppermute | solution.py:434
  40.3 1.4 %collective-permute-start.5 = (f32[96,128]{1,0:T(8,128)S(1)}, f32[96,128]{1,0:T(8,128)S(1)}, u32[]{:S(2)}, u32[]{:S(2)}) collective-permute-start(f32[96,128]{1,0:T(8,128)S(1)} %add.24), channel_id=1, source_target_pairs={{0,8},{1,9},{2,10},{3,11},{4,12},{5,13},{6,14},{7,15},{8,0},{9,1},... | collective-permute-start | bytes 147464 | tf_op jit(solution)/shard_map/ppermute | solution.py:434
  41.6 1.7 %collective-permute-done.5 = f32[96,128]{1,0:T(8,128)S(1)} collective-permute-done((f32[96,128]{1,0:T(8,128)S(1)}, f32[96,128]{1,0:T(8,128)S(1)}, u32[]{:S(2)}, u32[]{:S(2)}) %collective-permute-start.5) | collective-permute-done | bytes 49184 | tf_op jit(solution)/shard_map/ppermute | solution.py:434
  43.3 2.7 %collective-permute-start.6 = (f32[96,128]{1,0:T(8,128)S(1)}, f32[96,128]{1,0:T(8,128)S(1)}, u32[]{:S(2)}, u32[]{:S(2)}) collective-permute-start(f32[96,128]{1,0:T(8,128)S(1)} %add.25), channel_id=1, source_target_pairs={{0,16},{1,17},{2,18},{3,19},{4,20},{5,21},{6,22},{7,23},{8,24},{9,... | collective-permute-start | bytes 147464 | tf_op jit(solution)/shard_map/ppermute | solution.py:434
  46.0 1.5 %collective-permute-done.6 = f32[96,128]{1,0:T(8,128)S(1)} collective-permute-done((f32[96,128]{1,0:T(8,128)S(1)}, f32[96,128]{1,0:T(8,128)S(1)}, u32[]{:S(2)}, u32[]{:S(2)}) %collective-permute-start.6) | collective-permute-done | bytes 49184 | tf_op jit(solution)/shard_map/ppermute | solution.py:434
  47.5 3.3 %collective-permute-start.7 = (f32[96,128]{1,0:T(8,128)S(1)}, f32[96,128]{1,0:T(8,128)S(1)}, u32[]{:S(2)}, u32[]{:S(2)}) collective-permute-start(f32[96,128]{1,0:T(8,128)S(1)} %add.26.mine_ref), channel_id=1, source_target_pairs={{0,1},{1,0},{2,3},{3,2},{4,5},{5,4},{6,7},{7,6},{8,9},{9,8},{10,11... | collective-permute-start | bytes 147464 | tf_op jit(solution)/shard_map/ppermute | solution.py:434
  50.8 0.9 collective-permute-done.7.other_ref
  51.7 0.0 copy-done.10
  51.7 17.9 %back.1 = (bf16[576,2048]{1,0:T(8,128)(2,1)S(1)}, bf16[256,384]{1,0:T(8,128)(2,1)S(1)}, bf16[256,384]{1,0:T(8,128)(2,1)S(1)}) custom-call(s32[4]{0:T(128)S(1)} %pad_add_fusion.flags, f32[4]{0:T(128)S(1)} %copy-done.10, f32[96,128]{1,0:T(8,128)S(1)} %add.26.mine_ref, f32[96,128]{1,0:T(8,128)S(1)} %collective-permute-done.7.other_ref, ...), custom_call_target="tpu_custom_call" | custom-call | flops 1509949440 | bytes 8388608 | tf_op jit(solution)/shard_map/back/pallas_call | solution.py:537
  69.6 0.0 copy-start.2
  69.6 1.4 %copy-done.2 = bf16[576,2048]{1,0:T(8,128)(2,1)} copy-done((bf16[576,2048]{1,0:T(8,128)(2,1)}, bf16[576,2048]{1,0:T(8,128)(2,1)S(1)}, u32[]{:S(2)}) %copy-start.2) | copy-done | bytes 2359320
  71.0 0.0 copy-start.1
  71.1 0.6 collective-permute-start.8
  71.7 1.1 collective-permute-done.8
  72.8 0.1 add_convert_fusion
  72.9 0.8 reshape.57
  73.6 15.2 %all-to-all-start = ((bf16[128,2,384]{2,1,0:T(2,128)(2,1)}), bf16[128,2,384]{2,1,0:T(2,128)(2,1)S(1)}, u32[]{:S(2)}, u32[]{:S(2)}) async-start(bf16[128,2,384]{2,1,0:T(2,128)(2,1)} %reshape.57), calls=%async_computation | async-start | bytes 393216 | tf_op jit(solution)/shard_map/all_to_all | solution.py:571
  88.9 0.0 copy-done.1
  88.9 0.0 copy-start.3
  88.9 1.7 %copy-done.3 = bf16[576,2048]{1,0:T(8,128)(2,1)S(1)} copy-done((bf16[576,2048]{1,0:T(8,128)(2,1)S(1)}, bf16[576,2048]{1,0:T(8,128)(2,1)}, u32[]{:S(2)}) %copy-start.3) | copy-done | bytes 2359320
  90.5 2.6 %output.1 = bf16[192,8,256]{2,1,0:T(8,128)(2,1)} custom-call(bf16[576,2048]{1,0:T(8,128)(2,1)S(1)} %copy-done.3, bf16[192,576]{1,0:T(8,128)(2,1)S(1)} %bitcast.21, bf16[192,2048]{1,0:T(8,128)(2,1)S(1)} %get-tuple-element.49.std_ref, f32[8,2048]{1,0:T(8,128)S(1)} %get-tuple-element.54.inv_ref, bf16[192,8,256]{2,1,0:T(8,128)(2,1)S(1)} %bitcast.19, ...), custom_call_target="tpu_custom_call" | custom-call | flops 452984832 | bytes 6291456 | tf_op jit(solution)/shard_map/output/pallas_call | solution.py:558
  93.1 7.8 %all-to-all-done = bf16[128,2,384]{2,1,0:T(2,128)(2,1)S(1)} async-done(((bf16[128,2,384]{2,1,0:T(2,128)(2,1)}), bf16[128,2,384]{2,1,0:T(2,128)(2,1)S(1)}, u32[]{:S(2)}, u32[]{:S(2)}) %all-to-all-start) | async-done | bytes 196640 | tf_op jit(solution)/shard_map/all_to_all | solution.py:571
  100.9 0.2 reduce_sum.12
  101.2 0.1 broadcast_in_dim.9
  101.3 17.8 %all_to_all.10 = bf16[128,2,384]{2,1,0:T(2,128)(2,1)S(1)} all-to-all(bf16[128,2,384]{2,1,0:T(2,128)(2,1)S(1)} %broadcast_in_dim.9), channel_id=1, replica_groups=mesh['img'=8,'chip'=16,'core'=2] {'img','chip'}, dimensions={0} | all-to-all | bytes 393216 | tf_op jit(solution)/shard_map/all_to_all | solution.py:574
  119.0 0.1 reshape.59.mine_ref
  119.1 3.2 %collective-permute-start.9 = (bf16[256,384]{1,0:T(8,128)(2,1)S(1)}, bf16[256,384]{1,0:T(8,128)(2,1)S(1)}, u32[]{:S(2)}, u32[]{:S(2)}) collective-permute-start(bf16[256,384]{1,0:T(8,128)(2,1)S(1)} %reshape.59.mine_ref), channel_id=1, source_target_pairs={{0,1},{1,0},{2,3},{3,2},{4,5},{5,4},{6,7},{7,6},{8,9},{9,8},{10,11... | collective-permute-start | bytes 589832 | tf_op jit(solution)/shard_map/ppermute | solution.py:434
  122.3 1.1 collective-permute-done.9.other_ref
  123.4 1.6 %finish.1 = (f32[192,576]{1,0:T(8,128)}, f32[3,3,576]{2,1,0:T(4,128)}, f32[192,192]{1,0:T(8,128)}, f32[1,4]{1,0:T(1,128)}, f32[1,192]{1,0:T(1,128)}, /*index=5*/f32[1,192]{1,0:T(1,128)}) custom-call(s32[4]{0:T(128)S(1)} %pad_add_fusion.flags, bf16[256,384]{1,0:T(8,128)(2,1)S(1)} %reshape.59.mine_ref, bf16[256,384]{1,0:T(8,128)(2,1)S(1)} %collective-permute-done.9.other_ref, ...), custom_call_target="tpu_custom_call" | custom-call | bytes 2097152 | tf_op jit(solution)/shard_map/finish/pallas_call | solution.py:578
  (9 shorter events, 0.2 us)
Async XLA Ops:
  0.6 9.1 %copy-start.9 = (f32[192]{0:T(256)S(1)}, f32[192]{0:T(256)}, u32[]{:S(2)}) copy-start(f32[192]{0:T(256)} %param.15) | copy-start | bytes 2308
  0.6 9.1 %copy-start.8 = (f32[192]{0:T(256)S(1)}, f32[192]{0:T(256)}, u32[]{:S(2)}) copy-start(f32[192]{0:T(256)} %param.14) | copy-start | bytes 2308
  0.7 9.1 %copy-start.7 = (f32[576,3,3]{0,2,1:T(4,128)S(1)}, f32[576,3,3]{0,2,1:T(4,128)}, u32[]{:S(2)}) copy-start(f32[576,3,3]{0,2,1:T(4,128)} %param.11) | copy-start | bytes 62212
  0.8 1.1 copy-start
  1.9 1.1 copy-start.5
  3.0 6.7 %copy-start.4 = (bf16[576,192]{0,1:T(8,128)(2,1)S(1)}, bf16[576,192]{0,1:T(8,128)(2,1)}, u32[]{:S(2)}) copy-start(bf16[576,192]{0,1:T(8,128)(2,1)} %param.10) | copy-start | bytes 663556
  3.0 6.7 %copy-start.6 = (bf16[192,192]{1,0:T(8,128)(2,1)S(1)}, bf16[192,192]{1,0:T(8,128)(2,1)}, u32[]{:S(2)}) copy-start(bf16[192,192]{1,0:T(8,128)(2,1)} %wo_ref.1) | copy-start | bytes 221188
  4.5 7.5 %collective-permute-start.1 = (bf16[192,768]{1,0:T(8,128)(2,1)S(1)}, bf16[192,768]{1,0:T(8,128)(2,1)S(1)}, u32[]{:S(2)}, u32[]{:S(2)}) collective-permute-start(bf16[192,768]{1,0:T(8,128)(2,1)S(1)} %get-tuple-element.65), channel_id=1, source_target_pairs={{0,1},{1,0},{2,3},{3,2},{4,5},{5,4},{6,7},{7,6},{8,9},{9,8},{10,11... | collective-permute-start | bytes 884744 | tf_op jit(solution)/shard_map/ppermute | solution.py:476
  7.8 8.0 %collective-permute-start = (bf16[192,768]{1,0:T(8,128)(2,1)S(1)}, bf16[192,768]{1,0:T(8,128)(2,1)S(1)}, u32[]{:S(2)}, u32[]{:S(2)}) collective-permute-start(bf16[192,768]{1,0:T(8,128)(2,1)S(1)} %get-tuple-element.66), channel_id=1, source_target_pairs={{1,2},{3,4},{5,6},{7,8},{9,10},{11,12},{13,14},{15,16},{17,18},{19... | collective-permute-start | bytes 884744 | tf_op jit(solution)/shard_map/ppermute | solution.py:479
  29.8 1.3 %collective-permute-start.2 = (f32[96,128]{1,0:T(8,128)S(1)}, f32[96,128]{1,0:T(8,128)S(1)}, u32[]{:S(2)}, u32[]{:S(2)}) collective-permute-start(f32[96,128]{1,0:T(8,128)S(1)} %slice_select_fusion), channel_id=1, source_target_pairs={{0,1},{1,0},{2,3},{3,2},{4,5},{5,4},{6,7},{7,6},{8,9},{9,8},{10,11... | collective-permute-start | bytes 147464 | tf_op jit(solution)/shard_map/ppermute | solution.py:434
  31.1 4.0 %collective-permute-start.3 = (f32[96,128]{1,0:T(8,128)S(1)}, f32[96,128]{1,0:T(8,128)S(1)}, u32[]{:S(2)}, u32[]{:S(2)}) collective-permute-start(f32[96,128]{1,0:T(8,128)S(1)} %select_add_fusion), channel_id=1, source_target_pairs={{0,2},{1,3},{2,0},{3,1},{4,6},{5,7},{6,4},{7,5},{8,10},{9,11},{10,... | collective-permute-start | bytes 147464 | tf_op jit(solution)/shard_map/ppermute | solution.py:434
  31.2 20.5 %copy-start.10 = (f32[4]{0:T(128)S(1)}, f32[4]{0:T(128)}, u32[]{:S(2)}) copy-start(f32[4]{0:T(128)} %sharp.1) | copy-start | bytes 52
  35.2 5.1 %collective-permute-start.4 = (f32[96,128]{1,0:T(8,128)S(1)}, f32[96,128]{1,0:T(8,128)S(1)}, u32[]{:S(2)}, u32[]{:S(2)}) collective-permute-start(f32[96,128]{1,0:T(8,128)S(1)} %add.23), channel_id=1, source_target_pairs={{0,6},{1,7},{2,4},{3,5},{4,2},{5,3},{6,0},{7,1},{8,14},{9,15},{10,... | collective-permute-start | bytes 147464 | tf_op jit(solution)/shard_map/ppermute | solution.py:434
  40.3 3.0 %collective-permute-start.5 = (f32[96,128]{1,0:T(8,128)S(1)}, f32[96,128]{1,0:T(8,128)S(1)}, u32[]{:S(2)}, u32[]{:S(2)}) collective-permute-start(f32[96,128]{1,0:T(8,128)S(1)} %add.24), channel_id=1, source_target_pairs={{0,8},{1,9},{2,10},{3,11},{4,12},{5,13},{6,14},{7,15},{8,0},{9,1},... | collective-permute-start | bytes 147464 | tf_op jit(solution)/shard_map/ppermute | solution.py:434
  43.3 4.2 %collective-permute-start.6 = (f32[96,128]{1,0:T(8,128)S(1)}, f32[96,128]{1,0:T(8,128)S(1)}, u32[]{:S(2)}, u32[]{:S(2)}) collective-permute-start(f32[96,128]{1,0:T(8,128)S(1)} %add.25), channel_id=1, source_target_pairs={{0,16},{1,17},{2,18},{3,19},{4,20},{5,21},{6,22},{7,23},{8,24},{9,... | collective-permute-start | bytes 147464 | tf_op jit(solution)/shard_map/ppermute | solution.py:434
  47.5 4.2 %collective-permute-start.7 = (f32[96,128]{1,0:T(8,128)S(1)}, f32[96,128]{1,0:T(8,128)S(1)}, u32[]{:S(2)}, u32[]{:S(2)}) collective-permute-start(f32[96,128]{1,0:T(8,128)S(1)} %add.26.mine_ref), channel_id=1, source_target_pairs={{0,1},{1,0},{2,3},{3,2},{4,5},{5,4},{6,7},{7,6},{8,9},{9,8},{10,11... | collective-permute-start | bytes 147464 | tf_op jit(solution)/shard_map/ppermute | solution.py:434
  69.6 1.4 %copy-start.2 = (bf16[576,2048]{1,0:T(8,128)(2,1)}, bf16[576,2048]{1,0:T(8,128)(2,1)S(1)}, u32[]{:S(2)}) copy-start(bf16[576,2048]{1,0:T(8,128)(2,1)S(1)} %get-tuple-element.53.gp_ref) | copy-start | bytes 7077892
  71.0 17.8 %copy-start.1 = (bf16[1,192,8,256]{3,2,1,0:T(8,128)(2,1)S(1)}, bf16[1,192,8,256]{3,2,1,0:T(8,128)(2,1)}, u32[]{:S(2)}) copy-start(bf16[1,192,8,256]{3,2,1,0:T(8,128)(2,1)} %param.9) | copy-start | bytes 2359300
  71.1 1.7 %collective-permute-start.8 = (bf16[256,384]{1,0:T(8,128)(2,1)S(1)}, bf16[256,384]{1,0:T(8,128)(2,1)S(1)}, u32[]{:S(2)}, u32[]{:S(2)}) collective-permute-start(bf16[256,384]{1,0:T(8,128)(2,1)S(1)} %broadcast_select_fusion.4), channel_id=1, source_target_pairs={{0,1},{1,0},{2,3},{3,2},{4,5},{5,4},{6,7},{7,6},{8,9},{9,8},{10,11... | collective-permute-start | bytes 589832 | tf_op jit(solution)/shard_map/ppermute | solution.py:434
  73.6 27.3 %all-to-all-start = ((bf16[128,2,384]{2,1,0:T(2,128)(2,1)}), bf16[128,2,384]{2,1,0:T(2,128)(2,1)S(1)}, u32[]{:S(2)}, u32[]{:S(2)}) async-start(bf16[128,2,384]{2,1,0:T(2,128)(2,1)} %reshape.57), calls=%async_computation | async-start | bytes 393216 | tf_op jit(solution)/shard_map/all_to_all | solution.py:571
  88.9 1.7 %copy-start.3 = (bf16[576,2048]{1,0:T(8,128)(2,1)S(1)}, bf16[576,2048]{1,0:T(8,128)(2,1)}, u32[]{:S(2)}) copy-start(bf16[576,2048]{1,0:T(8,128)(2,1)} %copy-done.2) | copy-start | bytes 7077892
  119.1 4.2 %collective-permute-start.9 = (bf16[256,384]{1,0:T(8,128)(2,1)S(1)}, bf16[256,384]{1,0:T(8,128)(2,1)S(1)}, u32[]{:S(2)}, u32[]{:S(2)}) collective-permute-start(bf16[256,384]{1,0:T(8,128)(2,1)S(1)} %reshape.59.mine_ref), channel_id=1, source_target_pairs={{0,1},{1,0},{2,3},{3,2},{4,5},{5,4},{6,7},{7,6},{8,9},{9,8},{10,11... | collective-permute-start | bytes 589832 | tf_op jit(solution)/shard_map/ppermute | solution.py:434

commit v3 on v2

--- a/solution.py
+++ b/solution.py
@@ -13,7 +13,6 @@
 NT = (((1,), (1,)), ((), ()))
 TN = (((0,), (0,)), ((), ()))
 VMEM = pl.BlockSpec(memory_space=pltpu.VMEM)
-SMEM = pl.BlockSpec(memory_space=pltpu.SMEM)
 HBM = pl.BlockSpec(memory_space=pltpu.HBM)
 HI = lax.Precision.HIGHEST
 
@@ -22,12 +21,12 @@
     return pltpu.CompilerParams(vmem_limit_bytes=limit_mib << 20)
 
 
-def call(body, outs, n_in, smem=(), hbm=(), scratch=(), limit=32, flops=0, name=None, moved=0):
+def call(body, outs, n_in, hbm_out=(), scratch=(), limit=32, flops=0, name=None, moved=0):
     return pl.pallas_call(
         body,
         out_shape=tuple(jax.ShapeDtypeStruct(s, d) for s, d in outs),
-        in_specs=[SMEM if i in smem else HBM if i in hbm else VMEM for i in range(n_in)],
-        out_specs=tuple(VMEM for _ in outs),
+        in_specs=[VMEM for _ in range(n_in)],
+        out_specs=tuple(HBM if i in hbm_out else VMEM for i in range(len(outs))),
         scratch_shapes=list(scratch),
         compiler_params=params(limit),
         cost_estimate=pl.CostEstimate(flops=flops, bytes_accessed=moved, transcendentals=0),
@@ -58,31 +57,35 @@
     return jnp.concatenate(parts, axis=1)
 
 
-def shifters(w):
-    row, col = iota((w, w), 0), iota((w, w), 1)
-    right = jnp.where(row + 1 == col, 1.0, 0.0)
-    left = jnp.where(row == col + 1, 1.0, 0.0)
-    return jnp.concatenate([right, left], axis=1).astype(BF16)
-
-
-def moved_rows(blocks, shift):
-    w = blocks[0].shape[1]
-    n = blocks[0].shape[0]
-    both = mm(jnp.concatenate(blocks, axis=0), shift)
-    out = []
-    for i, v in enumerate(blocks):
-        at = slice(i * n, (i + 1) * n)
-        out.append((halves(both[at, 0:w]), [x.astype(F32) for x in halves(v)], halves(both[at, w:])))
-    return out
-
-
-def taps_sum(k, rows, order, i):
-    total = None
-    for a in range(3):
-        for b in range(3):
-            term = k[3 * a + b] * rows[order[a]][order[b]][i]
-            total = term if total is None else total + term
-    return total
+def shift_right(parts):
+    first = iota(parts[0].shape, 1) == 0
+    moved = [pltpu.roll(p, 1, 1) for p in parts]
+    before = [jnp.zeros_like(parts[0])] + moved[:-1]
+    return [jnp.where(first, b, m) for b, m in zip(before, moved)]
+
+
+def shift_left(parts):
+    last = iota(parts[0].shape, 1) == 127
+    moved = [pltpu.roll(p, 127, 1) for p in parts]
+    after = moved[1:] + [jnp.zeros_like(parts[0])]
+    return [jnp.where(last, a, m) for a, m in zip(after, moved)]
+
+
+def combine(k, window, order):
+    count = range(len(window[0]))
+    return [
+        [sum(k[3 * a + b] * window[order[a]][i] for a in range(3)) for i in count]
+        for b in range(3)
+    ]
+
+
+def each_group(total, body, batch=6):
+    def trip(g, carry):
+        for j in range(batch):
+            body(pl.ds(pl.multiple_of((g * batch + j) * 16, 16), 16))
+        return carry
+
+    lax.fori_loop(0, total // (16 * batch), trip, 0)
 
 
 def spread_body(flags, x_ref, dy_ref, x2_ref, dy2_ref, up_ref, dn_ref, s):
@@ -146,16 +149,14 @@
         p_ref[:, at] = mm(w_ref[...], normed).astype(BF16)
 
 
-def mix_rows(first, last, row, shift, cols_ref, ch, put):
+def mix_rows(first, last, row, cols_ref, ch, put):
     k = [cols_ref[t, ch, :] for t in range(9)]
-    moved = moved_rows([row(r) for r in range(first - 1, last + 1)], shift)
+    window = [row(first - 1), row(first), None]
     for r in range(first, last):
-        at = r - first
-        put(r, [taps_sum(k, moved[at : at + 3], (0, 1, 2), i) for i in range(len(moved[0][0]))])
-
-
-def channels(g):
-    return pl.ds(pl.multiple_of(g * 16, 16), 16)
+        window[2] = row(r + 1)
+        u = combine(k, window, (0, 1, 2))
+        put(r, [x + y + z for x, y, z in zip(u[1], shift_right(u[0]), shift_left(u[2]))])
+        window = [window[1], window[2], None]
 
 
 def row_reader(p_ref, ph_ref, ch, w):
@@ -171,26 +172,29 @@
     return row
 
 
+def wide_reader(p_ref, ph_ref, ch, w):
+    row = row_reader(p_ref, ph_ref, ch, w)
+    return lambda r: [v.astype(F32) for v in halves(row(r))]
+
+
 def mix_body(
     flags, p_ref, up_ref, dn_ref, dy2_ref, w_ref, wot_ref, cols_ref, affine_ref,
-    mixed_ref, ph_ref, pay_ref, t_ref, sq, gs, shift, *, w, heads,
+    mixed_ref, ph_ref, pay_ref, t_ref, sq, gs, *, w, heads,
 ):
     c3 = p_ref.shape[0]
     c = c3 // 3
     hs = c // heads
     rows = p_ref.shape[1] // w
     gain, bias = affine(affine_ref, w)
-    keep_up = 1.0 - flags[0].astype(F32)
-    keep_dn = 1.0 - flags[1].astype(F32)
-    shift[...] = shifters(w)
+    keep_up = flags[0:1, 0:1]
+    keep_dn = flags[1:2, 0:1]
     for src, keep, base in ((up_ref, keep_up, 0), (dn_ref, keep_dn, 2)):
         for h in range(2):
             normed = normalise(src[:, h * w : (h + 1) * w].astype(F32), gain, bias)[2]
             at = slice((base + h) * w, (base + h + 1) * w)
             ph_ref[:, at] = (mm(w_ref[...], normed) * keep).astype(BF16)
 
-    def group(g, carry):
-        ch = channels(g)
+    def group(ch):
         total = []
 
         def put(r, out):
@@ -202,11 +206,10 @@
                 if len(total) > 1:
                     total[:] = [total[0] + total[1]]
 
-        mix_rows(0, rows, row_reader(p_ref, ph_ref, ch, w), shift[...], cols_ref, ch, put)
-        sq[ch, :] = jnp.broadcast_to(jnp.sum(total[0], axis=1, keepdims=True), (16, 128))
-        return carry
-
-    lax.fori_loop(0, c3 // 16, group, 0)
+        mix_rows(0, rows, wide_reader(p_ref, ph_ref, ch, w), cols_ref, ch, put)
+        sq[ch, :] = total[0]
+
+    each_group(c3, group)
 
     query = mixed_ref[0:c, :]
     key = mixed_ref[c : 2 * c, :]
@@ -220,45 +223,37 @@
         at = slice(h * hs, (h + 1) * hs)
         gram = pltpu.roll(gs[0, at, :], (256 - hs * h) % 256, 1)[:, 0:128]
         grad = pltpu.roll(gs[1, at, :], (256 + hs - hs * h) % 256, 1)[:, 0:128]
-        key_sq = sq[c + h * hs : c + (h + 1) * hs, :]
-        rest = jnp.where(lane == 2 * hs, sq[at, :], key_sq)
+        query_sq = jnp.sum(sq[at, :], axis=1, keepdims=True)
+        key_sq = jnp.sum(sq[c + h * hs : c + (h + 1) * hs, :], axis=1, keepdims=True)
+        rest = jnp.where(lane == 2 * hs, query_sq, key_sq)
         pay_ref[at, :] = jnp.where(lane < hs, gram, jnp.where(lane < 2 * hs, grad, rest))
 
 
-def edge_body(p_ref, ph_ref, cols_ref, mh_ref, shift, *, w):
+def edge_body(p_ref, ph_ref, cols_ref, mh_ref, *, w):
     rows = p_ref.shape[1] // w
-    shift[...] = shifters(w)
-
-    def group(g, carry):
-        places = [channels(2 * g + part) for part in range(2)]
-        edges = (-1, rows)
-        blocks = []
-        for ch in places:
-            row = row_reader(p_ref, ph_ref, ch, w)
-            blocks += [row(r + d) for r in edges for d in (-1, 0, 1)]
-        moved = moved_rows(blocks, shift[...])
-        for j, ch in enumerate(places):
-            k = [cols_ref[t, ch, :] for t in range(9)]
-            for i in range(2):
-                near = moved[6 * j + 3 * i : 6 * j + 3 * i + 3]
-                out = [taps_sum(k, near, (0, 1, 2), q) for q in range(w // 128)]
+
+    def group(ch):
+        row = wide_reader(p_ref, ph_ref, ch, w)
+        for i, r in enumerate((-1, rows)):
+            def put(_, out):
                 mh_ref[ch, i * w : (i + 1) * w] = joined(out).astype(BF16)
-        return carry
-
-    lax.fori_loop(0, p_ref.shape[0] // 32, group, 0)
+
+            mix_rows(r, r + 1, row, cols_ref, ch, put)
+
+    each_group(p_ref.shape[0], group)
 
 
 def back_body(
     flags, sharp, mine_ref, other_ref, mixed_ref, mh_ref, p_ref, ph_ref, dy2_ref, up_ref, dn_ref,
     std_ref, t_ref, wot_ref, cols_ref,
-    gp_ref, left_ref, right_ref, pay, coef, mats, vecs, gm, aug, grads, shift, *, w, heads,
+    gp_hbm, left_ref, right_ref, pay, coef, sums, mats, vecs, gm, aug, grads, gp_ref, sem, *, w, heads,
 ):
     c = mixed_ref.shape[0] // 3
     hs = c // heads
     rows = p_ref.shape[1] // w
-    first_core = flags[3] == 0
     mine = mine_ref[...]
     other = other_ref[...]
+    first_core = jnp.broadcast_to(flags[3:4, :], mine.shape) < 0.5
     pay[0 : c // 2, :] = jnp.where(first_core, mine, other)
     pay[c // 2 : c, :] = jnp.where(first_core, other, mine)
     lane = iota((hs, 128), 1)
@@ -278,13 +273,13 @@
         )
         length = jnp.sqrt(query_sq) * jnp.sqrt(key_sq)
         cosine = gram / length
-        weights = jnp.where(valid, jnp.exp(cosine * sharp[h]), 0.0)
+        weights = jnp.where(valid, jnp.exp(cosine * sharp[0:1, h : h + 1]), 0.0)
         attention = weights / jnp.sum(weights, axis=1, keepdims=True)
         scores = attention * (grad - jnp.sum(attention * grad, axis=1, keepdims=True))
         terms = scores * cosine
         sharp_h = jnp.sum(jnp.sum(terms, axis=1, keepdims=True), axis=0, keepdims=True)
         sharp_row = jnp.where(iota((1, 128), 1) == h, sharp_h, sharp_row)
-        grad_cos = scores * sharp[h]
+        grad_cos = scores * sharp[0:1, h : h + 1]
         terms = grad_cos * cosine
         alpha = jnp.sum(terms, axis=1, keepdims=True) / query_sq
         beta = jnp.sum(terms, axis=0, keepdims=True) / key_sq
@@ -325,39 +320,53 @@
         )
         for i, part in enumerate(parts):
             if r == 0:
-                part = part * (1.0 - flags[0].astype(F32))
+                part = part * flags[0:1, 0:1]
             if r == rows + 1:
-                part = part * (1.0 - flags[1].astype(F32))
+                part = part * flags[1:2, 0:1]
             gm[i * c : (i + 1) * c, at] = part.astype(BF16)
 
-    shift[...] = shifters(w)
-
-    def group(g, carry):
-        ch = channels(g)
+    def input_grad(ch):
         k = [cols_ref[t, ch, :] for t in range(9)]
-        row = row_reader(p_ref, ph_ref, ch, w)
-        moved = moved_rows([gm[ch, r * w : (r + 1) * w] for r in range(rows + 2)], shift[...])
+
+        def row(r):
+            return [v.astype(F32) for v in halves(gm[ch, r * w : (r + 1) * w])]
+
+        window = [None, row(0), row(1)]
+        for r in range(rows):
+            window = [window[1], window[2], row(r + 2)]
+            u = combine(k, window, (2, 1, 0))
+            out = [x + y + z for x, y, z in zip(u[1], shift_left(u[0]), shift_right(u[2]))]
+            gp_ref[ch, r * w : (r + 1) * w] = joined(out).astype(BF16)
+
+    each_group(3 * c, input_grad)
+    copies = []
+    for i in range(3):
+        at = pl.ds(i * c, c)
+        copies.append(pltpu.make_async_copy(gp_ref.at[at], gp_hbm.at[at], sem.at[i]))
+        copies[-1].start()
+
+    def stencil(ch):
+        row = wide_reader(p_ref, ph_ref, ch, w)
         acc = [None] * 9
-        window = [None] + [[v.astype(F32) for v in halves(row(r))] for r in (-1, 0)]
+        window = [None, row(-1), row(0)]
         for r in range(rows):
-            window = [window[1], window[2], [v.astype(F32) for v in halves(row(r + 1))]]
-            parts = range(w // 128)
-            out = [taps_sum(k, moved[r : r + 3], (2, 1, 0), i) for i in parts]
-            gp_ref[ch, r * w : (r + 1) * w] = joined(out).astype(BF16)
-            for a in range(3):
-                for b in range(3):
-                    t = 3 * a + b
-                    for i in parts:
-                        term = moved[r + 1][2 - b][i] * window[a][i]
-                        acc[t] = term if acc[t] is None else acc[t] + term
-        lanes = iota((16, 128), 1)
-        out = jnp.zeros((16, 128), F32)
+            window = [window[1], window[2], row(r + 1)]
+            v = [x.astype(F32) for x in halves(gm[ch, (r + 1) * w : (r + 2) * w])]
+            moved = (shift_left(v), v, shift_right(v))
+            for t in range(9):
+                for x, y in zip(moved[t % 3], window[t // 3]):
+                    acc[t] = x * y if acc[t] is None else acc[t] + x * y
         for t in range(9):
-            out = jnp.where(lanes == t, jnp.sum(acc[t], axis=1, keepdims=True), out)
-        coef[ch, :] = out
-        return carry
-
-    lax.fori_loop(0, gm.shape[0] // 16, group, 0)
+            sums[ch, t * 128 : (t + 1) * 128] = acc[t]
+
+    each_group(3 * c, stencil)
+    place = iota((9 * 128, 128), 0) // 128 == iota((9 * 128, 128), 1)
+    place = jnp.where(place, 1.0, 0.0).astype(BF16)
+    for g in range(0, 3 * c, 64):
+        block = sums[g : g + 64, :]
+        high = block.astype(BF16)
+        low = (block - high.astype(F32)).astype(BF16)
+        coef[g : g + 64, :] = mm(high, place) + mm(low, place)
 
     aug[0:c, :] = std_ref[...]
     aug[c : c + 16, :] = jnp.where(iota((16, rows * w), 0) == 0, 1.0, 0.0).astype(BF16)
@@ -365,8 +374,7 @@
     grads[...] = jnp.zeros_like(grads)
     grads[0 : c + 16, 0:c3] = mm(aug[...], gp_ref[...], NT)
     grads[c + 16 : c + 32, :] = coef[...].T[0:16, :]
-    lead = 1.0 - jnp.minimum(flags[2], 1).astype(F32)
-    grads[c + 1 : c + 2, 0:128] = sharp_row * lead
+    grads[c + 1 : c + 2, 0:128] = sharp_row * flags[2:3, :]
     out_pad = jnp.concatenate([outgoing, jnp.zeros((c, 256 - c), F32)], axis=1)
     half = c3 % 128
     tail = grads[0:c, c3 - half : c3 - half + 128]
@@ -376,6 +384,8 @@
     right_ref[:, 0:256] = grads[:, 384:640].astype(BF16)
     right_ref[0:c, 256:384] = out_pad[:, 0:128].astype(BF16)
     right_ref[c:, 256:384] = jnp.zeros((grads.shape[0] - c, 128), BF16)
+    for copy in copies:
+        copy.wait()
 
 
 def output_body(gp_ref, wt_ref, std_ref, inv_ref, dy_ref, affine_ref, out_ref, s, *, w):
@@ -401,9 +411,9 @@
     triple_ref, taps_ref, outgoing_ref, sharp_ref, scaling_ref, offset_ref, full,
 ):
     c, c3 = wt_ref.shape
-    first_core = flags[3] == 0
     mine = mine_ref[...].astype(F32)
     other = other_ref[...].astype(F32)
+    first_core = jnp.broadcast_to(flags[3:4, 0:1], mine.shape) < 0.5
     full[:, 0:384] = jnp.where(first_core, mine, other)
     full[:, 384:768] = jnp.where(first_core, other, mine)
     m = full[0:c, 0:c3]
@@ -454,7 +464,8 @@
         n = rows * w
         core = lax.axis_index("core")
         place = lax.axis_index("chip") * 2 + core
-        flags = jnp.stack([place == 0, place == tile - 1, place, core]).astype(jnp.int32)
+        flags = jnp.stack([place != 0, place != tile - 1, place == 0, core == 1]).astype(F32)
+        flags = jnp.broadcast_to(jnp.pad(flags, (0, 4))[:, None], (8, 128))
         x3 = x.reshape(c, rows, w)
         dy3 = dy.reshape(c, rows, w)
         taps = jnp.transpose(stencil, (1, 2, 0))
@@ -466,7 +477,6 @@
             spread_body,
             [((c, n), BF16), ((c, n), BF16), ((c, 3 * w), BF16), ((c, 3 * w), BF16)],
             3,
-            smem=(0,),
             scratch=[pltpu.VMEM((2, w // 128, c * rows, 128), F32)],
             limit=8,
             name="spread",
@@ -501,11 +511,9 @@
             functools.partial(mix_body, w=w, heads=heads),
             [((c3, n), BF16), ((c3, 4 * w), BF16), ((c, 128), F32), ((c, c), F32)],
             9,
-            smem=(0,),
             scratch=[
                 pltpu.VMEM((c3, 128), F32),
                 pltpu.VMEM((2, c, 256), F32),
-                pltpu.VMEM((w, 2 * w), BF16),
             ],
             limit=12,
             flops=8 * c * c * n,
@@ -521,7 +529,6 @@
             functools.partial(edge_body, w=w),
             [((c3, 2 * w), BF16)],
             3,
-            scratch=[pltpu.VMEM((w, 2 * w), BF16)],
             limit=8,
             moved=6 << 20,
             name="edge",
@@ -538,22 +545,24 @@
             functools.partial(back_body, w=w, heads=heads),
             [((c3, n), BF16), ((size, 384), BF16), ((size, 384), BF16)],
             15,
-            smem=(0, 1),
+            hbm_out=(0,),
             scratch=[
                 pltpu.VMEM((c, 128), F32),
                 pltpu.VMEM((640, 128), F32),
+                pltpu.VMEM((c3, 9 * 128), F32),
                 pltpu.VMEM((2, c, 256), BF16),
                 pltpu.VMEM((c, 256), F32),
                 pltpu.VMEM((c3, (rows + 2) * w), BF16),
                 pltpu.VMEM((c + 16, n), BF16),
                 pltpu.VMEM((size, 640), F32),
-                pltpu.VMEM((w, 2 * w), BF16),
+                pltpu.VMEM((c3, n), BF16),
+                pltpu.SemaphoreType.DMA((3,)),
             ],
-            limit=20,
+            limit=24,
             flops=20 * c * c * n,
             moved=8 << 20,
             name="back",
-        )(flags, sharpness, mine, other, mixed, mh, p, ph, dy2, up_in, dn_in, std, t, wot, cols)
+        )(flags, sharpness.reshape(1, heads), mine, other, mixed, mh, p, ph, dy2, up_in, dn_in, std, t, wot, cols)
 
         (fm,) = call(
             functools.partial(output_body, w=w),
@@ -579,7 +588,6 @@
             finish_body,
             [((c, c3), F32), ((3, 3, c3), F32), ((c, c), F32), ((1, heads), F32), ((1, c), F32), ((1, c), F32)],
             6,
-            smem=(0,),
             scratch=[pltpu.VMEM((size, 768), F32)],
             limit=16,
             name="finish",

time: 125 us -> 110 us (0.88)
  Pallas kernels: 43.5 us -> 25.1 us
  starting transfers between devices: 35 us -> 36.5 us
    pallas_call x1, Pallas kernels: 13.9 us -> 5.54 us  [local(): call(functools.partial(mix_body, w=w, heads=heads), [((c3, n), BF16), ((c...]
    pallas_call x1, Pallas kernels: 17.9 us -> 11.7 us  [local(): call(functools.partial(back_body, w=w, heads=heads), [((c3, n), BF16), ((...]
    pallas_call x1, Pallas kernels: 3.92 us -> 1.12 us  [local(): call(functools.partial(edge_body, w=w), [((c3, 2 * w), BF16)], 3, limit=8...]
    ppermute x8, starting transfers between devices: 14.6 us -> 16.6 us  [swap(): return lax.ppermute(v, ALL, [(i, i ^ mask) for i in range(count)])]
    ppermute x8, waiting for transfers between devices: 9.24 us -> 10.5 us  [swap(): return lax.ppermute(v, ALL, [(i, i ^ mask) for i in range(count)])]
  transfers between devices with their start and end apart: 11 -> 11, of which waited for: 9 -> 10; matrix products, arithmetic and copies ran while one was open for 0% -> 0% of each run, Pallas kernels for 7% -> 5%
where the time goes in v3:
time: 110 us; the launch traced here: 109 us
  starting transfers between devices  36.5 us (33%)
  Pallas kernels  25.1 us (23%)
  waiting for transfers between devices  22.1 us (20%)
  blocking collectives  17.8 us (16%)
  local copies, waits for them, and re-layouts  6.39 us (6%)
    all_to_all x1, blocking collectives, local(): part = lax.all_to_all(jnp.broadcast_to(piece, got.shape), GROUP, 0, 0)  17.8 us
    ppermute x8, starting transfers between devices, swap(): return lax.ppermute(v, ALL, [(i, i ^ mask) for i in range(count)])  16.6 us
    all_to_all x1, starting transfers between devices, local(): got = lax.all_to_all(part.reshape(chips, each, 384), GROUP, 0, 0)  14.7 us
    pallas_call x1, Pallas kernels, local(): call(functools.partial(back_body, w=w, heads=heads), [((c3, n), BF16), ((...  11.7 us
    ppermute x8, waiting for transfers between devices, swap(): return lax.ppermute(v, ALL, [(i, i ^ mask) for i in range(count)])  10.5 us
    all_to_all x1, waiting for transfers between devices, local(): got = lax.all_to_all(part.reshape(chips, each, 384), GROUP, 0, 0)  7.81 us
    pallas_call x1, Pallas kernels, local(): call(functools.partial(mix_body, w=w, heads=heads), [((c3, n), BF16), ((c...  5.54 us
    unnamed x22, local copies, waits for them, and re-layouts  5.38 us
  transfers between devices with their start and end apart: 11, of which 10 were waited for; matrix products, arithmetic and copies ran while one was open for 0% of the time, Pallas kernels for 5%

profile of v3, /device:TPU:1, one launch (start us, length us, event | category | flops | bytes accessed | tf_op | source)
XLA Modules:
  0.0 109.3 jit_solution(17719125104727086582)
XLA Ops:
  0.6 0.0 copy-start.9
  0.6 0.0 copy-start.8
  0.7 0.0 copy-start.7
  0.7 0.1 pad_add_fusion
  0.8 0.1 broadcast_in_dim.6.flags
  0.8 0.0 copy-start
  0.8 1.1 %copy-done = bf16[1,192,8,256]{3,2,1,0:T(8,128)(2,1)S(1)} copy-done((bf16[1,192,8,256]{3,2,1,0:T(8,128)(2,1)S(1)}, bf16[1,192,8,256]{3,2,1,0:T(8,128)(2,1)}, u32[]{:S(2)}) %copy-start) | copy-done | bytes 786456
  2.0 0.0 copy-start.5
  2.0 1.1 %copy-done.5 = bf16[1,192,8,256]{3,2,1,0:T(8,128)(2,1)S(1)} copy-done((bf16[1,192,8,256]{3,2,1,0:T(8,128)(2,1)S(1)}, bf16[1,192,8,256]{3,2,1,0:T(8,128)(2,1)}, u32[]{:S(2)}) %copy-start.5) | copy-done | bytes 786456
  3.1 0.0 copy-start.4
  3.1 0.0 copy-start.6
  3.1 0.9 spread.1
  4.0 3.3 %collective-permute-start.1 = (bf16[192,768]{1,0:T(8,128)(2,1)S(1)}, bf16[192,768]{1,0:T(8,128)(2,1)S(1)}, u32[]{:S(2)}, u32[]{:S(2)}) collective-permute-start(bf16[192,768]{1,0:T(8,128)(2,1)S(1)} %get-tuple-element.65), channel_id=1, source_target_pairs={{0,1},{1,0},{2,3},{3,2},{4,5},{5,4},{6,7},{7,6},{8,9},{9,8},{10,11... | collective-permute-start | bytes 884744 | tf_op jit(solution)/shard_map/ppermute | solution.py:486
  7.3 1.9 %collective-permute-start = (bf16[192,768]{1,0:T(8,128)(2,1)S(1)}, bf16[192,768]{1,0:T(8,128)(2,1)S(1)}, u32[]{:S(2)}, u32[]{:S(2)}) collective-permute-start(bf16[192,768]{1,0:T(8,128)(2,1)S(1)} %get-tuple-element.66), channel_id=1, source_target_pairs={{1,2},{3,4},{5,6},{7,8},{9,10},{11,12},{13,14},{15,16},{17,18},{19... | collective-permute-start | bytes 884744 | tf_op jit(solution)/shard_map/ppermute | solution.py:489
  9.2 0.0 copy-done.9
  9.2 0.0 copy-done.8
  9.3 0.0 copy-done.7
  9.3 0.0 copy-done.4
  9.3 0.0 copy-done.6
  9.3 1.1 %columns.1 = (f32[9,576,128]{2,1,0:T(8,128)S(1)}, f32[2,192,128]{2,1,0:T(8,128)S(1)}, bf16[576,192]{1,0:T(8,128)(2,1)S(1)}, bf16[192,192]{1,0:T(8,128)(2,1)S(1)}) custom-call(f32[3,3,576]{2,1,0:T(4,128)S(1)} %bitcast.25, f32[1,192]{1,0:T(1,128)S(1)} %bitcast.26, f32[1,192]{1,0:T(1,128)S(1)} %bitcast.28, bf16[192,576]{1,0:T(8,128)(2,1)S(1)} %bitcast.21, ...), custom_call_target="tpu_custom_call" | custom-call | bytes 4194304 | tf_op jit(solution)/shard_map/columns/pallas_call | solution.py:490
  10.4 1.1 %project.1 = (bf16[576,2048]{1,0:T(8,128)(2,1)S(1)}, bf16[192,2048]{1,0:T(8,128)(2,1)S(1)}, f32[8,2048]{1,0:T(8,128)S(1)}) custom-call(bf16[192,2048]{1,0:T(8,128)(2,1)S(1)} %get-tuple-element.35.x2_ref, bf16[576,192]{1,0:T(8,128)(2,1)S(1)} %get-tuple-element.36.w_ref, f32[2,192,128]{2,1,0:T(8,128)S(1)} %get-tuple-element.37.affine_ref), custom_call_target="tpu_custom_call" | custom-call | flops 452984832 | bytes 8388608 | tf_op jit(solution)/shard_map/project/pallas_call | solution.py:499
  11.5 0.0 collective-permute-done.1
  11.5 3.8 %collective-permute-done = bf16[192,768]{1,0:T(8,128)(2,1)S(1)} collective-permute-done((bf16[192,768]{1,0:T(8,128)(2,1)S(1)}, bf16[192,768]{1,0:T(8,128)(2,1)S(1)}, u32[]{:S(2)}, u32[]{:S(2)}) %collective-permute-start) | collective-permute-done | bytes 294944 | tf_op jit(solution)/shard_map/ppermute | solution.py:489
  15.3 0.1 broadcast_select_fusion
  15.4 5.5 %mix.1 = (bf16[576,2048]{1,0:T(8,128)(2,1)S(1)}, bf16[576,1024]{1,0:T(8,128)(2,1)S(1)}, f32[192,128]{1,0:T(8,128)S(1)}, f32[192,192]{1,0:T(8,128)S(1)}) custom-call(f32[8,128]{1,0:T(8,128)S(1)} %broadcast_in_dim.6.flags, bf16[576,2048]{1,0:T(8,128)(2,1)S(1)} %get-tuple-element.38.p_ref, bf16[192,768]{1,0:T(8,128)(2,1)S(1)} %get-tuple-element.64.up_ref, ...), custom_call_target="tpu_custom_call" | custom-call | flops 603979776 | bytes 8388608 | tf_op jit(solution)/shard_map/mix/pallas_call | solution.py:510
  21.0 0.1 collective-permute-start.2
  21.1 1.2 %collective-permute-done.2 = f32[96,128]{1,0:T(8,128)S(1)} collective-permute-done((f32[96,128]{1,0:T(8,128)S(1)}, f32[96,128]{1,0:T(8,128)S(1)}, u32[]{:S(2)}, u32[]{:S(2)}) %collective-permute-start.2) | collective-permute-done | bytes 49184 | tf_op jit(solution)/shard_map/ppermute | solution.py:444
  22.3 0.1 collective-permute-start.3
  22.4 0.0 copy-start.10
  22.4 1.1 %edge.1.mh_ref = bf16[576,512]{1,0:T(8,128)(2,1)S(1)} custom-call(bf16[576,2048]{1,0:T(8,128)(2,1)S(1)} %get-tuple-element.38.p_ref, bf16[576,1024]{1,0:T(8,128)(2,1)S(1)} %get-tuple-element.45.ph_ref, f32[9,576,128]{2,1,0:T(8,128)S(1)} %get-tuple-element.43.cols_ref), custom_call_target="tpu_custom_call" | custom-call | bytes 6291456 | tf_op jit(solution)/shard_map/edge/pallas_call | solution.py:528
  23.6 1.8 %collective-permute-done.3 = f32[96,128]{1,0:T(8,128)S(1)} collective-permute-done((f32[96,128]{1,0:T(8,128)S(1)}, f32[96,128]{1,0:T(8,128)S(1)}, u32[]{:S(2)}, u32[]{:S(2)}) %collective-permute-start.3) | collective-permute-done | bytes 49184 | tf_op jit(solution)/shard_map/ppermute | solution.py:444
  25.4 3.2 %collective-permute-start.4 = (f32[96,128]{1,0:T(8,128)S(1)}, f32[96,128]{1,0:T(8,128)S(1)}, u32[]{:S(2)}, u32[]{:S(2)}) collective-permute-start(f32[96,128]{1,0:T(8,128)S(1)} %add.23), channel_id=1, source_target_pairs={{0,6},{1,7},{2,4},{3,5},{4,2},{5,3},{6,0},{7,1},{8,14},{9,15},{10,... | collective-permute-start | bytes 147464 | tf_op jit(solution)/shard_map/ppermute | solution.py:444
  28.6 1.5 %collective-permute-done.4 = f32[96,128]{1,0:T(8,128)S(1)} collective-permute-done((f32[96,128]{1,0:T(8,128)S(1)}, f32[96,128]{1,0:T(8,128)S(1)}, u32[]{:S(2)}, u32[]{:S(2)}) %collective-permute-start.4) | collective-permute-done | bytes 49184 | tf_op jit(solution)/shard_map/ppermute | solution.py:444
  30.1 1.7 %collective-permute-start.5 = (f32[96,128]{1,0:T(8,128)S(1)}, f32[96,128]{1,0:T(8,128)S(1)}, u32[]{:S(2)}, u32[]{:S(2)}) collective-permute-start(f32[96,128]{1,0:T(8,128)S(1)} %add.24), channel_id=1, source_target_pairs={{0,8},{1,9},{2,10},{3,11},{4,12},{5,13},{6,14},{7,15},{8,0},{9,1},... | collective-permute-start | bytes 147464 | tf_op jit(solution)/shard_map/ppermute | solution.py:444
  31.8 1.5 %collective-permute-done.5 = f32[96,128]{1,0:T(8,128)S(1)} collective-permute-done((f32[96,128]{1,0:T(8,128)S(1)}, f32[96,128]{1,0:T(8,128)S(1)}, u32[]{:S(2)}, u32[]{:S(2)}) %collective-permute-start.5) | collective-permute-done | bytes 49184 | tf_op jit(solution)/shard_map/ppermute | solution.py:444
  33.3 2.9 %collective-permute-start.6 = (f32[96,128]{1,0:T(8,128)S(1)}, f32[96,128]{1,0:T(8,128)S(1)}, u32[]{:S(2)}, u32[]{:S(2)}) collective-permute-start(f32[96,128]{1,0:T(8,128)S(1)} %add.25), channel_id=1, source_target_pairs={{0,16},{1,17},{2,18},{3,19},{4,20},{5,21},{6,22},{7,23},{8,24},{9,... | collective-permute-start | bytes 147464 | tf_op jit(solution)/shard_map/ppermute | solution.py:444
  36.2 1.5 %collective-permute-done.6 = f32[96,128]{1,0:T(8,128)S(1)} collective-permute-done((f32[96,128]{1,0:T(8,128)S(1)}, f32[96,128]{1,0:T(8,128)S(1)}, u32[]{:S(2)}, u32[]{:S(2)}) %collective-permute-start.6) | collective-permute-done | bytes 49184 | tf_op jit(solution)/shard_map/ppermute | solution.py:444
  37.7 5.0 %collective-permute-start.7 = (f32[96,128]{1,0:T(8,128)S(1)}, f32[96,128]{1,0:T(8,128)S(1)}, u32[]{:S(2)}, u32[]{:S(2)}) collective-permute-start(f32[96,128]{1,0:T(8,128)S(1)} %add.26.mine_ref), channel_id=1, source_target_pairs={{0,1},{1,0},{2,3},{3,2},{4,5},{5,4},{6,7},{7,6},{8,9},{9,8},{10,11... | collective-permute-start | bytes 147464 | tf_op jit(solution)/shard_map/ppermute | solution.py:444
  42.6 0.9 collective-permute-done.7.other_ref
  43.5 0.0 copy-done.10
  43.5 11.7 %back.1 = (bf16[576,2048]{1,0:T(8,128)(2,1)S(1)}, bf16[256,384]{1,0:T(8,128)(2,1)S(1)}, bf16[256,384]{1,0:T(8,128)(2,1)S(1)}) custom-call(f32[8,128]{1,0:T(8,128)S(1)} %broadcast_in_dim.6.flags, f32[1,4]{1,0:T(1,128)S(1)} %bitcast.30, f32[96,128]{1,0:T(8,128)S(1)} %add.26.mine_ref, f32[96,128]{1,0:T(8,128)S(1)} %collective-permute-done.7.other_ref, ...), custom_call_target="tpu_custom_call" | custom-call | flops 1509949440 | bytes 8388608 | tf_op jit(solution)/shard_map/back/pallas_call | solution.py:544
  55.2 0.0 copy-start.2
  55.2 1.4 %copy-done.2 = bf16[576,2048]{1,0:T(8,128)(2,1)} copy-done((bf16[576,2048]{1,0:T(8,128)(2,1)}, bf16[576,2048]{1,0:T(8,128)(2,1)S(1)}, u32[]{:S(2)}) %copy-start.2) | copy-done | bytes 2359320
  56.6 0.0 copy-start.1
  56.6 0.4 collective-permute-start.8
  57.1 1.1 %collective-permute-done.8 = bf16[256,384]{1,0:T(8,128)(2,1)S(1)} collective-permute-done((bf16[256,384]{1,0:T(8,128)(2,1)S(1)}, bf16[256,384]{1,0:T(8,128)(2,1)S(1)}, u32[]{:S(2)}, u32[]{:S(2)}) %collective-permute-start.8) | collective-permute-done | bytes 196640 | tf_op jit(solution)/shard_map/ppermute | solution.py:444
  58.2 0.1 add_convert_fusion
  58.3 0.8 reshape.62
  59.0 14.7 %all-to-all-start = ((bf16[128,2,384]{2,1,0:T(2,128)(2,1)}), bf16[128,2,384]{2,1,0:T(2,128)(2,1)S(1)}, u32[]{:S(2)}, u32[]{:S(2)}) async-start(bf16[128,2,384]{2,1,0:T(2,128)(2,1)} %reshape.62), calls=%async_computation | async-start | bytes 393216 | tf_op jit(solution)/shard_map/all_to_all | solution.py:580
  73.7 0.0 copy-done.1
  73.7 0.0 copy-start.3
  73.7 1.7 %copy-done.3 = bf16[576,2048]{1,0:T(8,128)(2,1)S(1)} copy-done((bf16[576,2048]{1,0:T(8,128)(2,1)S(1)}, bf16[576,2048]{1,0:T(8,128)(2,1)}, u32[]{:S(2)}) %copy-start.3) | copy-done | bytes 2359320
  75.4 2.6 %output.1 = bf16[192,8,256]{2,1,0:T(8,128)(2,1)} custom-call(bf16[576,2048]{1,0:T(8,128)(2,1)S(1)} %copy-done.3, bf16[192,576]{1,0:T(8,128)(2,1)S(1)} %bitcast.22, bf16[192,2048]{1,0:T(8,128)(2,1)S(1)} %get-tuple-element.49.std_ref, f32[8,2048]{1,0:T(8,128)S(1)} %get-tuple-element.54.inv_ref, bf16[192,8,256]{2,1,0:T(8,128)(2,1)S(1)} %bitcast.20, ...), custom_call_target="tpu_custom_call" | custom-call | flops 452984832 | bytes 6291456 | tf_op jit(solution)/shard_map/output/pallas_call | solution.py:567
  77.9 7.8 %all-to-all-done = bf16[128,2,384]{2,1,0:T(2,128)(2,1)S(1)} async-done(((bf16[128,2,384]{2,1,0:T(2,128)(2,1)}), bf16[128,2,384]{2,1,0:T(2,128)(2,1)S(1)}, u32[]{:S(2)}, u32[]{:S(2)}) %all-to-all-start) | async-done | bytes 196640 | tf_op jit(solution)/shard_map/all_to_all | solution.py:580
  85.8 0.2 reduce_sum.12
  86.0 0.1 broadcast_in_dim.16
  86.1 17.8 %all_to_all.10 = bf16[128,2,384]{2,1,0:T(2,128)(2,1)S(1)} all-to-all(bf16[128,2,384]{2,1,0:T(2,128)(2,1)S(1)} %broadcast_in_dim.16), channel_id=1, replica_groups=mesh['img'=8,'chip'=16,'core'=2] {'img','chip'}, dimensions={0} | all-to-all | bytes 393216 | tf_op jit(solution)/shard_map/all_to_all | solution.py:583
  103.9 0.1 reshape.64.mine_ref
  104.0 3.2 %collective-permute-start.9 = (bf16[256,384]{1,0:T(8,128)(2,1)S(1)}, bf16[256,384]{1,0:T(8,128)(2,1)S(1)}, u32[]{:S(2)}, u32[]{:S(2)}) collective-permute-start(bf16[256,384]{1,0:T(8,128)(2,1)S(1)} %reshape.64.mine_ref), channel_id=1, source_target_pairs={{0,1},{1,0},{2,3},{3,2},{4,5},{5,4},{6,7},{7,6},{8,9},{9,8},{10,11... | collective-permute-start | bytes 589832 | tf_op jit(solution)/shard_map/ppermute | solution.py:444
  107.1 1.1 collective-permute-done.9.other_ref
  108.2 1.1 %finish.1 = (f32[192,576]{1,0:T(8,128)}, f32[3,3,576]{2,1,0:T(4,128)}, f32[192,192]{1,0:T(8,128)}, f32[1,4]{1,0:T(1,128)}, f32[1,192]{1,0:T(1,128)}, /*index=5*/f32[1,192]{1,0:T(1,128)}) custom-call(f32[8,128]{1,0:T(8,128)S(1)} %broadcast_in_dim.6.flags, bf16[256,384]{1,0:T(8,128)(2,1)S(1)} %reshape.64.mine_ref, ...), custom_call_target="tpu_custom_call" | custom-call | bytes 2097152 | tf_op jit(solution)/shard_map/finish/pallas_call | solution.py:587
  (9 shorter events, 0.1 us)
Async XLA Ops:
  0.6 8.6 %copy-start.9 = (f32[192]{0:T(256)S(1)}, f32[192]{0:T(256)}, u32[]{:S(2)}) copy-start(f32[192]{0:T(256)} %param.15) | copy-start | bytes 2308
  0.6 8.6 %copy-start.8 = (f32[192]{0:T(256)S(1)}, f32[192]{0:T(256)}, u32[]{:S(2)}) copy-start(f32[192]{0:T(256)} %param.14) | copy-start | bytes 2308
  0.7 8.6 %copy-start.7 = (f32[576,3,3]{0,2,1:T(4,128)S(1)}, f32[576,3,3]{0,2,1:T(4,128)}, u32[]{:S(2)}) copy-start(f32[576,3,3]{0,2,1:T(4,128)} %param.11) | copy-start | bytes 62212
  0.8 1.1 %copy-start = (bf16[1,192,8,256]{3,2,1,0:T(8,128)(2,1)S(1)}, bf16[1,192,8,256]{3,2,1,0:T(8,128)(2,1)}, u32[]{:S(2)}) copy-start(bf16[1,192,8,256]{3,2,1,0:T(8,128)(2,1)} %param.9) | copy-start | bytes 2359300
  2.0 1.1 %copy-start.5 = (bf16[1,192,8,256]{3,2,1,0:T(8,128)(2,1)S(1)}, bf16[1,192,8,256]{3,2,1,0:T(8,128)(2,1)}, u32[]{:S(2)}) copy-start(bf16[1,192,8,256]{3,2,1,0:T(8,128)(2,1)} %param.8) | copy-start | bytes 2359300
  3.1 6.2 %copy-start.4 = (bf16[576,192]{0,1:T(8,128)(2,1)S(1)}, bf16[576,192]{0,1:T(8,128)(2,1)}, u32[]{:S(2)}) copy-start(bf16[576,192]{0,1:T(8,128)(2,1)} %param.10) | copy-start | bytes 663556
  3.1 6.2 %copy-start.6 = (bf16[192,192]{1,0:T(8,128)(2,1)S(1)}, bf16[192,192]{1,0:T(8,128)(2,1)}, u32[]{:S(2)}) copy-start(bf16[192,192]{1,0:T(8,128)(2,1)} %wo_ref.1) | copy-start | bytes 221188
  4.0 7.5 %collective-permute-start.1 = (bf16[192,768]{1,0:T(8,128)(2,1)S(1)}, bf16[192,768]{1,0:T(8,128)(2,1)S(1)}, u32[]{:S(2)}, u32[]{:S(2)}) collective-permute-start(bf16[192,768]{1,0:T(8,128)(2,1)S(1)} %get-tuple-element.65), channel_id=1, source_target_pairs={{0,1},{1,0},{2,3},{3,2},{4,5},{5,4},{6,7},{7,6},{8,9},{9,8},{10,11... | collective-permute-start | bytes 884744 | tf_op jit(solution)/shard_map/ppermute | solution.py:486
  7.3 8.0 %collective-permute-start = (bf16[192,768]{1,0:T(8,128)(2,1)S(1)}, bf16[192,768]{1,0:T(8,128)(2,1)S(1)}, u32[]{:S(2)}, u32[]{:S(2)}) collective-permute-start(bf16[192,768]{1,0:T(8,128)(2,1)S(1)} %get-tuple-element.66), channel_id=1, source_target_pairs={{1,2},{3,4},{5,6},{7,8},{9,10},{11,12},{13,14},{15,16},{17,18},{19... | collective-permute-start | bytes 884744 | tf_op jit(solution)/shard_map/ppermute | solution.py:489
  21.0 1.3 %collective-permute-start.2 = (f32[96,128]{1,0:T(8,128)S(1)}, f32[96,128]{1,0:T(8,128)S(1)}, u32[]{:S(2)}, u32[]{:S(2)}) collective-permute-start(f32[96,128]{1,0:T(8,128)S(1)} %slice_select_fusion), channel_id=1, source_target_pairs={{0,1},{1,0},{2,3},{3,2},{4,5},{5,4},{6,7},{7,6},{8,9},{9,8},{10,11... | collective-permute-start | bytes 147464 | tf_op jit(solution)/shard_map/ppermute | solution.py:444
  22.3 3.0 %collective-permute-start.3 = (f32[96,128]{1,0:T(8,128)S(1)}, f32[96,128]{1,0:T(8,128)S(1)}, u32[]{:S(2)}, u32[]{:S(2)}) collective-permute-start(f32[96,128]{1,0:T(8,128)S(1)} %select_add_fusion), channel_id=1, source_target_pairs={{0,2},{1,3},{2,0},{3,1},{4,6},{5,7},{6,4},{7,5},{8,10},{9,11},{10,... | collective-permute-start | bytes 147464 | tf_op jit(solution)/shard_map/ppermute | solution.py:444
  22.4 21.1 %copy-start.10 = (f32[4]{0:T(128)S(1)}, f32[4]{0:T(128)}, u32[]{:S(2)}) copy-start(f32[4]{0:T(128)} %param.13) | copy-start | bytes 52
  25.4 4.7 %collective-permute-start.4 = (f32[96,128]{1,0:T(8,128)S(1)}, f32[96,128]{1,0:T(8,128)S(1)}, u32[]{:S(2)}, u32[]{:S(2)}) collective-permute-start(f32[96,128]{1,0:T(8,128)S(1)} %add.23), channel_id=1, source_target_pairs={{0,6},{1,7},{2,4},{3,5},{4,2},{5,3},{6,0},{7,1},{8,14},{9,15},{10,... | collective-permute-start | bytes 147464 | tf_op jit(solution)/shard_map/ppermute | solution.py:444
  30.1 3.2 %collective-permute-start.5 = (f32[96,128]{1,0:T(8,128)S(1)}, f32[96,128]{1,0:T(8,128)S(1)}, u32[]{:S(2)}, u32[]{:S(2)}) collective-permute-start(f32[96,128]{1,0:T(8,128)S(1)} %add.24), channel_id=1, source_target_pairs={{0,8},{1,9},{2,10},{3,11},{4,12},{5,13},{6,14},{7,15},{8,0},{9,1},... | collective-permute-start | bytes 147464 | tf_op jit(solution)/shard_map/ppermute | solution.py:444
  33.3 4.4 %collective-permute-start.6 = (f32[96,128]{1,0:T(8,128)S(1)}, f32[96,128]{1,0:T(8,128)S(1)}, u32[]{:S(2)}, u32[]{:S(2)}) collective-permute-start(f32[96,128]{1,0:T(8,128)S(1)} %add.25), channel_id=1, source_target_pairs={{0,16},{1,17},{2,18},{3,19},{4,20},{5,21},{6,22},{7,23},{8,24},{9,... | collective-permute-start | bytes 147464 | tf_op jit(solution)/shard_map/ppermute | solution.py:444
  37.7 5.9 %collective-permute-start.7 = (f32[96,128]{1,0:T(8,128)S(1)}, f32[96,128]{1,0:T(8,128)S(1)}, u32[]{:S(2)}, u32[]{:S(2)}) collective-permute-start(f32[96,128]{1,0:T(8,128)S(1)} %add.26.mine_ref), channel_id=1, source_target_pairs={{0,1},{1,0},{2,3},{3,2},{4,5},{5,4},{6,7},{7,6},{8,9},{9,8},{10,11... | collective-permute-start | bytes 147464 | tf_op jit(solution)/shard_map/ppermute | solution.py:444
  55.2 1.4 %copy-start.2 = (bf16[576,2048]{1,0:T(8,128)(2,1)}, bf16[576,2048]{1,0:T(8,128)(2,1)S(1)}, u32[]{:S(2)}) copy-start(bf16[576,2048]{1,0:T(8,128)(2,1)S(1)} %get-tuple-element.53.gp_ref) | copy-start | bytes 7077892
  56.6 17.1 %copy-start.1 = (bf16[1,192,8,256]{3,2,1,0:T(8,128)(2,1)S(1)}, bf16[1,192,8,256]{3,2,1,0:T(8,128)(2,1)}, u32[]{:S(2)}) copy-start(bf16[1,192,8,256]{3,2,1,0:T(8,128)(2,1)} %param.9) | copy-start | bytes 2359300
  56.6 1.5 %collective-permute-start.8 = (bf16[256,384]{1,0:T(8,128)(2,1)S(1)}, bf16[256,384]{1,0:T(8,128)(2,1)S(1)}, u32[]{:S(2)}, u32[]{:S(2)}) collective-permute-start(bf16[256,384]{1,0:T(8,128)(2,1)S(1)} %broadcast_select_fusion.4), channel_id=1, source_target_pairs={{0,1},{1,0},{2,3},{3,2},{4,5},{5,4},{6,7},{7,6},{8,9},{9,8},{10,11... | collective-permute-start | bytes 589832 | tf_op jit(solution)/shard_map/ppermute | solution.py:444
  59.0 26.8 %all-to-all-start = ((bf16[128,2,384]{2,1,0:T(2,128)(2,1)}), bf16[128,2,384]{2,1,0:T(2,128)(2,1)S(1)}, u32[]{:S(2)}, u32[]{:S(2)}) async-start(bf16[128,2,384]{2,1,0:T(2,128)(2,1)} %reshape.62), calls=%async_computation | async-start | bytes 393216 | tf_op jit(solution)/shard_map/all_to_all | solution.py:580
  73.7 1.7 %copy-start.3 = (bf16[576,2048]{1,0:T(8,128)(2,1)S(1)}, bf16[576,2048]{1,0:T(8,128)(2,1)}, u32[]{:S(2)}) copy-start(bf16[576,2048]{1,0:T(8,128)(2,1)} %copy-done.2) | copy-start | bytes 7077892
  104.0 4.2 %collective-permute-start.9 = (bf16[256,384]{1,0:T(8,128)(2,1)S(1)}, bf16[256,384]{1,0:T(8,128)(2,1)S(1)}, u32[]{:S(2)}, u32[]{:S(2)}) collective-permute-start(bf16[256,384]{1,0:T(8,128)(2,1)S(1)} %reshape.64.mine_ref), channel_id=1, source_target_pairs={{0,1},{1,0},{2,3},{3,2},{4,5},{5,4},{6,7},{7,6},{8,9},{9,8},{10,11... | collective-permute-start | bytes 589832 | tf_op jit(solution)/shard_map/ppermute | solution.py:444

commit v4 on v3

--- a/solution.py
+++ b/solution.py
@@ -14,7 +14,6 @@
 TN = (((0,), (0,)), ((), ()))
 VMEM = pl.BlockSpec(memory_space=pltpu.VMEM)
 HBM = pl.BlockSpec(memory_space=pltpu.HBM)
-HI = lax.Precision.HIGHEST
 
 
 def params(limit_mib):
@@ -37,6 +36,12 @@
 def mm(a, b, dims=None, precision=None):
     dims = dims or (((1,), (0,)), ((), ()))
     return lax.dot_general(a, b, dims, preferred_element_type=F32, precision=precision)
+
+
+def mm_split(a, b, dims=None):
+    high = a.astype(BF16)
+    low = (a - high.astype(F32)).astype(BF16)
+    return mm(high, b, dims) + mm(low, b, dims)
 
 
 def iota(shape, axis):
@@ -177,9 +182,33 @@
     return lambda r: [v.astype(F32) for v in halves(row(r))]
 
 
+def store_rows(out_ref, total, ch, w):
+    def put(at, out):
+        out = joined(out).astype(BF16)
+        out_ref[ch, at * w : (at + 1) * w] = out
+        for v in halves(out):
+            v = v.astype(F32)
+            total[:] = [total[0] + v * v] if total else [v * v]
+
+    return put
+
+
+def inner_body(p_ref, cols_ref, mi_ref, sq_ref, *, w):
+    rows = p_ref.shape[1] // w
+
+    def group(ch):
+        total = []
+        put = store_rows(mi_ref, total, ch, w)
+        row = wide_reader(p_ref, None, ch, w)
+        mix_rows(1, rows - 1, row, cols_ref, ch, lambda r, out: put(r - 1, out))
+        sq_ref[ch, :] = total[0]
+
+    each_group(p_ref.shape[0], group)
+
+
 def mix_body(
-    flags, p_ref, up_ref, dn_ref, dy2_ref, w_ref, wot_ref, cols_ref, affine_ref,
-    mixed_ref, ph_ref, pay_ref, t_ref, sq, gs, *, w, heads,
+    flags, p_ref, up_ref, dn_ref, dy2_ref, w_ref, wot_ref, cols_ref, affine_ref, mi_ref, sqi_ref,
+    mo_ref, ph_ref, pay_ref, t_ref, sq, gs, *, w, heads,
 ):
     c3 = p_ref.shape[0]
     c = c3 // 3
@@ -195,29 +224,25 @@
             ph_ref[:, at] = (mm(w_ref[...], normed) * keep).astype(BF16)
 
     def group(ch):
-        total = []
-
-        def put(r, out):
-            out = joined(out).astype(BF16)
-            mixed_ref[ch, r * w : (r + 1) * w] = out
-            for v in halves(out):
-                v = v.astype(F32)
-                total.append(v * v)
-                if len(total) > 1:
-                    total[:] = [total[0] + total[1]]
-
-        mix_rows(0, rows, wide_reader(p_ref, ph_ref, ch, w), cols_ref, ch, put)
+        total = [sqi_ref[ch, :]]
+        put = store_rows(mo_ref, total, ch, w)
+        row = wide_reader(p_ref, ph_ref, ch, w)
+        for i, r in enumerate((0, rows - 1)):
+            mix_rows(r, r + 1, row, cols_ref, ch, lambda _, out, i=i: put(i, out))
         sq[ch, :] = total[0]
 
     each_group(c3, group)
 
-    query = mixed_ref[0:c, :]
-    key = mixed_ref[c : 2 * c, :]
-    value = mixed_ref[2 * c : 3 * c, :]
-    gs[0, :, 0:c] = mm(query, key, NT)
-    t = mm(dy2_ref[...], value, NT)
+    gram = mm(mi_ref[0:c, :], mi_ref[c : 2 * c, :], NT)
+    gs[0, :, 0:c] = gram + mm(mo_ref[0:c, :], mo_ref[c : 2 * c, :], NT)
+    last = (rows - 1) * w
+    t = mm(dy2_ref[:, w:last], mi_ref[2 * c : 3 * c, :], NT)
+    t = t + mm(dy2_ref[:, 0:w], mo_ref[2 * c : 3 * c, 0:w], NT)
+    t = t + mm(dy2_ref[:, last:], mo_ref[2 * c : 3 * c, w:], NT)
     t_ref[...] = t
-    gs[1, :, 0:c] = mm(wot_ref[...].astype(F32), t, precision=HI)
+    high = t.astype(BF16)
+    low = (t - high.astype(F32)).astype(BF16)
+    gs[1, :, 0:c] = mm(wot_ref[...], high) + mm(wot_ref[...], low)
     lane = iota((hs, 128), 1)
     for h in range(heads):
         at = slice(h * hs, (h + 1) * hs)
@@ -229,8 +254,13 @@
         pay_ref[at, :] = jnp.where(lane < hs, gram, jnp.where(lane < 2 * hs, grad, rest))
 
 
-def edge_body(p_ref, ph_ref, cols_ref, mh_ref, *, w):
+def edge_body(p_ref, ph_ref, cols_ref, wot_ref, dy2_ref, up_ref, dn_ref, mh_ref, ga_ref, *, w):
     rows = p_ref.shape[1] // w
+    wot = wot_ref[...]
+    ga_ref[:, 0:w] = mm(wot, up_ref[:, 2 * w : 3 * w]).astype(BF16)
+    for r in range(rows):
+        ga_ref[:, (r + 1) * w : (r + 2) * w] = mm(wot, dy2_ref[:, r * w : (r + 1) * w]).astype(BF16)
+    ga_ref[:, (rows + 1) * w :] = mm(wot, dn_ref[:, 2 * w : 3 * w]).astype(BF16)
 
     def group(ch):
         row = wide_reader(p_ref, ph_ref, ch, w)
@@ -244,11 +274,11 @@
 
 
 def back_body(
-    flags, sharp, mine_ref, other_ref, mixed_ref, mh_ref, p_ref, ph_ref, dy2_ref, up_ref, dn_ref,
-    std_ref, t_ref, wot_ref, cols_ref,
+    flags, sharp, mine_ref, other_ref, mi_ref, mo_ref, mh_ref, ga_ref, p_ref, ph_ref,
+    std_ref, t_ref, cols_ref,
     gp_hbm, left_ref, right_ref, pay, coef, sums, mats, vecs, gm, aug, grads, gp_ref, sem, *, w, heads,
 ):
-    c = mixed_ref.shape[0] // 3
+    c = p_ref.shape[0] // 3
     hs = c // heads
     rows = p_ref.shape[1] // w
     mine = mine_ref[...]
@@ -294,25 +324,21 @@
     grad_gram_t = grad_gram.astype(F32).T.astype(BF16)
     attention_b = mats[1, :, 0:c]
     attention_t = attention_b.astype(F32).T.astype(BF16)
-    outgoing = mm(t_ref[...], attention_b.astype(F32), NT, precision=HI)
+    outgoing = mm_split(t_ref[...], attention_b, NT)
     alpha = jnp.concatenate([vecs[:, 0:128]] * (w // 128), axis=1)
     beta = jnp.concatenate([vecs[:, 128:256]] * (w // 128), axis=1)
-    wot = wot_ref[...]
     for r in range(rows + 2):
         at = slice(r * w, (r + 1) * w)
-        if r == 0:
-            dy = up_ref[:, 2 * w : 3 * w]
-            src, own = (mh_ref, slice(0, w))
-        elif r == rows + 1:
-            dy = dn_ref[:, 2 * w : 3 * w]
-            src, own = (mh_ref, slice(w, 2 * w))
+        if r in (0, rows + 1):
+            src, own = (mh_ref, 0 if r == 0 else 1)
+        elif r in (1, rows):
+            src, own = (mo_ref, 0 if r == 1 else 1)
         else:
-            own = slice((r - 1) * w, r * w)
-            dy = dy2_ref[:, own]
-            src = mixed_ref
+            src, own = (mi_ref, r - 2)
+        own = slice(own * w, (own + 1) * w)
         query = src[0:c, own]
         key = src[c : 2 * c, own]
-        grad_attended = mm(wot, dy).astype(BF16)
+        grad_attended = ga_ref[:, at]
         parts = (
             mm(grad_gram, key) - query.astype(F32) * alpha,
             mm(grad_gram_t, query) - key.astype(F32) * beta,
@@ -364,9 +390,7 @@
     place = jnp.where(place, 1.0, 0.0).astype(BF16)
     for g in range(0, 3 * c, 64):
         block = sums[g : g + 64, :]
-        high = block.astype(BF16)
-        low = (block - high.astype(F32)).astype(BF16)
-        coef[g : g + 64, :] = mm(high, place) + mm(low, place)
+        coef[g : g + 64, :] = mm_split(block, place)
 
     aug[0:c, :] = std_ref[...]
     aug[c : c + 16, :] = jnp.where(iota((16, rows * w), 0) == 0, 1.0, 0.0).astype(BF16)
@@ -462,6 +486,7 @@
         heads = sharpness.shape[0]
         c3 = 3 * c
         n = rows * w
+        ext = n + 2 * w
         core = lax.axis_index("core")
         place = lax.axis_index("chip") * 2 + core
         flags = jnp.stack([place != 0, place != tile - 1, place == 0, core == 1]).astype(F32)
@@ -505,12 +530,21 @@
             moved=8 << 20,
             name="project",
         )(x2, w_row, aff)
+        mi, sqi = call(
+            functools.partial(inner_body, w=w),
+            [((c3, n - 2 * w), BF16), ((c3, 128), F32)],
+            2,
+            limit=8,
+            flops=400 * c3 * n,
+            moved=8 << 20,
+            name="inner",
+        )(p, cols)
         up_in = jnp.where(even, across, inside)
         dn_in = jnp.where(even, inside, across)
-        mixed, ph, pay, t = call(
+        mo, ph, pay, t = call(
             functools.partial(mix_body, w=w, heads=heads),
-            [((c3, n), BF16), ((c3, 4 * w), BF16), ((c, 128), F32), ((c, c), F32)],
-            9,
+            [((c3, 2 * w), BF16), ((c3, 4 * w), BF16), ((c, 128), F32), ((c, c), F32)],
+            11,
             scratch=[
                 pltpu.VMEM((c3, 128), F32),
                 pltpu.VMEM((2, c, 256), F32),
@@ -519,24 +553,24 @@
             flops=8 * c * c * n,
             moved=8 << 20,
             name="mix",
-        )(flags, p, up_in, dn_in, dy2, w_row, wot, cols, aff)
+        )(flags, p, up_in, dn_in, dy2, w_row, wot, cols, aff, mi, sqi)
 
         half = c // 2
         mine = jnp.where(core == 0, pay[:half], pay[half:])
         theirs = jnp.where(core == 0, pay[half:], pay[:half])
         mine = mine + swap(theirs, 1, total)
-        (mh,) = call(
+        mh, ga = call(
             functools.partial(edge_body, w=w),
-            [((c3, 2 * w), BF16)],
-            3,
+            [((c3, 2 * w), BF16), ((c, ext), BF16)],
+            7,
             limit=8,
             moved=6 << 20,
             name="edge",
-        )(p, ph, cols)
+        )(p, ph, cols, wot, dy2, up_in, dn_in)
         for i, mask in enumerate(bits(total, tile)):
             mine = mine + swap(mine, mask, total)
             if i == 0:
-                mine, mh = lax.optimization_barrier((mine, mh))
+                mine, mh, ga = lax.optimization_barrier((mine, mh, ga))
         other = swap(mine, 1, total)
 
         each = pl.cdiv(c + 32, 2 * chips) * 2
@@ -544,7 +578,7 @@
         gp, left, right = call(
             functools.partial(back_body, w=w, heads=heads),
             [((c3, n), BF16), ((size, 384), BF16), ((size, 384), BF16)],
-            15,
+            13,
             hbm_out=(0,),
             scratch=[
                 pltpu.VMEM((c, 128), F32),
@@ -562,7 +596,7 @@
             flops=20 * c * c * n,
             moved=8 << 20,
             name="back",
-        )(flags, sharpness.reshape(1, heads), mine, other, mixed, mh, p, ph, dy2, up_in, dn_in, std, t, wot, cols)
+        )(flags, sharpness.reshape(1, heads), mine, other, mi, mo, mh, ga, p, ph, std, t, cols)
 
         (fm,) = call(
             functools.partial(output_body, w=w),

time: 110 us -> 107 us (0.973)
  waiting for transfers between devices: 22.1 us -> 18 us
    ppermute x1, waiting for transfers between devices: 3.81 us -> 0.94 us  [local(): across = lax.ppermute(across, strip, pairs + [(j, i) for i, j in pairs])]
    pallas_call x2 -> x3, Pallas kernels: 6.66 us -> 7.21 us  [the longest x1 2.86 us: local(): call(functools.partial(inner_body, w=w), [((c3, n - 2 * w), BF16), ((c3,...]
  transfers between devices with their start and end apart: 11 -> 11, of which waited for: 10 -> 10; matrix products, arithmetic and copies ran while one was open for 0% -> 0% of each run, Pallas kernels for 5% -> 9%
where the time goes in v4:
time: 107 us; the launch traced here: 106 us
  starting transfers between devices  37.1 us (35%)
  Pallas kernels  25.3 us (24%)
  waiting for transfers between devices  18 us (17%)
  blocking collectives  18 us (17%)
  local copies, waits for them, and re-layouts  6.38 us (6%)
    all_to_all x1, blocking collectives, local(): part = lax.all_to_all(jnp.broadcast_to(piece, got.shape), GROUP, 0, 0)  18 us
    ppermute x8, starting transfers between devices, swap(): return lax.ppermute(v, ALL, [(i, i ^ mask) for i in range(count)])  17.2 us
    all_to_all x1, starting transfers between devices, local(): got = lax.all_to_all(part.reshape(chips, each, 384), GROUP, 0, 0)  14.7 us
    pallas_call x1, Pallas kernels, local(): call(functools.partial(back_body, w=w, heads=heads), [((c3, n), BF16), ((...  11.3 us
    ppermute x8, waiting for transfers between devices, swap(): return lax.ppermute(v, ALL, [(i, i ^ mask) for i in range(count)])  9.52 us
    all_to_all x1, waiting for transfers between devices, local(): got = lax.all_to_all(part.reshape(chips, each, 384), GROUP, 0, 0)  7.58 us
    unnamed x22, local copies, waits for them, and re-layouts  5.37 us
    ppermute x1, starting transfers between devices, local(): lax.ppermute(jnp.where(even, up, dn), strip, [(i, i ^ 1) for i in range(t...  3.29 us
  transfers between devices with their start and end apart: 11, of which 10 were waited for; matrix products, arithmetic and copies ran while one was open for 0% of the time, Pallas kernels for 9%

profile of v4, /device:TPU:1, one launch (start us, length us, event | category | flops | bytes accessed | tf_op | source)
XLA Modules:
  0.0 106.2 jit_solution(10872844698661565917)
XLA Ops:
  0.6 0.0 copy-start.9
  0.6 0.0 copy-start.8
  0.7 0.0 copy-start.7
  0.7 0.1 pad_add_fusion
  0.8 0.1 broadcast_in_dim.6.flags
  0.8 0.0 copy-start
  0.8 1.1 %copy-done = bf16[1,192,8,256]{3,2,1,0:T(8,128)(2,1)S(1)} copy-done((bf16[1,192,8,256]{3,2,1,0:T(8,128)(2,1)S(1)}, bf16[1,192,8,256]{3,2,1,0:T(8,128)(2,1)}, u32[]{:S(2)}) %copy-start) | copy-done | bytes 786456
  2.0 0.0 copy-start.5
  2.0 1.1 %copy-done.5 = bf16[1,192,8,256]{3,2,1,0:T(8,128)(2,1)S(1)} copy-done((bf16[1,192,8,256]{3,2,1,0:T(8,128)(2,1)S(1)}, bf16[1,192,8,256]{3,2,1,0:T(8,128)(2,1)}, u32[]{:S(2)}) %copy-start.5) | copy-done | bytes 786456
  3.1 0.0 copy-start.4
  3.1 0.0 copy-start.6
  3.1 0.9 spread.1
  4.0 3.3 %collective-permute-start.1 = (bf16[192,768]{1,0:T(8,128)(2,1)S(1)}, bf16[192,768]{1,0:T(8,128)(2,1)S(1)}, u32[]{:S(2)}, u32[]{:S(2)}) collective-permute-start(bf16[192,768]{1,0:T(8,128)(2,1)S(1)} %get-tuple-element.75), channel_id=1, source_target_pairs={{0,1},{1,0},{2,3},{3,2},{4,5},{5,4},{6,7},{7,6},{8,9},{9,8},{10,11... | collective-permute-start | bytes 884744 | tf_op jit(solution)/shard_map/ppermute | solution.py:511
  7.3 1.9 %collective-permute-start = (bf16[192,768]{1,0:T(8,128)(2,1)S(1)}, bf16[192,768]{1,0:T(8,128)(2,1)S(1)}, u32[]{:S(2)}, u32[]{:S(2)}) collective-permute-start(bf16[192,768]{1,0:T(8,128)(2,1)S(1)} %get-tuple-element.76), channel_id=1, source_target_pairs={{1,2},{3,4},{5,6},{7,8},{9,10},{11,12},{13,14},{15,16},{17,18},{19... | collective-permute-start | bytes 884744 | tf_op jit(solution)/shard_map/ppermute | solution.py:514
  9.2 0.0 copy-done.9
  9.2 0.0 copy-done.8
  9.3 0.0 copy-done.7
  9.3 0.0 copy-done.4
  9.3 0.0 copy-done.6
  9.3 1.1 %columns.1 = (f32[9,576,128]{2,1,0:T(8,128)S(1)}, f32[2,192,128]{2,1,0:T(8,128)S(1)}, bf16[576,192]{1,0:T(8,128)(2,1)S(1)}, bf16[192,192]{1,0:T(8,128)(2,1)S(1)}) custom-call(f32[3,3,576]{2,1,0:T(4,128)S(1)} %bitcast.25, f32[1,192]{1,0:T(1,128)S(1)} %bitcast.26, f32[1,192]{1,0:T(1,128)S(1)} %bitcast.28, bf16[192,576]{1,0:T(8,128)(2,1)S(1)} %bitcast.21, ...), custom_call_target="tpu_custom_call" | custom-call | bytes 4194304 | tf_op jit(solution)/shard_map/columns/pallas_call | solution.py:515
  10.4 1.1 %project.1 = (bf16[576,2048]{1,0:T(8,128)(2,1)S(1)}, bf16[192,2048]{1,0:T(8,128)(2,1)S(1)}, f32[8,2048]{1,0:T(8,128)S(1)}) custom-call(bf16[192,2048]{1,0:T(8,128)(2,1)S(1)} %get-tuple-element.40.x2_ref, bf16[576,192]{1,0:T(8,128)(2,1)S(1)} %get-tuple-element.41.w_ref, f32[2,192,128]{2,1,0:T(8,128)S(1)} %get-tuple-element.42.affine_ref), custom_call_target="tpu_custom_call" | custom-call | flops 452984832 | bytes 8388608 | tf_op jit(solution)/shard_map/project/pallas_call | solution.py:524
  11.5 2.9 %inner.1 = (bf16[576,1536]{1,0:T(8,128)(2,1)S(1)}, f32[576,128]{1,0:T(8,128)S(1)}) custom-call(bf16[576,2048]{1,0:T(8,128)(2,1)S(1)} %get-tuple-element.43.p_ref, f32[9,576,128]{2,1,0:T(8,128)S(1)} %get-tuple-element.48.cols_ref), custom_call_target="tpu_custom_call" | custom-call | flops 471859200 | bytes 8388608 | tf_op jit(solution)/shard_map/inner/pallas_call | solution.py:533
  14.4 0.0 collective-permute-done.1
  14.4 0.9 collective-permute-done
  15.4 2.8 %mix.1 = (bf16[576,512]{1,0:T(8,128)(2,1)S(1)}, bf16[576,1024]{1,0:T(8,128)(2,1)S(1)}, f32[192,128]{1,0:T(8,128)S(1)}, f32[192,192]{1,0:T(8,128)S(1)}) custom-call(f32[8,128]{1,0:T(8,128)S(1)} %broadcast_in_dim.6.flags, bf16[576,2048]{1,0:T(8,128)(2,1)S(1)} %get-tuple-element.43.p_ref, bf16[192,768]{1,0:T(8,128)(2,1)S(1)} %get-tuple-element.74.up_ref, ...), custom_call_target="tpu_custom_call" | custom-call | flops 603979776 | bytes 8388608 | tf_op jit(solution)/shard_map/mix/pallas_call | solution.py:544
  18.2 0.1 collective-permute-start.2
  18.3 1.2 %collective-permute-done.2 = f32[96,128]{1,0:T(8,128)S(1)} collective-permute-done((f32[96,128]{1,0:T(8,128)S(1)}, f32[96,128]{1,0:T(8,128)S(1)}, u32[]{:S(2)}, u32[]{:S(2)}) %collective-permute-start.2) | collective-permute-done | bytes 49184 | tf_op jit(solution)/shard_map/ppermute | solution.py:468
  19.6 0.7 collective-permute-start.3
  20.2 0.0 copy-start.10
  20.2 1.5 %edge.1 = (bf16[576,512]{1,0:T(8,128)(2,1)S(1)}, bf16[192,2560]{1,0:T(8,128)(2,1)S(1)}) custom-call(bf16[576,2048]{1,0:T(8,128)(2,1)S(1)} %get-tuple-element.43.p_ref, bf16[576,1024]{1,0:T(8,128)(2,1)S(1)} %get-tuple-element.52.ph_ref, f32[9,576,128]{2,1,0:T(8,128)S(1)} %get-tuple-element.48.cols_ref, bf16[192,192]{1,0:T(8,128)(2,1)S(1)} %get-tuple-element.47.wot_ref, ...), custom_call_target="tpu_custom_call" | custom-call | bytes 6291456 | tf_op jit(solution)/shard_map/edge/pallas_call | solution.py:562
  21.8 0.8 collective-permute-done.3
  22.6 3.2 %collective-permute-start.4 = (f32[96,128]{1,0:T(8,128)S(1)}, f32[96,128]{1,0:T(8,128)S(1)}, u32[]{:S(2)}, u32[]{:S(2)}) collective-permute-start(f32[96,128]{1,0:T(8,128)S(1)} %add.23), channel_id=1, source_target_pairs={{0,6},{1,7},{2,4},{3,5},{4,2},{5,3},{6,0},{7,1},{8,14},{9,15},{10,... | collective-permute-start | bytes 147464 | tf_op jit(solution)/shard_map/ppermute | solution.py:468
  25.8 1.5 %collective-permute-done.4 = f32[96,128]{1,0:T(8,128)S(1)} collective-permute-done((f32[96,128]{1,0:T(8,128)S(1)}, f32[96,128]{1,0:T(8,128)S(1)}, u32[]{:S(2)}, u32[]{:S(2)}) %collective-permute-start.4) | collective-permute-done | bytes 49184 | tf_op jit(solution)/shard_map/ppermute | solution.py:468
  27.3 1.7 %collective-permute-start.5 = (f32[96,128]{1,0:T(8,128)S(1)}, f32[96,128]{1,0:T(8,128)S(1)}, u32[]{:S(2)}, u32[]{:S(2)}) collective-permute-start(f32[96,128]{1,0:T(8,128)S(1)} %add.24), channel_id=1, source_target_pairs={{0,8},{1,9},{2,10},{3,11},{4,12},{5,13},{6,14},{7,15},{8,0},{9,1},... | collective-permute-start | bytes 147464 | tf_op jit(solution)/shard_map/ppermute | solution.py:468
  29.0 1.5 %collective-permute-done.5 = f32[96,128]{1,0:T(8,128)S(1)} collective-permute-done((f32[96,128]{1,0:T(8,128)S(1)}, f32[96,128]{1,0:T(8,128)S(1)}, u32[]{:S(2)}, u32[]{:S(2)}) %collective-permute-start.5) | collective-permute-done | bytes 49184 | tf_op jit(solution)/shard_map/ppermute | solution.py:468
  30.5 2.9 %collective-permute-start.6 = (f32[96,128]{1,0:T(8,128)S(1)}, f32[96,128]{1,0:T(8,128)S(1)}, u32[]{:S(2)}, u32[]{:S(2)}) collective-permute-start(f32[96,128]{1,0:T(8,128)S(1)} %add.25), channel_id=1, source_target_pairs={{0,16},{1,17},{2,18},{3,19},{4,20},{5,21},{6,22},{7,23},{8,24},{9,... | collective-permute-start | bytes 147464 | tf_op jit(solution)/shard_map/ppermute | solution.py:468
  33.4 1.5 %collective-permute-done.6 = f32[96,128]{1,0:T(8,128)S(1)} collective-permute-done((f32[96,128]{1,0:T(8,128)S(1)}, f32[96,128]{1,0:T(8,128)S(1)}, u32[]{:S(2)}, u32[]{:S(2)}) %collective-permute-start.6) | collective-permute-done | bytes 49184 | tf_op jit(solution)/shard_map/ppermute | solution.py:468
  34.9 5.0 %collective-permute-start.7 = (f32[96,128]{1,0:T(8,128)S(1)}, f32[96,128]{1,0:T(8,128)S(1)}, u32[]{:S(2)}, u32[]{:S(2)}) collective-permute-start(f32[96,128]{1,0:T(8,128)S(1)} %add.26.mine_ref), channel_id=1, source_target_pairs={{0,1},{1,0},{2,3},{3,2},{4,5},{5,4},{6,7},{7,6},{8,9},{9,8},{10,11... | collective-permute-start | bytes 147464 | tf_op jit(solution)/shard_map/ppermute | solution.py:468
  39.9 0.9 collective-permute-done.7.other_ref
  40.8 0.0 copy-done.10
  40.8 11.3 %back.1 = (bf16[576,2048]{1,0:T(8,128)(2,1)S(1)}, bf16[256,384]{1,0:T(8,128)(2,1)S(1)}, bf16[256,384]{1,0:T(8,128)(2,1)S(1)}) custom-call(f32[8,128]{1,0:T(8,128)S(1)} %broadcast_in_dim.6.flags, f32[1,4]{1,0:T(1,128)S(1)} %bitcast.30, f32[96,128]{1,0:T(8,128)S(1)} %add.26.mine_ref, f32[96,128]{1,0:T(8,128)S(1)} %collective-permute-done.7.other_ref, ...), custom_call_target="tpu_custom_call" | custom-call | flops 1509949440 | bytes 8388608 | tf_op jit(solution)/shard_map/back/pallas_call | solution.py:578
  52.1 0.0 copy-start.2
  52.1 1.4 %copy-done.2 = bf16[576,2048]{1,0:T(8,128)(2,1)} copy-done((bf16[576,2048]{1,0:T(8,128)(2,1)}, bf16[576,2048]{1,0:T(8,128)(2,1)S(1)}, u32[]{:S(2)}) %copy-start.2) | copy-done | bytes 2359320
  53.5 0.0 copy-start.1
  53.6 0.4 collective-permute-start.8
  54.0 1.1 %collective-permute-done.8 = bf16[256,384]{1,0:T(8,128)(2,1)S(1)} collective-permute-done((bf16[256,384]{1,0:T(8,128)(2,1)S(1)}, bf16[256,384]{1,0:T(8,128)(2,1)S(1)}, u32[]{:S(2)}, u32[]{:S(2)}) %collective-permute-start.8) | collective-permute-done | bytes 196640 | tf_op jit(solution)/shard_map/ppermute | solution.py:468
  55.1 0.1 add_convert_fusion
  55.2 0.8 reshape.62
  55.9 14.7 %all-to-all-start = ((bf16[128,2,384]{2,1,0:T(2,128)(2,1)}), bf16[128,2,384]{2,1,0:T(2,128)(2,1)S(1)}, u32[]{:S(2)}, u32[]{:S(2)}) async-start(bf16[128,2,384]{2,1,0:T(2,128)(2,1)} %reshape.62), calls=%async_computation | async-start | bytes 393216 | tf_op jit(solution)/shard_map/all_to_all | solution.py:614
  70.6 0.0 copy-done.1
  70.6 0.0 copy-start.3
  70.6 1.7 %copy-done.3 = bf16[576,2048]{1,0:T(8,128)(2,1)S(1)} copy-done((bf16[576,2048]{1,0:T(8,128)(2,1)S(1)}, bf16[576,2048]{1,0:T(8,128)(2,1)}, u32[]{:S(2)}) %copy-start.3) | copy-done | bytes 2359320
  72.3 2.6 %output.1 = bf16[192,8,256]{2,1,0:T(8,128)(2,1)} custom-call(bf16[576,2048]{1,0:T(8,128)(2,1)S(1)} %copy-done.3, bf16[192,576]{1,0:T(8,128)(2,1)S(1)} %bitcast.22, bf16[192,2048]{1,0:T(8,128)(2,1)S(1)} %get-tuple-element.59.std_ref, f32[8,2048]{1,0:T(8,128)S(1)} %get-tuple-element.64.inv_ref, bf16[192,8,256]{2,1,0:T(8,128)(2,1)S(1)} %bitcast.20, ...), custom_call_target="tpu_custom_call" | custom-call | flops 452984832 | bytes 6291456 | tf_op jit(solution)/shard_map/output/pallas_call | solution.py:601
  74.9 7.6 %all-to-all-done = bf16[128,2,384]{2,1,0:T(2,128)(2,1)S(1)} async-done(((bf16[128,2,384]{2,1,0:T(2,128)(2,1)}), bf16[128,2,384]{2,1,0:T(2,128)(2,1)S(1)}, u32[]{:S(2)}, u32[]{:S(2)}) %all-to-all-start) | async-done | bytes 196640 | tf_op jit(solution)/shard_map/all_to_all | solution.py:614
  82.4 0.2 reduce_sum.12
  82.7 0.1 broadcast_in_dim.16
  82.8 18.0 %all_to_all.10 = bf16[128,2,384]{2,1,0:T(2,128)(2,1)S(1)} all-to-all(bf16[128,2,384]{2,1,0:T(2,128)(2,1)S(1)} %broadcast_in_dim.16), channel_id=1, replica_groups=mesh['img'=8,'chip'=16,'core'=2] {'img','chip'}, dimensions={0} | all-to-all | bytes 393216 | tf_op jit(solution)/shard_map/all_to_all | solution.py:617
  100.8 0.1 reshape.64.mine_ref
  100.9 3.2 %collective-permute-start.9 = (bf16[256,384]{1,0:T(8,128)(2,1)S(1)}, bf16[256,384]{1,0:T(8,128)(2,1)S(1)}, u32[]{:S(2)}, u32[]{:S(2)}) collective-permute-start(bf16[256,384]{1,0:T(8,128)(2,1)S(1)} %reshape.64.mine_ref), channel_id=1, source_target_pairs={{0,1},{1,0},{2,3},{3,2},{4,5},{5,4},{6,7},{7,6},{8,9},{9,8},{10,11... | collective-permute-start | bytes 589832 | tf_op jit(solution)/shard_map/ppermute | solution.py:468
  104.0 1.1 %collective-permute-done.9.other_ref = bf16[256,384]{1,0:T(8,128)(2,1)S(1)} collective-permute-done((bf16[256,384]{1,0:T(8,128)(2,1)S(1)}, bf16[256,384]{1,0:T(8,128)(2,1)S(1)}, u32[]{:S(2)}, u32[]{:S(2)}) %collective-permute-start.9) | collective-permute-done | bytes 196640 | tf_op jit(solution)/shard_map/ppermute | solution.py:468
  105.1 1.1 %finish.1 = (f32[192,576]{1,0:T(8,128)}, f32[3,3,576]{2,1,0:T(4,128)}, f32[192,192]{1,0:T(8,128)}, f32[1,4]{1,0:T(1,128)}, f32[1,192]{1,0:T(1,128)}, /*index=5*/f32[1,192]{1,0:T(1,128)}) custom-call(f32[8,128]{1,0:T(8,128)S(1)} %broadcast_in_dim.6.flags, bf16[256,384]{1,0:T(8,128)(2,1)S(1)} %reshape.64.mine_ref, ...), custom_call_target="tpu_custom_call" | custom-call | bytes 2097152 | tf_op jit(solution)/shard_map/finish/pallas_call | solution.py:621
  (10 shorter events, 0.2 us)
Async XLA Ops:
  0.6 8.6 %copy-start.9 = (f32[192]{0:T(256)S(1)}, f32[192]{0:T(256)}, u32[]{:S(2)}) copy-start(f32[192]{0:T(256)} %param.15) | copy-start | bytes 2308
  0.6 8.6 %copy-start.8 = (f32[192]{0:T(256)S(1)}, f32[192]{0:T(256)}, u32[]{:S(2)}) copy-start(f32[192]{0:T(256)} %param.14) | copy-start | bytes 2308
  0.7 8.6 %copy-start.7 = (f32[576,3,3]{0,2,1:T(4,128)S(1)}, f32[576,3,3]{0,2,1:T(4,128)}, u32[]{:S(2)}) copy-start(f32[576,3,3]{0,2,1:T(4,128)} %param.11) | copy-start | bytes 62212
  0.8 1.1 %copy-start = (bf16[1,192,8,256]{3,2,1,0:T(8,128)(2,1)S(1)}, bf16[1,192,8,256]{3,2,1,0:T(8,128)(2,1)}, u32[]{:S(2)}) copy-start(bf16[1,192,8,256]{3,2,1,0:T(8,128)(2,1)} %param.9) | copy-start | bytes 2359300
  2.0 1.1 %copy-start.5 = (bf16[1,192,8,256]{3,2,1,0:T(8,128)(2,1)S(1)}, bf16[1,192,8,256]{3,2,1,0:T(8,128)(2,1)}, u32[]{:S(2)}) copy-start(bf16[1,192,8,256]{3,2,1,0:T(8,128)(2,1)} %param.8) | copy-start | bytes 2359300
  3.1 6.2 %copy-start.4 = (bf16[576,192]{0,1:T(8,128)(2,1)S(1)}, bf16[576,192]{0,1:T(8,128)(2,1)}, u32[]{:S(2)}) copy-start(bf16[576,192]{0,1:T(8,128)(2,1)} %param.10) | copy-start | bytes 663556
  3.1 6.2 %copy-start.6 = (bf16[192,192]{1,0:T(8,128)(2,1)S(1)}, bf16[192,192]{1,0:T(8,128)(2,1)}, u32[]{:S(2)}) copy-start(bf16[192,192]{1,0:T(8,128)(2,1)} %wo_ref.1) | copy-start | bytes 221188
  4.0 10.4 %collective-permute-start.1 = (bf16[192,768]{1,0:T(8,128)(2,1)S(1)}, bf16[192,768]{1,0:T(8,128)(2,1)S(1)}, u32[]{:S(2)}, u32[]{:S(2)}) collective-permute-start(bf16[192,768]{1,0:T(8,128)(2,1)S(1)} %get-tuple-element.75), channel_id=1, source_target_pairs={{0,1},{1,0},{2,3},{3,2},{4,5},{5,4},{6,7},{7,6},{8,9},{9,8},{10,11... | collective-permute-start | bytes 884744 | tf_op jit(solution)/shard_map/ppermute | solution.py:511
  7.3 8.0 %collective-permute-start = (bf16[192,768]{1,0:T(8,128)(2,1)S(1)}, bf16[192,768]{1,0:T(8,128)(2,1)S(1)}, u32[]{:S(2)}, u32[]{:S(2)}) collective-permute-start(bf16[192,768]{1,0:T(8,128)(2,1)S(1)} %get-tuple-element.76), channel_id=1, source_target_pairs={{1,2},{3,4},{5,6},{7,8},{9,10},{11,12},{13,14},{15,16},{17,18},{19... | collective-permute-start | bytes 884744 | tf_op jit(solution)/shard_map/ppermute | solution.py:514
  18.2 1.3 %collective-permute-start.2 = (f32[96,128]{1,0:T(8,128)S(1)}, f32[96,128]{1,0:T(8,128)S(1)}, u32[]{:S(2)}, u32[]{:S(2)}) collective-permute-start(f32[96,128]{1,0:T(8,128)S(1)} %slice_select_fusion), channel_id=1, source_target_pairs={{0,1},{1,0},{2,3},{3,2},{4,5},{5,4},{6,7},{7,6},{8,9},{9,8},{10,11... | collective-permute-start | bytes 147464 | tf_op jit(solution)/shard_map/ppermute | solution.py:468
  19.6 3.0 %collective-permute-start.3 = (f32[96,128]{1,0:T(8,128)S(1)}, f32[96,128]{1,0:T(8,128)S(1)}, u32[]{:S(2)}, u32[]{:S(2)}) collective-permute-start(f32[96,128]{1,0:T(8,128)S(1)} %select_add_fusion), channel_id=1, source_target_pairs={{0,2},{1,3},{2,0},{3,1},{4,6},{5,7},{6,4},{7,5},{8,10},{9,11},{10,... | collective-permute-start | bytes 147464 | tf_op jit(solution)/shard_map/ppermute | solution.py:468
  20.2 20.5 %copy-start.10 = (f32[4]{0:T(128)S(1)}, f32[4]{0:T(128)}, u32[]{:S(2)}) copy-start(f32[4]{0:T(128)} %param.13) | copy-start | bytes 52
  22.6 4.7 %collective-permute-start.4 = (f32[96,128]{1,0:T(8,128)S(1)}, f32[96,128]{1,0:T(8,128)S(1)}, u32[]{:S(2)}, u32[]{:S(2)}) collective-permute-start(f32[96,128]{1,0:T(8,128)S(1)} %add.23), channel_id=1, source_target_pairs={{0,6},{1,7},{2,4},{3,5},{4,2},{5,3},{6,0},{7,1},{8,14},{9,15},{10,... | collective-permute-start | bytes 147464 | tf_op jit(solution)/shard_map/ppermute | solution.py:468
  27.3 3.2 %collective-permute-start.5 = (f32[96,128]{1,0:T(8,128)S(1)}, f32[96,128]{1,0:T(8,128)S(1)}, u32[]{:S(2)}, u32[]{:S(2)}) collective-permute-start(f32[96,128]{1,0:T(8,128)S(1)} %add.24), channel_id=1, source_target_pairs={{0,8},{1,9},{2,10},{3,11},{4,12},{5,13},{6,14},{7,15},{8,0},{9,1},... | collective-permute-start | bytes 147464 | tf_op jit(solution)/shard_map/ppermute | solution.py:468
  30.5 4.4 %collective-permute-start.6 = (f32[96,128]{1,0:T(8,128)S(1)}, f32[96,128]{1,0:T(8,128)S(1)}, u32[]{:S(2)}, u32[]{:S(2)}) collective-permute-start(f32[96,128]{1,0:T(8,128)S(1)} %add.25), channel_id=1, source_target_pairs={{0,16},{1,17},{2,18},{3,19},{4,20},{5,21},{6,22},{7,23},{8,24},{9,... | collective-permute-start | bytes 147464 | tf_op jit(solution)/shard_map/ppermute | solution.py:468
  34.9 5.9 %collective-permute-start.7 = (f32[96,128]{1,0:T(8,128)S(1)}, f32[96,128]{1,0:T(8,128)S(1)}, u32[]{:S(2)}, u32[]{:S(2)}) collective-permute-start(f32[96,128]{1,0:T(8,128)S(1)} %add.26.mine_ref), channel_id=1, source_target_pairs={{0,1},{1,0},{2,3},{3,2},{4,5},{5,4},{6,7},{7,6},{8,9},{9,8},{10,11... | collective-permute-start | bytes 147464 | tf_op jit(solution)/shard_map/ppermute | solution.py:468
  52.1 1.4 %copy-start.2 = (bf16[576,2048]{1,0:T(8,128)(2,1)}, bf16[576,2048]{1,0:T(8,128)(2,1)S(1)}, u32[]{:S(2)}) copy-start(bf16[576,2048]{1,0:T(8,128)(2,1)S(1)} %get-tuple-element.63.gp_ref) | copy-start | bytes 7077892
  53.5 17.1 %copy-start.1 = (bf16[1,192,8,256]{3,2,1,0:T(8,128)(2,1)S(1)}, bf16[1,192,8,256]{3,2,1,0:T(8,128)(2,1)}, u32[]{:S(2)}) copy-start(bf16[1,192,8,256]{3,2,1,0:T(8,128)(2,1)} %param.9) | copy-start | bytes 2359300
  53.6 1.5 %collective-permute-start.8 = (bf16[256,384]{1,0:T(8,128)(2,1)S(1)}, bf16[256,384]{1,0:T(8,128)(2,1)S(1)}, u32[]{:S(2)}, u32[]{:S(2)}) collective-permute-start(bf16[256,384]{1,0:T(8,128)(2,1)S(1)} %broadcast_select_fusion.4), channel_id=1, source_target_pairs={{0,1},{1,0},{2,3},{3,2},{4,5},{5,4},{6,7},{7,6},{8,9},{9,8},{10,11... | collective-permute-start | bytes 589832 | tf_op jit(solution)/shard_map/ppermute | solution.py:468
  55.9 26.5 %all-to-all-start = ((bf16[128,2,384]{2,1,0:T(2,128)(2,1)}), bf16[128,2,384]{2,1,0:T(2,128)(2,1)S(1)}, u32[]{:S(2)}, u32[]{:S(2)}) async-start(bf16[128,2,384]{2,1,0:T(2,128)(2,1)} %reshape.62), calls=%async_computation | async-start | bytes 393216 | tf_op jit(solution)/shard_map/all_to_all | solution.py:614
  70.6 1.7 %copy-start.3 = (bf16[576,2048]{1,0:T(8,128)(2,1)S(1)}, bf16[576,2048]{1,0:T(8,128)(2,1)}, u32[]{:S(2)}) copy-start(bf16[576,2048]{1,0:T(8,128)(2,1)} %copy-done.2) | copy-start | bytes 7077892
  100.9 4.3 %collective-permute-start.9 = (bf16[256,384]{1,0:T(8,128)(2,1)S(1)}, bf16[256,384]{1,0:T(8,128)(2,1)S(1)}, u32[]{:S(2)}, u32[]{:S(2)}) collective-permute-start(bf16[256,384]{1,0:T(8,128)(2,1)S(1)} %reshape.64.mine_ref), channel_id=1, source_target_pairs={{0,1},{1,0},{2,3},{3,2},{4,5},{5,4},{6,7},{7,6},{8,9},{9,8},{10,11... | collective-permute-start | bytes 589832 | tf_op jit(solution)/shard_map/ppermute | solution.py:468
